TPU v7x, 256 devices: a whole 4x4x8 slice. The times are simulated.
256 devices in a mesh: dp: 32 (over y, x, z_lo), tensor: 8 (over z_hi, core).
Axes of the slice: x: 4, y: 4, z: 8 (z_hi: 4, z_lo: 2; z = z_hi * 2 + z_lo), core: 2. Of those that a mesh axis runs over, the one named last changes fastest.
Arguments:
- grad_out: bfloat16 [24576, 4096], P(('dp', 'tensor')), may hold values from -0.15625 to 0.15625
- activations: bfloat16 [24576, 14336], P('dp', 'tensor'), may hold values from -6 to 6
- grad_dither: float32 [24576, 4096], P(('dp', 'tensor')), may hold values from -0.5 to 0.5
- hidden_dither: float32 [32, 14336], P('dp', 'tensor'), may hold values from -0.25 to 0.25
- feature_dither: float32 [32, 4096], P('dp'), may hold values from -0.25 to 0.25
Outputs:
- weight_grad: float32 [4096, 14336], P('dp', 'tensor')
All inputs are finite; a program needn't handle non-finite values.
Results may differ from a plain program's by a relative error of at most 0.014.
Values may be sent and summed in bfloat16 or wider, within the bound.
A program may use at most 128 MiB of HBM per device.

v0:
```python
import jax
import jax.numpy as jnp
from jax import lax
from jax.sharding import PartitionSpec as P

BLOCK = 128
Y_LEVELS = 8
W_LEVELS = 7
ROW_TILE = 512


epsilon = 1e-06


def decode_rows(code_rows, scale_rows):
    row_total = code_rows.shape[0]
    block_count = code_rows.shape[1] // BLOCK
    held = lax.optimization_barrier(code_rows).astype(jnp.float32)
    values = (
        held.reshape(row_total, block_count, BLOCK) * scale_rows.astype(jnp.float32)[:, :, None]
    )
    return values.reshape(row_total, block_count * BLOCK).astype(jnp.bfloat16)


def decode_terms(code_block, block_scale):
    feat_rows, unit_cols = code_block.shape
    block_count = feat_rows // BLOCK
    held = lax.optimization_barrier(code_block).astype(jnp.float32)
    values = (
        held.reshape(block_count, BLOCK, unit_cols) * block_scale.astype(jnp.float32)[:, None, :]
    )
    return values.reshape(feat_rows, unit_cols).astype(jnp.bfloat16)


def quantize(partial_value, feature_part, hidden_part):
    feat_rows, unit_cols = partial_value.shape
    block_count = feat_rows // BLOCK
    blocks = partial_value.reshape(block_count, BLOCK, unit_cols)
    magnitude = jnp.max(jnp.abs(blocks), axis=1)
    block_scale = ((magnitude + epsilon) / W_LEVELS).astype(jnp.bfloat16)
    scaled = (blocks / block_scale.astype(jnp.float32)[:, None, :]).reshape(feat_rows, unit_cols)
    code_block = (scaled + hidden_part[None, :] + feature_part[:, None]).astype(jnp.bfloat16)
    return (code_block, block_scale)


def per_device(grad_out, activations, grad_dither, hidden_dither, feature_dither):
    row_count, feat_width = grad_out.shape
    block_count = feat_width // BLOCK
    grad_float = grad_out.astype(jnp.float32)
    magnitude = jnp.max(jnp.abs(grad_float).reshape(row_count, block_count, BLOCK), axis=2)
    y_scale = ((magnitude + epsilon) / Y_LEVELS).astype(jnp.bfloat16)
    scaled = (
        grad_float.reshape(row_count, block_count, BLOCK) / y_scale.astype(jnp.float32)[:, :, None]
    )
    y_code = (scaled.reshape(row_count, feat_width) + grad_dither).astype(jnp.bfloat16)
    code_rows, scale_rows = (
        lax.all_gather(y_code, "tensor", axis=0, tiled=True),
        lax.all_gather(y_scale, "tensor", axis=0, tiled=True),
    )
    y_hat = decode_rows(code_rows, scale_rows)
    unit_count = activations.shape[1]
    owners = lax.axis_size("dp")
    own_rows = feat_width // owners
    hidden_noise = hidden_dither[0]
    feature_noise = feature_dither[0]

    def feature_tile(tile_start):
        feat_cols = lax.dynamic_slice_in_dim(y_hat, tile_start, ROW_TILE, 1)
        partial_value = lax.dot_general(
            feat_cols, activations, (((0,), (0,)), ((), ())), preferred_element_type=jnp.float32
        )
        feature_part = lax.dynamic_slice_in_dim(feature_noise, tile_start, ROW_TILE, 0)
        return quantize(partial_value, feature_part, hidden_noise)

    tile_starts = jnp.arange(feat_width // ROW_TILE, dtype=jnp.int32) * ROW_TILE
    code_tiles, scale_tiles = lax.map(feature_tile, tile_starts)
    all_codes = code_tiles.reshape(feat_width, unit_count)
    all_scales = scale_tiles.reshape(block_count, unit_count)
    code_part = lax.all_to_all(all_codes, "dp", split_axis=0, concat_axis=0, tiled=True)
    scale_part = lax.all_to_all(all_scales, "dp", split_axis=0, concat_axis=0, tiled=True)
    unit_cols = code_part.shape[1]
    terms = decode_terms(code_part, scale_part)
    held = lax.optimization_barrier(terms).astype(jnp.float32).reshape(owners, own_rows, unit_cols)
    return jnp.sum(held, axis=0)


def solution(mesh):
    placed = (
        P(("dp", "tensor"), None),
        P("dp", "tensor"),
        P(("dp", "tensor"), None),
        P("dp", "tensor"),
        P("dp", None),
    )
    return jax.shard_map(
        per_device, mesh=mesh, in_specs=placed, out_specs=P("dp", "tensor"), check_vma=False
    )
```

profile of v0, /device:TPU:32, one launch (start us, length us, event | category | flops | bytes accessed | tf_op | source)
XLA Modules:
  0.0 474.8 jit_solution(6907904781474757774)
XLA Ops:
  9.2 3.4 fusion.11
  12.7 17.3 %all-gather = bf16[8,96,32]{1,2,0:T(8,128)(2,1)S(1)} all-gather(bf16[1,96,32]{1,2,0:T(8,128)(2,1)S(1)} %copy.11), channel_id=1, replica_groups=mesh['dp'=32,'tensor'=8] {'tensor'}, dimensions={0}, use_global_device_ids=true | all-gather | bytes 55296 | tf_op jit(solution)/shard_map/all_gather | solution.py:58
  30.1 54.7 %all-gather.3.cloned.1.call-done = bf16[768,4096]{1,0:T(8,128)(2,1)} async-done(((bf16[96,4096]{1,0:T(8,128)(2,1)}), bf16[768,4096]{1,0:T(8,128)(2,1)}) %all-gather.3.cloned.1.call-update) | async-done | bytes 6291472 | tf_op jit(solution)/shard_map/all_gather | solution.py:57
  84.8 7.1 %mul.31 = f32[768,32,128]{2,1,0:T(8,128)} broadcast(f32[768,32]{1,0:T(8,128)S(1)} %bitcast.57), dimensions={0,1} | broadcast | bytes 12681216 | tf_op jit(solution)/shard_map/mul | solution.py:20
  91.9 16.8 %fusion.8 = bf16[768,4096]{1,0:T(8,128)(2,1)} fusion(f32[96,8,32,128]{3,2,1,0:T(8,128)} %bitcast.53, bf16[768,4096]{1,0:T(8,128)(2,1)} %all-gather.3.cloned.1.call-done), kind=kLoop, calls=%fused_computation.16 | loop fusion | flops 9437184 | bytes 25165824 | tf_op jit(solution)/shard_map/convert_element_type | solution.py:22
  108.8 65.0 %while.12 = (s32[]{:T(128)}, bf16[8,512,1792]{2,1,0:T(8,128)(2,1)}, bf16[8,4,1792]{2,1,0:T(4,128)(2,1)S(1)}, s32[8]{0:T(128)S(1)}, bf16[768,4096]{1,0:T(8,128)(2...) while((s32[]{:T(128)}, bf16[8,512,1792]{2,1,0:T(8,128)(2,1)}, ...), condition=%wide.region_3.4_spmd, body=%wide.region_1.3_spmd.sunk | while | flops 1414834176 | bytes 12899519 | solution.py:76
  112.1 3.0 bitcast_reduce_fusion.2
  115.2 1.7 bitcast_dynamic-update-slice_fusion.4
  120.2 3.0 bitcast_reduce_fusion.2
  128.3 3.0 bitcast_reduce_fusion.2
  131.4 1.7 bitcast_dynamic-update-slice_fusion.4
  136.5 3.0 bitcast_reduce_fusion.2
  139.5 1.8 bitcast_dynamic-update-slice_fusion.4
  144.6 3.0 bitcast_reduce_fusion.2
  147.7 1.8 bitcast_dynamic-update-slice_fusion.4
  152.8 3.0 bitcast_reduce_fusion.2
  160.9 3.0 bitcast_reduce_fusion.2
  169.0 2.9 bitcast_reduce_fusion.2
  172.0 1.7 bitcast_dynamic-update-slice_fusion.4
  175.7 16.0 %all_to_all.22 = bf16[32,2,896]{2,1,0:T(2,128)(2,1)S(1)} all-to-all(bf16[32,2,896]{2,1,0:T(2,128)(2,1)S(1)} %reshape.72), channel_id=1, replica_groups=mesh['dp'=32,'tensor'=8] {'dp'}, dimensions={0} | all-to-all | bytes 229376 | tf_op jit(solution)/shard_map/all_to_all | solution.py:80
  191.6 6.0 %all-to-all-start = ((bf16[32,128,1792]{2,1,0:T(8,128)(2,1)}), bf16[32,128,1792]{2,1,0:T(8,128)(2,1)}, u32[]{:S(2)}, u32[]{:S(2)}) async-start(bf16[32,128,1792]{2,1,0:T(8,128)(2,1)} %bitcast.54), calls=%async_computation | async-start | bytes 29360128 | tf_op jit(solution)/shard_map/all_to_all | solution.py:79
  197.8 247.6 %all-to-all-done = bf16[32,128,1792]{2,1,0:T(8,128)(2,1)} async-done(((bf16[32,128,1792]{2,1,0:T(8,128)(2,1)}), bf16[32,128,1792]{2,1,0:T(8,128)(2,1)}, u32[]{:S(2)}, u32[]{:S(2)}) %all-to-all-start) | async-done | bytes 14680096 | tf_op jit(solution)/shard_map/all_to_all | solution.py:79
  445.4 14.1 %fusion.7 = bf16[4096,1792]{1,0:T(8,128)(2,1)} fusion(bf16[4096,1792]{1,0:T(8,128)(2,1)} %bitcast.9, f32[32,1792]{1,0:T(8,128)S(1)} %bitcast.58), kind=kLoop, calls=%fused_computation.14 | loop fusion | flops 22020096 | bytes 29589504 | tf_op jit(solution)/shard_map/convert_element_type | solution.py:32
  459.5 8.5 %convert_reduce_fusion = f32[128,1792]{1,0:T(8,128)} fusion(bf16[32,128,1792]{2,1,0:T(8,128)(2,1)} %bitcast.52), kind=kLoop, calls=%fused_computation.12 | loop fusion | flops 14450688 | bytes 15597568 | tf_op jit(solution)/shard_map/reduce_sum | solution.py:84
  (67 shorter events, 21.3 us)
Async XLA Ops:
  6.5 2.6 copy-start.1
  6.5 78.3 %all-gather.3.cloned.1.call-start = ((), (), s32[]{:S(2)}) async-start(), calls=%async_computation.2 | async-start | bytes 7077888 | tf_op jit(solution)/shard_map/all_gather | solution.py:57
  91.9 16.8 %copy-start = (bf16[768,1792]{1,0:T(8,128)(2,1)S(1)}, bf16[768,1792]{1,0:T(8,128)(2,1)}, u32[]{:S(2)}) copy-start(bf16[768,1792]{1,0:T(8,128)(2,1)} %param.8) | copy-start | bytes 8257540
  91.9 16.8 %copy-start.2 = (f32[1,1792]{1,0:T(1,128)S(1)}, f32[1,1792]{1,0:T(1,128)}, u32[]{:S(2)}) copy-start(f32[1,1792]{1,0:T(1,128)} %param.10) | copy-start | bytes 21508
  191.6 253.7 %all-to-all-start = ((bf16[32,128,1792]{2,1,0:T(8,128)(2,1)}), bf16[32,128,1792]{2,1,0:T(8,128)(2,1)}, u32[]{:S(2)}, u32[]{:S(2)}) async-start(bf16[32,128,1792]{2,1,0:T(8,128)(2,1)} %bitcast.54), calls=%async_computation | async-start | bytes 29360128 | tf_op jit(solution)/shard_map/all_to_all | solution.py:79
Sparse Core Ops, SparseCore 0:
  12.7 72.0 all-gather.2
where the time goes:
time: 481 us; the launch traced here: 475 us
  waiting for transfers between devices  302 us (63%)
  other arithmetic  60.4 us (13%)
  blocking collectives  33.2 us (7%)
  matrix products  23.9 us (5%)
  local copies, waits for them, and re-layouts  19.7 us (4%)
  loops' own time  15.7 us (3%)
  between operations  13.5 us (3%)
  starting transfers between devices  6.01 us (1%)
    all_to_all x1, waiting for transfers between devices, per_device(): lax.all_to_all(all_codes, 'dp', split_axis=0, concat_axis=0, tiled=True)  248 us
    all_gather x1, waiting for transfers between devices, per_device(): lax.all_gather(y_code, 'tensor', axis=0, tiled=True)  54.7 us
    dot_general x8, matrix products, feature_tile(): lax.dot_general(feat_cols, activations, (((0,), (0,)), ((), ())), preferr...  23.9 us
    all_gather x1, blocking collectives, per_device(): lax.all_gather(y_scale, 'tensor', axis=0, tiled=True)  17.3 us
    convert_element_type x1, other arithmetic, decode_rows(): return values.reshape(row_total, block_count * BLOCK).astype(jnp.bfloat16)  16.8 us
    all_to_all x1, blocking collectives, per_device(): lax.all_to_all(all_scales, 'dp', split_axis=0, concat_axis=0, tiled=True)  16 us
    another operation x1, loops' own time, per_device(): code_tiles, scale_tiles = lax.map(feature_tile, tile_starts)  15.7 us
    dynamic_update_slice x16, other arithmetic, per_device(): code_tiles, scale_tiles = lax.map(feature_tile, tile_starts)  14.2 us
  transfers between devices with their start and end apart: 2, of which 2 were waited for; matrix products, arithmetic and copies ran while one was open for 0% of the time, Pallas kernels for 0%

commit v1 on v0

v1 whole, which is shorter than its diff:
```python
import jax
import jax.numpy as jnp
from jax import lax
from jax.sharding import PartitionSpec as P

BLOCK = 128
Y_LEVELS = 8
W_LEVELS = 7
COL_CHUNKS = 2


epsilon = 1e-06


def code_rows(grad_out, grad_dither):
    row_count, feat_width = grad_out.shape
    block_count = feat_width // BLOCK
    grad_float = grad_out.astype(jnp.float32).reshape(row_count, block_count, BLOCK)
    magnitude = jnp.max(jnp.abs(grad_float), axis=2)
    y_scale = ((magnitude + epsilon) / Y_LEVELS).astype(jnp.bfloat16)
    scaled = grad_float / y_scale.astype(jnp.float32)[:, :, None]
    y_code = (scaled.reshape(row_count, feat_width) + grad_dither).astype(jnp.bfloat16)
    held = lax.optimization_barrier(y_code).astype(jnp.float32)
    values = held.reshape(row_count, block_count, BLOCK) * y_scale.astype(jnp.float32)[:, :, None]
    return values.reshape(row_count, feat_width).astype(jnp.bfloat16)


def group_terms(partial_value, feature_part, hidden_part):
    feat_rows, unit_cols = partial_value.shape
    block_count = feat_rows // BLOCK
    blocks = partial_value.reshape(block_count, BLOCK, unit_cols)
    magnitude = jnp.max(jnp.abs(blocks), axis=1)
    block_scale = ((magnitude + epsilon) / W_LEVELS).astype(jnp.bfloat16)
    scaled = (blocks / block_scale.astype(jnp.float32)[:, None, :]).reshape(feat_rows, unit_cols)
    code_block = (scaled + hidden_part[None, :] + feature_part[:, None]).astype(jnp.bfloat16)
    held = lax.optimization_barrier(code_block).astype(jnp.float32)
    values = held.reshape(block_count, BLOCK, unit_cols) * block_scale.astype(jnp.float32)[:, None, :]
    return values.reshape(feat_rows, unit_cols).astype(jnp.bfloat16)


def per_device(grad_out, activations, grad_dither, hidden_dither, feature_dither):
    feat_width = grad_out.shape[1]
    y_local = code_rows(grad_out, grad_dither)
    y_hat = lax.all_gather(y_local, "tensor", axis=0, tiled=True)
    unit_count = activations.shape[1]
    owners = lax.axis_size("dp")
    own_rows = feat_width // owners
    hidden_noise = hidden_dither[0]
    feature_noise = feature_dither[0]
    width = unit_count // COL_CHUNKS
    sums = []
    for chunk in range(COL_CHUNKS):
        cols = slice(chunk * width, (chunk + 1) * width)
        partial_value = lax.dot_general(
            y_hat, activations[:, cols], (((0,), (0,)), ((), ())), preferred_element_type=jnp.float32
        )
        terms = group_terms(partial_value, feature_noise, hidden_noise[cols])
        arrived = lax.all_to_all(terms, "dp", split_axis=0, concat_axis=0, tiled=True)
        held = lax.optimization_barrier(arrived).astype(jnp.float32)
        sums.append(jnp.sum(held.reshape(owners, own_rows, width), axis=0))
    return jnp.concatenate(sums, axis=1)


def solution(mesh):
    placed = (
        P(("dp", "tensor"), None),
        P("dp", "tensor"),
        P(("dp", "tensor"), None),
        P("dp", "tensor"),
        P("dp", None),
    )
    return jax.shard_map(
        per_device, mesh=mesh, in_specs=placed, out_specs=P("dp", "tensor"), check_vma=False
    )
```

time: 481 us -> 384 us (0.80)
  blocking collectives: 33.2 us -> 0 us
  waiting for transfers between devices: 302 us -> 279 us
  other arithmetic: 60.4 us -> 37.6 us
  starting transfers between devices: 6.01 us -> 27.1 us
  local copies, waits for them, and re-layouts: 19.7 us -> 0.79 us
  loops' own time: 15.7 us -> 0 us
    all_to_all x1 -> x2, waiting for transfers between devices: 248 us -> 207 us  [per_device(): lax.all_to_all(terms, 'dp', split_axis=0, concat_axis=0, tiled=True)]
    all_to_all x1 -> x2, starting transfers between devices: 6.01 us -> 27.1 us  [per_device(): lax.all_to_all(terms, 'dp', split_axis=0, concat_axis=0, tiled=True)]
    all_gather x1, waiting for transfers between devices: 54.7 us -> 72.1 us  [per_device(): y_hat = lax.all_gather(y_local, 'tensor', axis=0, tiled=True)]
    all_gather x1 -> x0, blocking collectives: 17.3 us -> none  [per_device(): lax.all_gather(y_scale, 'tensor', axis=0, tiled=True)]
    all_to_all x1 -> x0, blocking collectives: 16 us -> none  [per_device(): lax.all_to_all(all_scales, 'dp', split_axis=0, concat_axis=0, tiled=True)]
    another operation x1 -> x0, loops' own time: 15.7 us -> none  [per_device(): code_tiles, scale_tiles = lax.map(feature_tile, tile_starts)]
    dynamic_update_slice x16 -> x0, other arithmetic: 14.2 us -> none  [per_device(): code_tiles, scale_tiles = lax.map(feature_tile, tile_starts)]
    dynamic_slice x16 -> x0, local copies, waits for them, and re-layouts: 10.9 us -> none  [the longest x8 6.22 us: feature_tile(): lax.dynamic_slice_in_dim(feature_noise, tile_start, ROW_TILE, 0)]
  transfers between devices with their start and end apart: 2 -> 3, of which waited for: 2 -> 3; matrix products, arithmetic and copies ran while one was open for 0% -> 3% of each run, Pallas kernels for 0% -> 0%
where the time goes in v1:
time: 384 us; the launch traced here: 378 us
  waiting for transfers between devices  279 us (73%)
  other arithmetic  37.6 us (10%)
  starting transfers between devices  27.1 us (7%)
  matrix products  20.3 us (5%)
  between operations  13.5 us (4%)
    all_to_all x2, waiting for transfers between devices, per_device(): lax.all_to_all(terms, 'dp', split_axis=0, concat_axis=0, tiled=True)  207 us
    all_gather x1, waiting for transfers between devices, per_device(): y_hat = lax.all_gather(y_local, 'tensor', axis=0, tiled=True)  72.1 us
    all_to_all x2, starting transfers between devices, per_device(): lax.all_to_all(terms, 'dp', split_axis=0, concat_axis=0, tiled=True)  27.1 us
    dot_general x2, matrix products, per_device(): lax.dot_general(y_hat, activations[:, cols], (((0,), (0,)), ((), ())), pr...  20.3 us
    convert_element_type x2, other arithmetic, group_terms(): return values.reshape(feat_rows, unit_cols).astype(jnp.bfloat16)  12.1 us
    convert_element_type x1, other arithmetic, group_terms(): (scaled + hidden_part[None, :] + feature_part[:, None]).astype(jnp.bfloat16)  9.97 us
    reduce_sum x2, other arithmetic, per_device(): sums.append(jnp.sum(held.reshape(owners, own_rows, width), axis=0))  8.3 us
  transfers between devices with their start and end apart: 3, of which 3 were waited for; matrix products, arithmetic and copies ran while one was open for 3% of the time, Pallas kernels for 0%

profile of v1, /device:TPU:32, one launch (start us, length us, event | category | flops | bytes accessed | tf_op | source)
XLA Modules:
  0.0 378.3 jit_solution(3777527201818774682)
XLA Ops:
  6.5 0.0 all-gather.2.cloned.1.call-start
  6.5 1.4 fusion.8
  7.9 0.0 copy-start.2
  7.9 0.3 copy.6
  8.2 0.5 reduce_max.27
  8.7 0.5 div.47
  9.2 2.5 fusion.10
  11.7 1.8 fusion.11
  13.5 0.0 all-gather.2.cloned.1.call-update
  13.6 0.0 copy-start.4
  13.6 72.1 %all-gather.2.cloned.1.call-done = bf16[768,4096]{1,0:T(8,128)(2,1)} async-done(((bf16[96,4096]{1,0:T(8,128)(2,1)}), bf16[768,4096]{1,0:T(8,128)(2,1)}) %all-gather.2.cloned.1.call-update) | async-done | bytes 6291472 | tf_op jit(solution)/shard_map/all_gather | solution.py:44
  85.7 10.0 %bitcast_reduce_fusion = (f32[32,896]{1,0:T(8,128)S(1)}, f32[4096,896]{1,0:T(8,128)S(1)}) fusion(bf16[768,4096]{1,0:T(8,128)(2,1)} %all-gather.2.cloned.1.call-done, bf16[768,1792]{1,0:T(8,128)(2,1)} %param.6), kind=kOutput, calls=%fused_computation.14 | convolution fusion | flops 5644455936 | bytes 22462464 | tf_op jit(solution)/shard_map/dot_general | solution.py:54
  95.7 0.0 copy-start.1
  95.7 10.3 %bitcast_reduce_fusion.1 = (f32[32,896]{1,0:T(8,128)S(1)}, f32[4096,896]{1,0:T(8,128)}) fusion(bf16[768,4096]{1,0:T(8,128)(2,1)S(1)} %copy-done.3, bf16[768,1792]{1,0:T(8,128)(2,1)S(1)} %copy-done.4), kind=kOutput, calls=%fused_computation.15 | convolution fusion | flops 5644455936 | bytes 22462464 | tf_op jit(solution)/shard_map/dot_general | solution.py:54
  106.1 10.0 %fusion.2 = (bf16[4096,896]{1,0:T(8,128)(2,1)}, bf16[4096,896]{1,0:T(8,128)(2,1)S(1)}) fusion(f32[4096,896]{1,0:T(8,128)} %get-tuple-element.10, f32[4096]{0:T(1024)S(1)} %bitcast.51, f32[896]{0:T(1024)S(1)} %get-tuple-element.5, f32[32,896]{1,0:T(8,128)S(1)} %get-tuple-element.13, f32[896]{0:T(1024)S(1)} %get-tuple-element.6, ...), kind=kLoop, calls=%fused_computation.6 | loop fusion | flops 29360128 | bytes 44293120 | tf_op jit(solution)/shard_map/convert_element_type | solution.py:35
  116.0 4.6 %fusion.7 = bf16[4096,896]{1,0:T(8,128)(2,1)} fusion(bf16[4096,896]{1,0:T(8,128)(2,1)S(1)} %get-tuple-element.8, f32[32,896]{1,0:T(8,128)S(1)} %get-tuple-element.14), kind=kLoop, calls=%fused_computation.11 | loop fusion | flops 11010048 | bytes 14794752 | tf_op jit(solution)/shard_map/convert_element_type | solution.py:38
  120.6 8.7 %all-to-all-start.1 = ((bf16[32,128,896]{2,1,0:T(8,128)(2,1)}), bf16[32,128,896]{2,1,0:T(8,128)(2,1)}, u32[]{:S(2)}, u32[]{:S(2)}) async-start(bf16[32,128,896]{2,1,0:T(8,128)(2,1)} %bitcast.47), calls=%async_computation.1 | async-start | bytes 14680064 | tf_op jit(solution)/shard_map/all_to_all | solution.py:58
  129.3 7.5 %fusion.3 = bf16[4096,896]{1,0:T(8,128)(2,1)} fusion(bf16[4096,896]{1,0:T(8,128)(2,1)} %get-tuple-element.7, f32[32,896]{1,0:T(8,128)S(1)} %get-tuple-element.13), kind=kLoop, calls=%fused_computation.7 | loop fusion | flops 11010048 | bytes 14794752 | tf_op jit(solution)/shard_map/convert_element_type | solution.py:38
  136.8 106.1 %all-to-all-done.1 = bf16[32,128,896]{2,1,0:T(8,128)(2,1)} async-done(((bf16[32,128,896]{2,1,0:T(8,128)(2,1)}), bf16[32,128,896]{2,1,0:T(8,128)(2,1)}, u32[]{:S(2)}, u32[]{:S(2)}) %all-to-all-start.1) | async-done | bytes 7340064 | tf_op jit(solution)/shard_map/all_to_all | solution.py:58
  242.9 18.5 %all-to-all-start = ((bf16[32,128,896]{2,1,0:T(8,128)(2,1)}), bf16[32,128,896]{2,1,0:T(8,128)(2,1)}, u32[]{:S(2)}, u32[]{:S(2)}) async-start(bf16[32,128,896]{2,1,0:T(8,128)(2,1)} %bitcast.46), calls=%async_computation | async-start | bytes 14680064 | tf_op jit(solution)/shard_map/all_to_all | solution.py:58
  261.4 4.2 %convert_reduce_fusion = f32[128,896]{1,0:T(8,128)S(1)} fusion(bf16[32,128,896]{2,1,0:T(8,128)(2,1)} %bitcast.12), kind=kLoop, calls=%fused_computation.12 | loop fusion | flops 7225344 | bytes 7798784 | tf_op jit(solution)/shard_map/reduce_sum | solution.py:60
  265.5 100.8 %all-to-all-done = bf16[32,128,896]{2,1,0:T(8,128)(2,1)} async-done(((bf16[32,128,896]{2,1,0:T(8,128)(2,1)}), bf16[32,128,896]{2,1,0:T(8,128)(2,1)}, u32[]{:S(2)}, u32[]{:S(2)}) %all-to-all-start) | async-done | bytes 7340064 | tf_op jit(solution)/shard_map/all_to_all | solution.py:58
  366.4 4.2 %convert_reduce_fusion.1 = f32[128,896]{1,0:T(8,128)S(1)} fusion(bf16[32,128,896]{2,1,0:T(8,128)(2,1)} %bitcast.11), kind=kLoop, calls=%fused_computation.13 | loop fusion | flops 7225344 | bytes 7798784 | tf_op jit(solution)/shard_map/reduce_sum | solution.py:60
  370.5 1.0 pad_maximum_fusion
  (10 shorter events, 0.1 us)
Async XLA Ops:
  6.5 2.6 copy-start
  6.5 79.2 %all-gather.2.cloned.1.call-start = ((), (), s32[]{:S(2)}) async-start(), calls=%async_computation.2 | async-start | bytes 7077888 | tf_op jit(solution)/shard_map/all_gather | solution.py:44
  7.9 5.6 %copy-start.2 = (f32[1,1792]{1,0:T(1,128)S(1)}, f32[1,1792]{1,0:T(1,128)}, u32[]{:S(2)}) copy-start(f32[1,1792]{1,0:T(1,128)} %param.8) | copy-start | bytes 21508
  13.6 82.1 %copy-start.4 = (bf16[768,1792]{1,0:T(8,128)(2,1)S(1)}, bf16[768,1792]{1,0:T(8,128)(2,1)}, u32[]{:S(2)}) copy-start(bf16[768,1792]{1,0:T(8,128)(2,1)} %param.6) | copy-start | bytes 8257540
  85.7 10.0 %copy-start.3 = (bf16[768,4096]{1,0:T(8,128)(2,1)S(1)}, bf16[768,4096]{1,0:T(8,128)(2,1)}, u32[]{:S(2)}) copy-start(bf16[768,4096]{1,0:T(8,128)(2,1)} %all-gather.2.cloned.1.call-done) | copy-start | bytes 18874372
  95.7 10.4 %copy-start.1 = (f32[1,4096]{1,0:T(1,128)S(1)}, f32[1,4096]{1,0:T(1,128)}, u32[]{:S(2)}) copy-start(f32[1,4096]{1,0:T(1,128)} %param.9) | copy-start | bytes 49156
  120.6 122.3 %all-to-all-start.1 = ((bf16[32,128,896]{2,1,0:T(8,128)(2,1)}), bf16[32,128,896]{2,1,0:T(8,128)(2,1)}, u32[]{:S(2)}, u32[]{:S(2)}) async-start(bf16[32,128,896]{2,1,0:T(8,128)(2,1)} %bitcast.47), calls=%async_computation.1 | async-start | bytes 14680064 | tf_op jit(solution)/shard_map/all_to_all | solution.py:58
  242.9 123.5 %all-to-all-start = ((bf16[32,128,896]{2,1,0:T(8,128)(2,1)}), bf16[32,128,896]{2,1,0:T(8,128)(2,1)}, u32[]{:S(2)}, u32[]{:S(2)}) async-start(bf16[32,128,896]{2,1,0:T(8,128)(2,1)} %bitcast.46), calls=%async_computation | async-start | bytes 14680064 | tf_op jit(solution)/shard_map/all_to_all | solution.py:58
Sparse Core Ops, SparseCore 0:
  13.6 72.0 all-gather.1

commit v2 on v1

--- a/solution.py
+++ b/solution.py
@@ -6,7 +6,6 @@
 BLOCK = 128
 Y_LEVELS = 8
 W_LEVELS = 7
-COL_CHUNKS = 2
 
 
 epsilon = 1e-06
@@ -38,27 +37,78 @@
     return values.reshape(feat_rows, unit_cols).astype(jnp.bfloat16)
 
 
+def ring_perm(step_of):
+    return [(i, step_of(i)) for i in range(32)]
+
+
+def x_of(i):
+    return (i // 2) % 4
+
+
+def y_of(i):
+    return i // 8
+
+
+def dp_index(y, x, z):
+    return y * 8 + x * 2 + z
+
+
+X_FWD = ring_perm(lambda i: dp_index(y_of(i), (x_of(i) + 1) % 4, i % 2))
+X_BWD = ring_perm(lambda i: dp_index(y_of(i), (x_of(i) + 3) % 4, i % 2))
+Y_FWD = ring_perm(lambda i: dp_index((y_of(i) + 1) % 4, x_of(i), i % 2))
+Y_BWD = ring_perm(lambda i: dp_index((y_of(i) + 3) % 4, x_of(i), i % 2))
+Z_SWAP = ring_perm(lambda i: i ^ 1)
+
+
+def chunk(data, index):
+    return lax.dynamic_index_in_dim(data, index, axis=0, keepdims=False)
+
+
+def ring_reduce(local, pos, fwd, bwd):
+    n = local.shape[0]
+    half = local.shape[-2] // 2
+    right_local = local[..., :half, :]
+    left_local = local[..., half:, :]
+    right_acc = chunk(right_local, (pos + n - 1) % n).astype(jnp.float32)
+    left_acc = chunk(left_local, (pos + 1) % n).astype(jnp.float32)
+    for step in range(n - 1):
+        right_got = lax.ppermute(right_acc.astype(jnp.bfloat16), "dp", fwd)
+        left_got = lax.ppermute(left_acc.astype(jnp.bfloat16), "dp", bwd)
+        right_acc = right_got.astype(jnp.float32) + chunk(right_local, (pos + 2 * n - step - 2) % n).astype(jnp.float32)
+        left_acc = left_got.astype(jnp.float32) + chunk(left_local, (pos + step + 2) % n).astype(jnp.float32)
+    return jnp.concatenate([right_acc, left_acc], axis=-2)
+
+
+def reduce_terms(terms, owners):
+    feat_rows, unit_cols = terms.shape
+    own_rows = feat_rows // owners
+    width = unit_cols // 2
+    dp = lax.axis_index("dp")
+    y, x, z = dp // 8, (dp // 2) % 4, dp % 2
+    blocks = terms.reshape(4, 4, 2, own_rows, unit_cols)
+    first = blocks[..., :width]
+    second = blocks[..., width:]
+    first = ring_reduce(jnp.swapaxes(first, 0, 1), x, X_FWD, X_BWD)
+    second = ring_reduce(second, y, Y_FWD, Y_BWD)
+    first = ring_reduce(first, y, Y_FWD, Y_BWD)
+    second = ring_reduce(second, x, X_FWD, X_BWD)
+    both = jnp.stack([first, second])
+    mine = lax.dynamic_index_in_dim(both, z, axis=1, keepdims=False)
+    other = lax.dynamic_index_in_dim(both, 1 - z, axis=1, keepdims=False)
+    got = lax.ppermute(other.astype(jnp.bfloat16), "dp", Z_SWAP)
+    total = mine + got.astype(jnp.float32)
+    return jnp.concatenate([total[0], total[1]], axis=1)
+
+
 def per_device(grad_out, activations, grad_dither, hidden_dither, feature_dither):
-    feat_width = grad_out.shape[1]
     y_local = code_rows(grad_out, grad_dither)
     y_hat = lax.all_gather(y_local, "tensor", axis=0, tiled=True)
-    unit_count = activations.shape[1]
     owners = lax.axis_size("dp")
-    own_rows = feat_width // owners
-    hidden_noise = hidden_dither[0]
-    feature_noise = feature_dither[0]
-    width = unit_count // COL_CHUNKS
-    sums = []
-    for chunk in range(COL_CHUNKS):
-        cols = slice(chunk * width, (chunk + 1) * width)
-        partial_value = lax.dot_general(
-            y_hat, activations[:, cols], (((0,), (0,)), ((), ())), preferred_element_type=jnp.float32
-        )
-        terms = group_terms(partial_value, feature_noise, hidden_noise[cols])
-        arrived = lax.all_to_all(terms, "dp", split_axis=0, concat_axis=0, tiled=True)
-        held = lax.optimization_barrier(arrived).astype(jnp.float32)
-        sums.append(jnp.sum(held.reshape(owners, own_rows, width), axis=0))
-    return jnp.concatenate(sums, axis=1)
+    partial_value = lax.dot_general(
+        y_hat, activations, (((0,), (0,)), ((), ())), preferred_element_type=jnp.float32
+    )
+    terms = group_terms(partial_value, feature_dither[0], hidden_dither[0])
+    return reduce_terms(terms, owners)
 
 
 def solution(mesh):

time: 384 us -> 275 us (0.72)
  the two profiles are of different devices: /device:TPU:32 before, /device:TPU:30 now
where the time goes in v2:
time: 275 us; the launch traced here: 271 us
  waiting for transfers between devices  133 us (48%)
  other arithmetic  47.8 us (17%)
  starting transfers between devices  28.6 us (10%)
  local copies, waits for them, and re-layouts  27.5 us (10%)
  matrix products  19.8 us (7%)
  between operations  14.1 us (5%)
    all_gather x1, waiting for transfers between devices, per_device(): y_hat = lax.all_gather(y_local, 'tensor', axis=0, tiled=True)  72.9 us
    ppermute x12, waiting for transfers between devices, ring_reduce(): right_got = lax.ppermute(right_acc.astype(jnp.bfloat16), 'dp', fwd)  31 us
    ppermute x12, waiting for transfers between devices, ring_reduce(): left_got = lax.ppermute(left_acc.astype(jnp.bfloat16), 'dp', bwd)  21.4 us
    dot_general x1, matrix products, per_device(): lax.dot_general(y_hat, activations, (((0,), (0,)), ((), ())), preferred_e...  19.8 us
    ppermute x12, starting transfers between devices, ring_reduce(): right_got = lax.ppermute(right_acc.astype(jnp.bfloat16), 'dp', fwd)  18.9 us
    convert_element_type x1, other arithmetic, group_terms(): (scaled + hidden_part[None, :] + feature_part[:, None]).astype(jnp.bfloat16)  12.6 us
    unnamed x23, local copies, waits for them, and re-layouts  9.31 us
    ppermute x12, starting transfers between devices, ring_reduce(): left_got = lax.ppermute(left_acc.astype(jnp.bfloat16), 'dp', bwd)  9.16 us
  transfers between devices with their start and end apart: 26, of which 15 were waited for; matrix products, arithmetic and copies ran while one was open for 11% of the time, Pallas kernels for 0%

profile of v2, /device:TPU:30, one launch (start us, length us, event | category | flops | bytes accessed | tf_op | source)
XLA Modules:
  0.0 271.0 jit_solution(18006083838538167737)
XLA Ops:
  9.4 2.6 reduce_max.18
  16.8 72.9 %all-gather.2.cloned.1.call-done = bf16[768,4096]{1,0:T(8,128)(2,1)} async-done(((bf16[96,4096]{1,0:T(8,128)(2,1)}), bf16[768,4096]{1,0:T(8,128)(2,1)}) %all-gather.2.cloned.1.call-update) | async-done | bytes 6291472 | tf_op jit(solution)/shard_map/all_gather | solution.py:105
  89.7 19.8 %bitcast_reduce_fusion = (f32[32,1792]{1,0:T(8,128)S(1)}, f32[4096,1792]{1,0:T(8,128)}) fusion(bf16[768,4096]{1,0:T(8,128)(2,1)} %all-gather.2.cloned.1.call-done, bf16[768,1792]{1,0:T(8,128)(2,1)S(1)} %copy-done), kind=kOutput, calls=%fused_computation.6 | convolution fusion | flops 11288911872 | bytes 38633472 | tf_op jit(solution)/shard_map/dot_general | solution.py:107
  109.6 12.6 %fusion.2 = bf16[4096,1792]{1,0:T(8,128)(2,1)S(1)} fusion(f32[4096,1792]{1,0:T(8,128)} %get-tuple-element.12, f32[4096]{0:T(1024)S(1)} %bitcast.153, f32[1792]{0:T(1024)S(1)} %reduce, f32[32,1792]{1,0:T(8,128)S(1)} %fusion.34), kind=kLoop, calls=%fused_computation.4 | loop fusion | flops 29360128 | bytes 44293120 | tf_op jit(solution)/shard_map/convert_element_type | solution.py:34
  122.1 3.2 %fusion.3 = bf16[4096,1792]{1,0:T(8,128)(2,1)S(1)} fusion(bf16[4096,1792]{1,0:T(8,128)(2,1)S(1)} %fusion.2, f32[32,1792]{1,0:T(8,128)S(1)} %fusion.34), kind=kLoop, calls=%fused_computation.5 | loop fusion | flops 22020096 | bytes 29589504 | tf_op jit(solution)/shard_map/convert_element_type | solution.py:37
  125.3 5.2 %copy-done.2 = bf16[4096,1792]{1,0:T(8,128)(2,1)} copy-done((bf16[4096,1792]{1,0:T(8,128)(2,1)}, bf16[4096,1792]{1,0:T(8,128)(2,1)S(1)}, u32[]{:S(2)}) %copy-start.2) | copy-done | bytes 14680088
  130.5 3.9 %fusion.36 = (bf16[4,4,2,64,896]{4,3,2,1,0:T(8,128)(2,1)}, bf16[4,4,2,64,896]{4,3,2,1,0:T(8,128)(2,1)}) fusion(bf16[4,4,2,128,1792]{4,3,2,1,0:T(8,128)(2,1)S(1)} %bitcast.148), kind=kLoop, calls=%fused_computation.86 | loop fusion | bytes 14680064 | tf_op jit(solution)/shard_map/slice | solution.py:70
  134.4 4.0 %slice_bitcast_fusion = bf16[4,4,2,128,896]{4,3,2,0,1:T(8,128)(2,1)S(1)} fusion(bf16[4,4,2,128,1792]{4,3,2,1,0:T(8,128)(2,1)} %bitcast.149), kind=kLoop, calls=%fused_computation.7 | loop fusion | bytes 14680064 | tf_op jit(solution)/shard_map/transpose | solution.py:91
  145.0 2.8 %fusion.37 = (bf16[4,4,2,64,896]{4,3,2,0,1:T(8,128)(2,1)S(1)}, bf16[4,4,2,64,896]{4,3,2,0,1:T(8,128)(2,1)}) fusion(bf16[4,4,2,128,896]{4,3,2,0,1:T(8,128)(2,1)S(1)} %slice_bitcast_fusion), kind=kLoop, calls=%fused_computation.87 | loop fusion | bytes 14680064 | tf_op jit(solution)/shard_map/slice | solution.py:70
  154.1 9.4 %collective-permute-done.12 = bf16[4,2,64,896]{3,2,1,0:T(8,128)(2,1)} collective-permute-done((bf16[4,2,64,896]{3,2,1,0:T(8,128)(2,1)}, bf16[4,2,64,896]{3,2,1,0:T(8,128)(2,1)}, u32[]{:S(2)}, u32[]{:S(2)}) %collective-permute-start.12) | collective-permute-done | bytes 917536 | tf_op jit(solution)/shard_map/ppermute | solution.py:75
  163.5 2.6 fusion.7
  175.9 2.6 fusion.9
  178.7 9.4 %collective-permute-done.13 = bf16[4,2,64,896]{3,2,1,0:T(8,128)(2,1)} collective-permute-done((bf16[4,2,64,896]{3,2,1,0:T(8,128)(2,1)}, bf16[4,2,64,896]{3,2,1,0:T(8,128)(2,1)}, u32[]{:S(2)}, u32[]{:S(2)}) %collective-permute-start.13) | collective-permute-done | bytes 917536 | tf_op jit(solution)/shard_map/ppermute | solution.py:75
  188.1 2.7 fusion.6
  190.8 3.0 %collective-permute-start.14 = (bf16[4,2,64,896]{3,2,1,0:T(8,128)(2,1)}, bf16[4,2,64,896]{3,2,1,0:T(8,128)(2,1)}, u32[]{:S(2)}, u32[]{:S(2)}) collective-permute-start(bf16[4,2,64,896]{3,2,1,0:T(8,128)(2,1)} %fusion.6), channel_id=1, source_target_pairs={{0,64},{8,72},{16,80},{24,88},{32,96},{40,104},{48,112},{56,120},{... | collective-permute-start | bytes 2752520 | tf_op jit(solution)/shard_map/ppermute | solution.py:75
  202.3 10.5 %collective-permute-done.14 = bf16[4,2,64,896]{3,2,1,0:T(8,128)(2,1)} collective-permute-done((bf16[4,2,64,896]{3,2,1,0:T(8,128)(2,1)}, bf16[4,2,64,896]{3,2,1,0:T(8,128)(2,1)}, u32[]{:S(2)}, u32[]{:S(2)}) %collective-permute-start.14) | collective-permute-done | bytes 917536 | tf_op jit(solution)/shard_map/ppermute | solution.py:75
  214.9 2.7 collective-permute-done.20
  221.8 2.7 %collective-permute-start.3 = (bf16[2,64,896]{2,1,0:T(8,128)(2,1)S(1)}, bf16[2,64,896]{2,1,0:T(8,128)(2,1)S(1)}, u32[]{:S(2)}, u32[]{:S(2)}) collective-permute-start(bf16[2,64,896]{2,1,0:T(8,128)(2,1)S(1)} %fusion.30), channel_id=1, source_target_pairs={{0,64},{8,72},{16,80},{24,88},{32,96},{40,104},{48,112},{56,120},{... | collective-permute-start | bytes 688136 | tf_op jit(solution)/shard_map/ppermute | solution.py:75
  229.2 3.0 %collective-permute-start.4 = (bf16[2,64,896]{2,1,0:T(8,128)(2,1)S(1)}, bf16[2,64,896]{2,1,0:T(8,128)(2,1)S(1)}, u32[]{:S(2)}, u32[]{:S(2)}) collective-permute-start(bf16[2,64,896]{2,1,0:T(8,128)(2,1)S(1)} %fusion.29), channel_id=1, source_target_pairs={{0,64},{8,72},{16,80},{24,88},{32,96},{40,104},{48,112},{56,120},{... | collective-permute-start | bytes 688136 | tf_op jit(solution)/shard_map/ppermute | solution.py:75
  232.2 3.3 %collective-permute-done.9 = bf16[2,64,896]{2,1,0:T(8,128)(2,1)S(1)} collective-permute-done((bf16[2,64,896]{2,1,0:T(8,128)(2,1)S(1)}, bf16[2,64,896]{2,1,0:T(8,128)(2,1)S(1)}, u32[]{:S(2)}, u32[]{:S(2)}) %collective-permute-start.9) | collective-permute-done | bytes 229408 | tf_op jit(solution)/shard_map/ppermute | solution.py:76
  238.1 3.3 %collective-permute-start.5 = (bf16[2,64,896]{2,1,0:T(8,128)(2,1)S(1)}, bf16[2,64,896]{2,1,0:T(8,128)(2,1)S(1)}, u32[]{:S(2)}, u32[]{:S(2)}) collective-permute-start(bf16[2,64,896]{2,1,0:T(8,128)(2,1)S(1)} %fusion.28), channel_id=1, source_target_pairs={{0,64},{8,72},{16,80},{24,88},{32,96},{40,104},{48,112},{56,120},{... | collective-permute-start | bytes 688136 | tf_op jit(solution)/shard_map/ppermute | solution.py:75
  241.4 3.3 %collective-permute-done.10 = bf16[2,64,896]{2,1,0:T(8,128)(2,1)S(1)} collective-permute-done((bf16[2,64,896]{2,1,0:T(8,128)(2,1)S(1)}, bf16[2,64,896]{2,1,0:T(8,128)(2,1)S(1)}, u32[]{:S(2)}, u32[]{:S(2)}) %collective-permute-start.10) | collective-permute-done | bytes 229408 | tf_op jit(solution)/shard_map/ppermute | solution.py:76
  245.0 6.9 %collective-permute-done.11 = bf16[2,64,896]{2,1,0:T(8,128)(2,1)S(1)} collective-permute-done((bf16[2,64,896]{2,1,0:T(8,128)(2,1)S(1)}, bf16[2,64,896]{2,1,0:T(8,128)(2,1)S(1)}, u32[]{:S(2)}, u32[]{:S(2)}) %collective-permute-start.11) | collective-permute-done | bytes 229408 | tf_op jit(solution)/shard_map/ppermute | solution.py:76
  253.7 7.8 %collective-permute-done.24 = bf16[2,128,896]{2,1,0:T(8,128)(2,1)S(1)} collective-permute-done((bf16[2,128,896]{2,1,0:T(8,128)(2,1)S(1)}, bf16[2,128,896]{2,1,0:T(8,128)(2,1)S(1)}, u32[]{:S(2)}, u32[]{:S(2)}) %collective-permute-start.24) | collective-permute-done | bytes 458784 | tf_op jit(solution)/shard_map/ppermute | solution.py:98
  (104 shorter events, 56.6 us)
Async XLA Ops:
  6.5 83.2 %all-gather.2.cloned.1.call-start = ((), (), s32[]{:S(2)}) async-start(), calls=%async_computation | async-start | bytes 7077888 | tf_op jit(solution)/shard_map/all_gather | solution.py:105
  140.7 22.8 %collective-permute-start.12 = (bf16[4,2,64,896]{3,2,1,0:T(8,128)(2,1)}, bf16[4,2,64,896]{3,2,1,0:T(8,128)(2,1)}, u32[]{:S(2)}, u32[]{:S(2)}) collective-permute-start(bf16[4,2,64,896]{3,2,1,0:T(8,128)(2,1)} %dynamic-slice_bitcast_fusion.1), channel_id=1, source_target_pairs={{0,64},{8,72},{16,80},{24,88},{32,96},{40,104},{48,112},{56,120},{... | collective-permute-start | bytes 2752520 | tf_op jit(solution)/shard_map/ppermute | solution.py:75
  143.0 24.7 %collective-permute-start.18 = (bf16[4,2,64,896]{3,2,1,0:T(8,128)(2,1)}, bf16[4,2,64,896]{3,2,1,0:T(8,128)(2,1)S(1)}, u32[]{:S(2)}, u32[]{:S(2)}) collective-permute-start(bf16[4,2,64,896]{3,2,1,0:T(8,128)(2,1)} %dynamic-slice_bitcast_fusion), channel_id=1, source_target_pairs={{0,192},{8,200},{16,208},{24,216},{32,224},{40,232},{48,240},{56,2... | collective-permute-start | bytes 2752520 | tf_op jit(solution)/shard_map/ppermute | solution.py:76
  149.7 22.2 %collective-permute-start = (bf16[4,2,64,896]{3,2,1,0:T(8,128)(2,1)S(1)}, bf16[4,2,64,896]{3,2,1,0:T(8,128)(2,1)S(1)}, u32[]{:S(2)}, u32[]{:S(2)}) collective-permute-start(bf16[4,2,64,896]{3,2,1,0:T(8,128)(2,1)S(1)} %dynamic-slice_bitcast_fusion.3), channel_id=1, source_target_pairs={{0,16},{8,24},{16,32},{24,40},{32,48},{40,56},{48,0},{56,8},{64,80... | collective-permute-start | bytes 2752520 | tf_op jit(solution)/shard_map/ppermute | solution.py:75
  152.7 23.2 %collective-permute-start.6 = (bf16[4,2,64,896]{3,2,1,0:T(8,128)(2,1)}, bf16[4,2,64,896]{3,2,1,0:T(8,128)(2,1)}, u32[]{:S(2)}, u32[]{:S(2)}) collective-permute-start(bf16[4,2,64,896]{3,2,1,0:T(8,128)(2,1)} %dynamic-slice_bitcast_fusion.2), channel_id=1, source_target_pairs={{0,48},{8,56},{16,0},{24,8},{32,16},{40,24},{48,32},{56,40},{64,11... | collective-permute-start | bytes 2752520 | tf_op jit(solution)/shard_map/ppermute | solution.py:76
  166.1 22.0 %collective-permute-start.13 = (bf16[4,2,64,896]{3,2,1,0:T(8,128)(2,1)}, bf16[4,2,64,896]{3,2,1,0:T(8,128)(2,1)}, u32[]{:S(2)}, u32[]{:S(2)}) collective-permute-start(bf16[4,2,64,896]{3,2,1,0:T(8,128)(2,1)} %fusion.7), channel_id=1, source_target_pairs={{0,64},{8,72},{16,80},{24,88},{32,96},{40,104},{48,112},{56,120},{... | collective-permute-start | bytes 2752520 | tf_op jit(solution)/shard_map/ppermute | solution.py:75
  170.0 23.9 %collective-permute-start.19 = (bf16[4,2,64,896]{3,2,1,0:T(8,128)(2,1)}, bf16[4,2,64,896]{3,2,1,0:T(8,128)(2,1)S(1)}, u32[]{:S(2)}, u32[]{:S(2)}) collective-permute-start(bf16[4,2,64,896]{3,2,1,0:T(8,128)(2,1)} %fusion.5), channel_id=1, source_target_pairs={{0,192},{8,200},{16,208},{24,216},{32,224},{40,232},{48,240},{56,2... | collective-permute-start | bytes 2752520 | tf_op jit(solution)/shard_map/ppermute | solution.py:76
  173.3 22.2 %collective-permute-start.1 = (bf16[4,2,64,896]{3,2,1,0:T(8,128)(2,1)S(1)}, bf16[4,2,64,896]{3,2,1,0:T(8,128)(2,1)S(1)}, u32[]{:S(2)}, u32[]{:S(2)}) collective-permute-start(bf16[4,2,64,896]{3,2,1,0:T(8,128)(2,1)S(1)} %fusion.11), channel_id=1, source_target_pairs={{0,16},{8,24},{16,32},{24,40},{32,48},{40,56},{48,0},{56,8},{64,80... | collective-permute-start | bytes 2752520 | tf_op jit(solution)/shard_map/ppermute | solution.py:75
  178.5 22.3 %collective-permute-start.7 = (bf16[4,2,64,896]{3,2,1,0:T(8,128)(2,1)}, bf16[4,2,64,896]{3,2,1,0:T(8,128)(2,1)}, u32[]{:S(2)}, u32[]{:S(2)}) collective-permute-start(bf16[4,2,64,896]{3,2,1,0:T(8,128)(2,1)} %fusion.9), channel_id=1, source_target_pairs={{0,48},{8,56},{16,0},{24,8},{32,16},{40,24},{48,32},{56,40},{64,11... | collective-permute-start | bytes 2752520 | tf_op jit(solution)/shard_map/ppermute | solution.py:76
  190.8 22.0 %collective-permute-start.14 = (bf16[4,2,64,896]{3,2,1,0:T(8,128)(2,1)}, bf16[4,2,64,896]{3,2,1,0:T(8,128)(2,1)}, u32[]{:S(2)}, u32[]{:S(2)}) collective-permute-start(bf16[4,2,64,896]{3,2,1,0:T(8,128)(2,1)} %fusion.6), channel_id=1, source_target_pairs={{0,64},{8,72},{16,80},{24,88},{32,96},{40,104},{48,112},{56,120},{... | collective-permute-start | bytes 2752520 | tf_op jit(solution)/shard_map/ppermute | solution.py:75
  195.4 22.1 %collective-permute-start.20 = (bf16[4,2,64,896]{3,2,1,0:T(8,128)(2,1)S(1)}, bf16[4,2,64,896]{3,2,1,0:T(8,128)(2,1)S(1)}, u32[]{:S(2)}, u32[]{:S(2)}) collective-permute-start(bf16[4,2,64,896]{3,2,1,0:T(8,128)(2,1)S(1)} %fusion.4), channel_id=1, source_target_pairs={{0,192},{8,200},{16,208},{24,216},{32,224},{40,232},{48,240},{56,2... | collective-permute-start | bytes 2752520 | tf_op jit(solution)/shard_map/ppermute | solution.py:76
  197.0 23.4 %collective-permute-start.2 = (bf16[4,2,64,896]{3,2,1,0:T(8,128)(2,1)S(1)}, bf16[4,2,64,896]{3,2,1,0:T(8,128)(2,1)S(1)}, u32[]{:S(2)}, u32[]{:S(2)}) collective-permute-start(bf16[4,2,64,896]{3,2,1,0:T(8,128)(2,1)S(1)} %fusion.10), channel_id=1, source_target_pairs={{0,16},{8,24},{16,32},{24,40},{32,48},{40,56},{48,0},{56,8},{64,80... | collective-permute-start | bytes 2752520 | tf_op jit(solution)/shard_map/ppermute | solution.py:75
  202.3 23.6 %collective-permute-start.8 = (bf16[4,2,64,896]{3,2,1,0:T(8,128)(2,1)S(1)}, bf16[4,2,64,896]{3,2,1,0:T(8,128)(2,1)S(1)}, u32[]{:S(2)}, u32[]{:S(2)}) collective-permute-start(bf16[4,2,64,896]{3,2,1,0:T(8,128)(2,1)S(1)} %fusion.8), channel_id=1, source_target_pairs={{0,48},{8,56},{16,0},{24,8},{32,16},{40,24},{48,32},{56,40},{64,11... | collective-permute-start | bytes 2752520 | tf_op jit(solution)/shard_map/ppermute | solution.py:76
  214.5 12.4 %collective-permute-start.15 = (bf16[2,64,896]{2,1,0:T(8,128)(2,1)S(1)}, bf16[2,64,896]{2,1,0:T(8,128)(2,1)S(1)}, u32[]{:S(2)}, u32[]{:S(2)}) collective-permute-start(bf16[2,64,896]{2,1,0:T(8,128)(2,1)S(1)} %fusion.32), channel_id=1, source_target_pairs={{0,16},{8,24},{16,32},{24,40},{32,48},{40,56},{48,0},{56,8},{64,80... | collective-permute-start | bytes 688136 | tf_op jit(solution)/shard_map/ppermute | solution.py:75
  219.0 9.3 %collective-permute-start.21 = (bf16[2,64,896]{2,1,0:T(8,128)(2,1)S(1)}, bf16[2,64,896]{2,1,0:T(8,128)(2,1)S(1)}, u32[]{:S(2)}, u32[]{:S(2)}) collective-permute-start(bf16[2,64,896]{2,1,0:T(8,128)(2,1)S(1)} %fusion.33), channel_id=1, source_target_pairs={{0,48},{8,56},{16,0},{24,8},{32,16},{40,24},{48,32},{56,40},{64,11... | collective-permute-start | bytes 688136 | tf_op jit(solution)/shard_map/ppermute | solution.py:76
  221.8 7.4 %collective-permute-start.3 = (bf16[2,64,896]{2,1,0:T(8,128)(2,1)S(1)}, bf16[2,64,896]{2,1,0:T(8,128)(2,1)S(1)}, u32[]{:S(2)}, u32[]{:S(2)}) collective-permute-start(bf16[2,64,896]{2,1,0:T(8,128)(2,1)S(1)} %fusion.30), channel_id=1, source_target_pairs={{0,64},{8,72},{16,80},{24,88},{32,96},{40,104},{48,112},{56,120},{... | collective-permute-start | bytes 688136 | tf_op jit(solution)/shard_map/ppermute | solution.py:75
  226.1 9.5 %collective-permute-start.9 = (bf16[2,64,896]{2,1,0:T(8,128)(2,1)S(1)}, bf16[2,64,896]{2,1,0:T(8,128)(2,1)S(1)}, u32[]{:S(2)}, u32[]{:S(2)}) collective-permute-start(bf16[2,64,896]{2,1,0:T(8,128)(2,1)S(1)} %fusion.31), channel_id=1, source_target_pairs={{0,192},{8,200},{16,208},{24,216},{32,224},{40,232},{48,240},{56,2... | collective-permute-start | bytes 688136 | tf_op jit(solution)/shard_map/ppermute | solution.py:76
  227.0 8.8 %collective-permute-start.16 = (bf16[2,64,896]{2,1,0:T(8,128)(2,1)S(1)}, bf16[2,64,896]{2,1,0:T(8,128)(2,1)S(1)}, u32[]{:S(2)}, u32[]{:S(2)}) collective-permute-start(bf16[2,64,896]{2,1,0:T(8,128)(2,1)S(1)} %fusion.25), channel_id=1, source_target_pairs={{0,16},{8,24},{16,32},{24,40},{32,48},{40,56},{48,0},{56,8},{64,80... | collective-permute-start | bytes 688136 | tf_op jit(solution)/shard_map/ppermute | solution.py:75
  228.3 7.5 %collective-permute-start.22 = (bf16[2,64,896]{2,1,0:T(8,128)(2,1)S(1)}, bf16[2,64,896]{2,1,0:T(8,128)(2,1)S(1)}, u32[]{:S(2)}, u32[]{:S(2)}) collective-permute-start(bf16[2,64,896]{2,1,0:T(8,128)(2,1)S(1)} %fusion.23), channel_id=1, source_target_pairs={{0,48},{8,56},{16,0},{24,8},{32,16},{40,24},{48,32},{56,40},{64,11... | collective-permute-start | bytes 688136 | tf_op jit(solution)/shard_map/ppermute | solution.py:76
  229.2 8.8 %collective-permute-start.4 = (bf16[2,64,896]{2,1,0:T(8,128)(2,1)S(1)}, bf16[2,64,896]{2,1,0:T(8,128)(2,1)S(1)}, u32[]{:S(2)}, u32[]{:S(2)}) collective-permute-start(bf16[2,64,896]{2,1,0:T(8,128)(2,1)S(1)} %fusion.29), channel_id=1, source_target_pairs={{0,64},{8,72},{16,80},{24,88},{32,96},{40,104},{48,112},{56,120},{... | collective-permute-start | bytes 688136 | tf_op jit(solution)/shard_map/ppermute | solution.py:75
  235.6 9.0 %collective-permute-start.10 = (bf16[2,64,896]{2,1,0:T(8,128)(2,1)S(1)}, bf16[2,64,896]{2,1,0:T(8,128)(2,1)S(1)}, u32[]{:S(2)}, u32[]{:S(2)}) collective-permute-start(bf16[2,64,896]{2,1,0:T(8,128)(2,1)S(1)} %fusion.27), channel_id=1, source_target_pairs={{0,192},{8,200},{16,208},{24,216},{32,224},{40,232},{48,240},{56,2... | collective-permute-start | bytes 688136 | tf_op jit(solution)/shard_map/ppermute | solution.py:76
  235.8 9.0 %collective-permute-start.17 = (bf16[2,64,896]{2,1,0:T(8,128)(2,1)S(1)}, bf16[2,64,896]{2,1,0:T(8,128)(2,1)S(1)}, u32[]{:S(2)}, u32[]{:S(2)}) collective-permute-start(bf16[2,64,896]{2,1,0:T(8,128)(2,1)S(1)} %fusion.24), channel_id=1, source_target_pairs={{0,16},{8,24},{16,32},{24,40},{32,48},{40,56},{48,0},{56,8},{64,80... | collective-permute-start | bytes 688136 | tf_op jit(solution)/shard_map/ppermute | solution.py:75
  235.9 8.9 %collective-permute-start.23 = (bf16[2,64,896]{2,1,0:T(8,128)(2,1)S(1)}, bf16[2,64,896]{2,1,0:T(8,128)(2,1)S(1)}, u32[]{:S(2)}, u32[]{:S(2)}) collective-permute-start(bf16[2,64,896]{2,1,0:T(8,128)(2,1)S(1)} %fusion.22), channel_id=1, source_target_pairs={{0,48},{8,56},{16,0},{24,8},{32,16},{40,24},{48,32},{56,40},{64,11... | collective-permute-start | bytes 688136 | tf_op jit(solution)/shard_map/ppermute | solution.py:76
  253.0 8.5 %collective-permute-start.24 = (bf16[2,128,896]{2,1,0:T(8,128)(2,1)S(1)}, bf16[2,128,896]{2,1,0:T(8,128)(2,1)S(1)}, u32[]{:S(2)}, u32[]{:S(2)}) collective-permute-start(bf16[2,128,896]{2,1,0:T(8,128)(2,1)S(1)} %fusion.21), channel_id=1, source_target_pairs={{0,8},{8,0},{16,24},{24,16},{32,40},{40,32},{48,56},{56,48},{64,72... | collective-permute-start | bytes 1376264 | tf_op jit(solution)/shard_map/ppermute | solution.py:98
  (13 other events, 221.9 us)
Sparse Core Ops, SparseCore 0:
  16.8 72.8 all-gather.1

commit v3 on v1

--- a/solution.py
+++ b/solution.py
@@ -1,12 +1,13 @@
 import jax
 import jax.numpy as jnp
 from jax import lax
+from jax.experimental import pallas as pl
+from jax.experimental.pallas import tpu as pltpu
 from jax.sharding import PartitionSpec as P
 
 BLOCK = 128
 Y_LEVELS = 8
 W_LEVELS = 7
-COL_CHUNKS = 2
 
 
 epsilon = 1e-06
@@ -38,27 +39,143 @@
     return values.reshape(feat_rows, unit_cols).astype(jnp.bfloat16)
 
 
+MESH = pl.DeviceIdType.MESH
+RING = 4
+
+
+def dp_at(y, x, z):
+    return y * 8 + x * 2 + z
+
+
+def rs_kernel(terms_ref, out_ref, recv1, send1, res1, recv2, send2, res2, recvz, sendz,
+              ss1, sr1, ss2, sr2, ssz, srz):
+    dp = lax.axis_index("dp")
+    y, x, z = dp // 8, (dp // 2) % 4, dp % 2
+    rows, cols = terms_ref.shape[3], terms_ref.shape[4]
+    half, width = rows // 2, cols // 2
+    x_up, x_dn = dp_at(y, (x + 1) % RING, z), dp_at(y, (x + RING - 1) % RING, z)
+    y_up, y_dn = dp_at((y + 1) % RING, x, z), dp_at((y + RING - 1) % RING, x, z)
+    z_other = dp_at(y, x, 1 - z)
+
+    barrier = pltpu.get_barrier_semaphore()
+    for peer in (x_up, x_dn, y_up, y_dn, z_other):
+        pl.semaphore_signal(barrier, inc=1, device_id={"dp": peer}, device_id_type=MESH)
+    pl.semaphore_wait(barrier, 5)
+
+    first = [
+        (x, 1, x_up, 0, 0, True),
+        (x, -1, x_dn, half, 0, True),
+        (y, 1, y_up, 0, width, False),
+        (y, -1, y_dn, half, width, False),
+    ]
+
+    def local1(k, index):
+        _, _, _, r0, c0, over_x = first[k]
+        if over_x:
+            return terms_ref.at[:, index, :, pl.ds(r0, half), pl.ds(c0, width)]
+        return terms_ref.at[index, :, :, pl.ds(r0, half), pl.ds(c0, width)]
+
+    def sent_index(pos, direction, step):
+        return (pos - direction * (step + 1) + 2 * RING) % RING
+
+    def ring_copy(src, dst, send_sem, recv_sem, target):
+        return pltpu.make_async_remote_copy(
+            src_ref=src, dst_ref=dst, send_sem=send_sem, recv_sem=recv_sem,
+            device_id={"dp": target}, device_id_type=MESH)
+
+    pending = []
+    copies = [None] * 4
+    for k, (pos, direction, target, _, _, _) in enumerate(first):
+        copies[k] = ring_copy(local1(k, sent_index(pos, direction, 0)), recv1.at[k, 0],
+                              ss1.at[k, 0], sr1.at[k, 0], target)
+        copies[k].start()
+        pending.append(copies[k])
+    for step in range(1, RING - 1):
+        for k, (pos, direction, target, _, _, _) in enumerate(first):
+            copies[k].wait_recv()
+            index = sent_index(pos, direction, step)
+            acc = recv1[k, step - 1].astype(jnp.float32) + local1(k, index)[...].astype(jnp.float32)
+            send1[k, step - 1] = acc.astype(jnp.bfloat16)
+            copies[k] = ring_copy(send1.at[k, step - 1], recv1.at[k, step],
+                                  ss1.at[k, step], sr1.at[k, step], target)
+            copies[k].start()
+            pending.append(copies[k])
+    for k, (pos, _, _, _, _, _) in enumerate(first):
+        copies[k].wait_recv()
+        res1[k] = recv1[k, RING - 2].astype(jnp.float32) + local1(k, pos)[...].astype(jnp.float32)
+
+    second = [(y, 1, y_up), (y, -1, y_dn), (x, 1, x_up), (x, -1, x_dn)]
+    for k, (pos, direction, target) in enumerate(second):
+        send2[k, 0] = res1[k, sent_index(pos, direction, 0)].astype(jnp.bfloat16)
+        copies[k] = ring_copy(send2.at[k, 0], recv2.at[k, 0], ss2.at[k, 0], sr2.at[k, 0], target)
+        copies[k].start()
+        pending.append(copies[k])
+    for step in range(1, RING - 1):
+        for k, (pos, direction, target) in enumerate(second):
+            copies[k].wait_recv()
+            index = sent_index(pos, direction, step)
+            acc = recv2[k, step - 1].astype(jnp.float32) + res1[k, index]
+            send2[k, step] = acc.astype(jnp.bfloat16)
+            copies[k] = ring_copy(send2.at[k, step], recv2.at[k, step],
+                                  ss2.at[k, step], sr2.at[k, step], target)
+            copies[k].start()
+            pending.append(copies[k])
+    for k, (pos, _, _) in enumerate(second):
+        copies[k].wait_recv()
+        res2[k] = recv2[k, RING - 2].astype(jnp.float32) + res1[k, pos]
+
+    for k in range(4):
+        sendz[k] = res2[k, 1 - z].astype(jnp.bfloat16)
+    swap = ring_copy(sendz, recvz, ssz, srz, z_other)
+    swap.start()
+    swap.wait_recv()
+    for k, (r0, c0) in enumerate([(0, 0), (half, 0), (0, width), (half, width)]):
+        out_ref[pl.ds(r0, half), pl.ds(c0, width)] = res2[k, z] + recvz[k].astype(jnp.float32)
+    for copy in pending:
+        copy.wait_send()
+    swap.wait_send()
+
+
+def reduce_scatter_terms(terms):
+    feat_rows, cols = terms.shape
+    rows = feat_rows // 32
+    half, width = rows // 2, cols // 2
+    blocks = terms.reshape(RING, RING, 2, rows, cols)
+    chunk = (RING, 2, half, width)
+    return pl.pallas_call(
+        rs_kernel,
+        out_shape=jax.ShapeDtypeStruct((rows, cols), jnp.float32),
+        in_specs=[pl.BlockSpec(memory_space=pltpu.VMEM)],
+        out_specs=pl.BlockSpec(memory_space=pltpu.VMEM),
+        scratch_shapes=[
+            pltpu.VMEM((4, RING - 1) + chunk, jnp.bfloat16),
+            pltpu.VMEM((4, RING - 2) + chunk, jnp.bfloat16),
+            pltpu.VMEM((4,) + chunk, jnp.float32),
+            pltpu.VMEM((4, RING - 1, 2, half, width), jnp.bfloat16),
+            pltpu.VMEM((4, RING - 1, 2, half, width), jnp.bfloat16),
+            pltpu.VMEM((4, 2, half, width), jnp.float32),
+            pltpu.VMEM((4, half, width), jnp.bfloat16),
+            pltpu.VMEM((4, half, width), jnp.bfloat16),
+            pltpu.SemaphoreType.DMA((4, RING - 1)),
+            pltpu.SemaphoreType.DMA((4, RING - 1)),
+            pltpu.SemaphoreType.DMA((4, RING - 1)),
+            pltpu.SemaphoreType.DMA((4, RING - 1)),
+            pltpu.SemaphoreType.DMA(()),
+            pltpu.SemaphoreType.DMA(()),
+        ],
+        compiler_params=pltpu.CompilerParams(
+            collective_id=0, has_side_effects=True, vmem_limit_bytes=62 * 1024 * 1024),
+    )(blocks)
+
+
 def per_device(grad_out, activations, grad_dither, hidden_dither, feature_dither):
-    feat_width = grad_out.shape[1]
     y_local = code_rows(grad_out, grad_dither)
     y_hat = lax.all_gather(y_local, "tensor", axis=0, tiled=True)
-    unit_count = activations.shape[1]
-    owners = lax.axis_size("dp")
-    own_rows = feat_width // owners
-    hidden_noise = hidden_dither[0]
-    feature_noise = feature_dither[0]
-    width = unit_count // COL_CHUNKS
-    sums = []
-    for chunk in range(COL_CHUNKS):
-        cols = slice(chunk * width, (chunk + 1) * width)
-        partial_value = lax.dot_general(
-            y_hat, activations[:, cols], (((0,), (0,)), ((), ())), preferred_element_type=jnp.float32
-        )
-        terms = group_terms(partial_value, feature_noise, hidden_noise[cols])
-        arrived = lax.all_to_all(terms, "dp", split_axis=0, concat_axis=0, tiled=True)
-        held = lax.optimization_barrier(arrived).astype(jnp.float32)
-        sums.append(jnp.sum(held.reshape(owners, own_rows, width), axis=0))
-    return jnp.concatenate(sums, axis=1)
+    partial_value = lax.dot_general(
+        y_hat, activations, (((0,), (0,)), ((), ())), preferred_element_type=jnp.float32
+    )
+    terms = group_terms(partial_value, feature_dither[0], hidden_dither[0])
+    return reduce_scatter_terms(terms)
 
 
 def solution(mesh):

time: 384 us -> 240 us (0.62); the launches traced: 378 us -> 239 us
  waiting for transfers between devices: 279 us -> 72.1 us
  Pallas kernels: 0 us -> 105 us
  starting transfers between devices: 27.1 us -> 0.01 us
  other arithmetic: 37.6 us -> 26.3 us
    all_to_all x2 -> x0, waiting for transfers between devices: 207 us -> none  [per_device(): lax.all_to_all(terms, 'dp', split_axis=0, concat_axis=0, tiled=True)]
    pallas_call x0 -> x1, Pallas kernels: none -> 105 us  [reduce_scatter_terms(): pl.pallas_call(rs_kernel, out_shape=jax.ShapeDtypeStruct((rows, cols), jn...]
    all_to_all x2 -> x0, starting transfers between devices: 27.1 us -> none  [per_device(): lax.all_to_all(terms, 'dp', split_axis=0, concat_axis=0, tiled=True)]
    reduce_sum x2 -> x0, other arithmetic: 8.3 us -> none  [per_device(): sums.append(jnp.sum(held.reshape(owners, own_rows, width), axis=0))]
    convert_element_type x2 -> x1, other arithmetic: 12.1 us -> 7.35 us  [group_terms(): return values.reshape(feat_rows, unit_cols).astype(jnp.bfloat16)]
    dot_general x2 -> x1, matrix products: 20.3 us -> 19.7 us  [per_device(): lax.dot_general(y_hat, activations, (((0,), (0,)), ((), ())), preferred_e...]
  transfers between devices with their start and end apart: 3 -> 1, of which waited for: 3 -> 1; matrix products, arithmetic and copies ran while one was open for 3% -> 0% of each run, Pallas kernels for 0% -> 0%
where the time goes in v3:
time: 240 us; the launch traced here: 239 us
  Pallas kernels  105 us (44%)
  waiting for transfers between devices  72.1 us (30%)
  other arithmetic  26.3 us (11%)
  matrix products  19.7 us (8%)
  between operations  13.5 us (6%)
  local copies, waits for them, and re-layouts  2.92 us (1%)
    pallas_call x1, Pallas kernels, reduce_scatter_terms(): pl.pallas_call(rs_kernel, out_shape=jax.ShapeDtypeStruct((rows, cols), jn...  105 us
    all_gather x1, waiting for transfers between devices, per_device(): y_hat = lax.all_gather(y_local, 'tensor', axis=0, tiled=True)  72.1 us
    dot_general x1, matrix products, per_device(): lax.dot_general(y_hat, activations, (((0,), (0,)), ((), ())), preferred_e...  19.7 us
    convert_element_type x1, other arithmetic, group_terms(): (scaled + hidden_part[None, :] + feature_part[:, None]).astype(jnp.bfloat16)  12.6 us
    convert_element_type x1, other arithmetic, group_terms(): return values.reshape(feat_rows, unit_cols).astype(jnp.bfloat16)  7.35 us
  transfers between devices with their start and end apart: 1, of which 1 were waited for; matrix products, arithmetic and copies ran while one was open for 0% of the time, Pallas kernels for 0%

profile of v3, /device:TPU:32, one launch (start us, length us, event | category | flops | bytes accessed | tf_op | source)
XLA Modules:
  0.0 239.4 jit_solution(12656262500705674720)
XLA Ops:
  6.5 0.0 copy-start
  6.5 0.0 all-gather.2.cloned.1.call-start
  6.5 1.4 fusion.4
  7.9 0.3 copy.6
  8.2 0.0 copy-start.2
  8.2 0.5 reduce_max.18
  8.7 0.5 div.36
  9.2 0.0 copy-start.3
  9.2 0.0 copy-done
  9.2 2.7 %fusion.6 = bf16[96,4096]{1,0:T(8,128)(2,1)S(1)} fusion(f32[96,4096]{1,0:T(8,128)} %param.7, bf16[96,4096]{1,0:T(8,128)(2,1)S(1)} %copy-done, f32[12,8,32,128]{3,2,1,0:T(8,128)S(1)} %bitcast.27), kind=kLoop, calls=%fused_computation.11 | loop fusion | flops 1572864 | bytes 4718592 | tf_op jit(solution)/shard_map/convert_element_type | solution.py:23
  11.9 1.8 fusion.7
  13.7 0.0 all-gather.2.cloned.1.call-update
  13.7 0.0 copy-done.2
  13.7 0.0 copy-start.1
  13.7 72.1 %all-gather.2.cloned.1.call-done = bf16[768,4096]{1,0:T(8,128)(2,1)} async-done(((bf16[96,4096]{1,0:T(8,128)(2,1)}), bf16[768,4096]{1,0:T(8,128)(2,1)}) %all-gather.2.cloned.1.call-update) | async-done | bytes 6291472 | tf_op jit(solution)/shard_map/all_gather | solution.py:173
  85.8 0.0 copy-done.3
  85.8 19.7 %bitcast_reduce_fusion = (f32[32,1792]{1,0:T(8,128)S(1)}, f32[4096,1792]{1,0:T(8,128)}) fusion(bf16[768,4096]{1,0:T(8,128)(2,1)} %all-gather.2.cloned.1.call-done, bf16[768,1792]{1,0:T(8,128)(2,1)S(1)} %copy-done.3), kind=kOutput, calls=%fused_computation.6 | convolution fusion | flops 11288911872 | bytes 38633472 | tf_op jit(solution)/shard_map/dot_general | solution.py:174
  105.6 0.0 copy-done.1
  105.6 12.6 %fusion.2 = bf16[4096,1792]{1,0:T(8,128)(2,1)S(1)} fusion(f32[4096,1792]{1,0:T(8,128)} %get-tuple-element.6, f32[4096]{0:T(1024)S(1)} %bitcast.30, f32[1792]{0:T(1024)S(1)} %reduce, f32[32,1792]{1,0:T(8,128)S(1)} %fusion.8), kind=kLoop, calls=%fused_computation.4 | loop fusion | flops 29360128 | bytes 44293120 | tf_op jit(solution)/shard_map/convert_element_type | solution.py:36
  118.2 7.4 %fusion.3 = bf16[4096,1792]{1,0:T(8,128)(2,1)} fusion(bf16[4096,1792]{1,0:T(8,128)(2,1)S(1)} %fusion.2, f32[32,1792]{1,0:T(8,128)S(1)} %fusion.8), kind=kLoop, calls=%fused_computation.5 | loop fusion | flops 22020096 | bytes 29589504 | tf_op jit(solution)/shard_map/convert_element_type | solution.py:39
  125.6 104.8 %shard_map.55 = f32[128,1792]{1,0:T(8,128)} custom-call(bf16[4,4,2,128,1792]{4,3,2,1,0:T(8,128)(2,1)} %bitcast.26), custom_call_target="tpu_custom_call" | custom-call | tf_op jit(solution)/shard_map/pallas_call | solution.py:145
  230.4 2.2 copy.11
  (3 shorter events, 0.1 us)
Async XLA Ops:
  6.5 2.6 %copy-start = (bf16[96,4096]{1,0:T(8,128)(2,1)S(1)}, bf16[96,4096]{1,0:T(8,128)(2,1)}, u32[]{:S(2)}) copy-start(bf16[96,4096]{1,0:T(8,128)(2,1)} %param.5) | copy-start | bytes 2359300
  6.5 79.3 %all-gather.2.cloned.1.call-start = ((), (), s32[]{:S(2)}) async-start(), calls=%async_computation | async-start | bytes 7077888 | tf_op jit(solution)/shard_map/all_gather | solution.py:173
  8.2 5.5 %copy-start.2 = (f32[1,1792]{1,0:T(1,128)S(1)}, f32[1,1792]{1,0:T(1,128)}, u32[]{:S(2)}) copy-start(f32[1,1792]{1,0:T(1,128)} %param.8) | copy-start | bytes 21508
  9.2 76.7 %copy-start.3 = (bf16[768,1792]{1,0:T(8,128)(2,1)S(1)}, bf16[768,1792]{1,0:T(8,128)(2,1)}, u32[]{:S(2)}) copy-start(bf16[768,1792]{1,0:T(8,128)(2,1)} %param.6) | copy-start | bytes 8257540
  13.7 91.9 %copy-start.1 = (f32[1,4096]{1,0:T(1,128)S(1)}, f32[1,4096]{1,0:T(1,128)}, u32[]{:S(2)}) copy-start(f32[1,4096]{1,0:T(1,128)} %param.9) | copy-start | bytes 49156
Sparse Core Ops, SparseCore 0:
  13.8 72.0 all-gather.1

commit v4 on v3

--- a/solution.py
+++ b/solution.py
@@ -168,9 +168,71 @@
     )(blocks)
 
 
+TENSOR_RING = (0, 1, 3, 2, 4, 5, 7, 6)
+
+
+def ring_member(position):
+    pair, within = position // 2, position % 2
+    return pair * 2 + (within + pair) % 2
+
+
+def gather_kernel(local_ref, out_ref, send_sem, recv_sem):
+    n = len(TENSOR_RING)
+    me = lax.axis_index("tensor")
+    pair = me // 2
+    pos = pair * 2 + (me % 2 + pair) % 2
+    right = ring_member((pos + 1) % n)
+    left = ring_member((pos + n - 1) % n)
+    rows, cols = local_ref.shape
+    width = cols // 2
+
+    barrier = pltpu.get_barrier_semaphore()
+    for peer in (left, right):
+        pl.semaphore_signal(barrier, inc=1, device_id={"tensor": peer}, device_id_type=MESH)
+    pl.semaphore_wait(barrier, 2)
+
+    out_ref[pl.ds(pl.multiple_of(me * rows, rows), rows), :] = local_ref[...]
+    streams = [(right, 1, 0), (left, -1, width)]
+    pending = []
+    copies = [None, None]
+    for step in range(n - 1):
+        for d, (target, direction, c0) in enumerate(streams):
+            if step == 0:
+                src = local_ref.at[:, pl.ds(c0, width)]
+            else:
+                copies[d].wait_recv()
+                owner = ring_member((pos - direction * step + 2 * n) % n)
+                src = out_ref.at[pl.ds(pl.multiple_of(owner * rows, rows), rows), pl.ds(c0, width)]
+            owner = ring_member((pos - direction * step + 2 * n) % n)
+            copies[d] = pltpu.make_async_remote_copy(
+                src_ref=src,
+                dst_ref=out_ref.at[pl.ds(pl.multiple_of(owner * rows, rows), rows), pl.ds(c0, width)],
+                send_sem=send_sem.at[d, step], recv_sem=recv_sem.at[d, step],
+                device_id={"tensor": target}, device_id_type=MESH)
+            copies[d].start()
+            pending.append(copies[d])
+    for d in range(2):
+        copies[d].wait_recv()
+    for copy in pending:
+        copy.wait_send()
+
+
+def gather_rows(local):
+    rows, cols = local.shape
+    n = len(TENSOR_RING)
+    return pl.pallas_call(
+        gather_kernel,
+        out_shape=jax.ShapeDtypeStruct((n * rows, cols), local.dtype),
+        in_specs=[pl.BlockSpec(memory_space=pltpu.VMEM)],
+        out_specs=pl.BlockSpec(memory_space=pltpu.VMEM),
+        scratch_shapes=[pltpu.SemaphoreType.DMA((2, n - 1)), pltpu.SemaphoreType.DMA((2, n - 1))],
+        compiler_params=pltpu.CompilerParams(collective_id=1, has_side_effects=True),
+    )(local)
+
+
 def per_device(grad_out, activations, grad_dither, hidden_dither, feature_dither):
     y_local = code_rows(grad_out, grad_dither)
-    y_hat = lax.all_gather(y_local, "tensor", axis=0, tiled=True)
+    y_hat = gather_rows(y_local)
     partial_value = lax.dot_general(
         y_hat, activations, (((0,), (0,)), ((), ())), preferred_element_type=jnp.float32
     )

time: 240 us -> 229 us (0.954)
  Pallas kernels: 105 us -> 179 us
  waiting for transfers between devices: 72.1 us -> 0 us
  between operations: 13.5 us -> 0.08 us
    pallas_call x0 -> x1, Pallas kernels: none -> 73.3 us  [gather_rows(): pl.pallas_call(gather_kernel, out_shape=jax.ShapeDtypeStruct((n * rows, c...]
    all_gather x1 -> x0, waiting for transfers between devices: 72.1 us -> none  [per_device(): y_hat = lax.all_gather(y_local, 'tensor', axis=0, tiled=True)]
  transfers between devices with their start and end apart: 1 -> 0, of which waited for: 1 -> 0; matrix products, arithmetic and copies ran while one was open for 0% -> 0% of each run, Pallas kernels for 0% -> 0%
where the time goes in v4:
time: 229 us
  Pallas kernels  179 us (78%)
  other arithmetic  26.9 us (12%)
  matrix products  20.4 us (9%)
  local copies, waits for them, and re-layouts  2.91 us (1%)
    pallas_call x1, Pallas kernels, reduce_scatter_terms(): pl.pallas_call(rs_kernel, out_shape=jax.ShapeDtypeStruct((rows, cols), jn...  105 us
    pallas_call x1, Pallas kernels, gather_rows(): pl.pallas_call(gather_kernel, out_shape=jax.ShapeDtypeStruct((n * rows, c...  73.3 us
    dot_general x1, matrix products, per_device(): lax.dot_general(y_hat, activations, (((0,), (0,)), ((), ())), preferred_e...  20.4 us
    convert_element_type x1, other arithmetic, group_terms(): (scaled + hidden_part[None, :] + feature_part[:, None]).astype(jnp.bfloat16)  12.6 us
    convert_element_type x1, other arithmetic, group_terms(): return values.reshape(feat_rows, unit_cols).astype(jnp.bfloat16)  7.35 us

profile of v4, /device:TPU:32, one launch (start us, length us, event | category | flops | bytes accessed | tf_op | source)
XLA Modules:
  0.0 228.9 jit_solution(4633297894455081651)
XLA Ops:
  0.0 0.0 copy-start
  0.0 0.8 reduce
  0.8 1.3 fusion.4
  2.1 0.3 copy.6
  2.4 0.5 reduce_max.18
  2.9 0.5 div.36
  3.3 0.0 copy-done
  3.4 2.5 %fusion.6 = bf16[96,4096]{1,0:T(8,128)(2,1)S(1)} fusion(f32[96,4096]{1,0:T(8,128)} %param.7, bf16[96,4096]{1,0:T(8,128)(2,1)S(1)} %copy-done, f32[12,8,32,128]{3,2,1,0:T(8,128)S(1)} %bitcast.27), kind=kLoop, calls=%fused_computation.11 | loop fusion | flops 1572864 | bytes 4718592 | tf_op jit(solution)/shard_map/convert_element_type | solution.py:23
  5.9 1.8 fusion.7.local_ref
  7.7 73.3 %shard_map.55 = bf16[768,4096]{1,0:T(8,128)(2,1)} custom-call(bf16[96,4096]{1,0:T(8,128)(2,1)} %fusion.7.local_ref), custom_call_target="tpu_custom_call" | custom-call | tf_op jit(solution)/shard_map/pallas_call | solution.py:223
  81.0 0.0 copy-start.1
  81.0 20.4 %bitcast_reduce_fusion = (f32[32,1792]{1,0:T(8,128)S(1)}, f32[4096,1792]{1,0:T(8,128)}) fusion(bf16[768,4096]{1,0:T(8,128)(2,1)} %shard_map.55, bf16[768,1792]{1,0:T(8,128)(2,1)} %param.6), kind=kOutput, calls=%fused_computation.6 | convolution fusion | flops 11288911872 | bytes 38633472 | tf_op jit(solution)/shard_map/dot_general | solution.py:236
  101.5 0.0 copy-done.1
  101.5 12.6 %fusion.2 = bf16[4096,1792]{1,0:T(8,128)(2,1)S(1)} fusion(f32[4096,1792]{1,0:T(8,128)} %get-tuple-element.6, f32[4096]{0:T(1024)S(1)} %bitcast.30, f32[1792]{0:T(1024)S(1)} %reduce, f32[32,1792]{1,0:T(8,128)S(1)} %fusion.8), kind=kLoop, calls=%fused_computation.4 | loop fusion | flops 29360128 | bytes 44293120 | tf_op jit(solution)/shard_map/convert_element_type | solution.py:36
  114.1 7.4 %fusion.3 = bf16[4096,1792]{1,0:T(8,128)(2,1)} fusion(bf16[4096,1792]{1,0:T(8,128)(2,1)S(1)} %fusion.2, f32[32,1792]{1,0:T(8,128)S(1)} %fusion.8), kind=kLoop, calls=%fused_computation.5 | loop fusion | flops 22020096 | bytes 29589504 | tf_op jit(solution)/shard_map/convert_element_type | solution.py:39
  121.4 105.3 %shard_map.56 = f32[128,1792]{1,0:T(8,128)} custom-call(bf16[4,4,2,128,1792]{4,3,2,1,0:T(8,128)(2,1)} %bitcast.26), custom_call_target="tpu_custom_call" | custom-call | tf_op jit(solution)/shard_map/pallas_call | solution.py:145
  226.7 2.2 copy.11
  (2 shorter events, 0.0 us)
Async XLA Ops:
  0.0 3.3 %copy-start = (bf16[96,4096]{1,0:T(8,128)(2,1)S(1)}, bf16[96,4096]{1,0:T(8,128)(2,1)}, u32[]{:S(2)}) copy-start(bf16[96,4096]{1,0:T(8,128)(2,1)} %param.5) | copy-start | bytes 2359300
  81.0 20.5 %copy-start.1 = (f32[1,4096]{1,0:T(1,128)S(1)}, f32[1,4096]{1,0:T(1,128)}, u32[]{:S(2)}) copy-start(f32[1,4096]{1,0:T(1,128)} %param.9) | copy-start | bytes 49156

commit v5 on v4

--- a/solution.py
+++ b/solution.py
@@ -11,6 +11,10 @@
 
 
 epsilon = 1e-06
+
+
+def as_bf16_value(value):
+    return lax.reduce_precision(value, exponent_bits=8, mantissa_bits=7)
 
 
 def code_rows(grad_out, grad_dither):
@@ -20,8 +24,7 @@
     magnitude = jnp.max(jnp.abs(grad_float), axis=2)
     y_scale = ((magnitude + epsilon) / Y_LEVELS).astype(jnp.bfloat16)
     scaled = grad_float / y_scale.astype(jnp.float32)[:, :, None]
-    y_code = (scaled.reshape(row_count, feat_width) + grad_dither).astype(jnp.bfloat16)
-    held = lax.optimization_barrier(y_code).astype(jnp.float32)
+    held = as_bf16_value(scaled.reshape(row_count, feat_width) + grad_dither)
     values = held.reshape(row_count, block_count, BLOCK) * y_scale.astype(jnp.float32)[:, :, None]
     return values.reshape(row_count, feat_width).astype(jnp.bfloat16)
 
@@ -33,8 +36,7 @@
     magnitude = jnp.max(jnp.abs(blocks), axis=1)
     block_scale = ((magnitude + epsilon) / W_LEVELS).astype(jnp.bfloat16)
     scaled = (blocks / block_scale.astype(jnp.float32)[:, None, :]).reshape(feat_rows, unit_cols)
-    code_block = (scaled + hidden_part[None, :] + feature_part[:, None]).astype(jnp.bfloat16)
-    held = lax.optimization_barrier(code_block).astype(jnp.float32)
+    held = as_bf16_value(scaled + hidden_part[None, :] + feature_part[:, None])
     values = held.reshape(block_count, BLOCK, unit_cols) * block_scale.astype(jnp.float32)[:, None, :]
     return values.reshape(feat_rows, unit_cols).astype(jnp.bfloat16)
 

time: 229 us -> 227 us (level)
  other arithmetic: 26.9 us -> 24.2 us
    convert_element_type x2 -> x0, other arithmetic: 15.1 us -> none  [the longest x1 12.6 us: group_terms(): (scaled + hidden_part[None, :] + feature_part[:, None]).astype(jnp.bfloat16)]
    convert_element_type x1, other arithmetic: 7.35 us -> 18.1 us  [group_terms(): return values.reshape(feat_rows, unit_cols).astype(jnp.bfloat16)]
where the time goes in v5:
time: 227 us; the launch traced here: 226 us
  Pallas kernels  179 us (79%)
  other arithmetic  24.2 us (11%)
  matrix products  20.4 us (9%)
  local copies, waits for them, and re-layouts  2.91 us (1%)
    pallas_call x1, Pallas kernels, reduce_scatter_terms(): pl.pallas_call(rs_kernel, out_shape=jax.ShapeDtypeStruct((rows, cols), jn...  105 us
    pallas_call x1, Pallas kernels, gather_rows(): pl.pallas_call(gather_kernel, out_shape=jax.ShapeDtypeStruct((n * rows, c...  73.3 us
    dot_general x1, matrix products, per_device(): lax.dot_general(y_hat, activations, (((0,), (0,)), ((), ())), preferred_e...  20.4 us
    convert_element_type x1, other arithmetic, group_terms(): return values.reshape(feat_rows, unit_cols).astype(jnp.bfloat16)  18.1 us

profile of v5, /device:TPU:32, one launch (start us, length us, event | category | flops | bytes accessed | tf_op | source)
XLA Modules:
  0.0 226.1 jit_solution(9305761371016478446)
XLA Ops:
  0.0 0.0 copy-start
  0.0 0.8 reduce
  0.8 1.3 fusion.4
  2.1 0.3 copy.6
  2.4 0.5 reduce_max.18
  2.9 0.5 div.36
  3.3 0.0 copy-done
  3.4 3.5 %fusion.8.local_ref = bf16[96,4096]{1,0:T(8,128)(2,1)} fusion(f32[96,4096]{1,0:T(8,128)} %param.7, f32[12,8,32,128]{3,2,1,0:T(8,128)S(1)} %bitcast.29, bf16[96,4096]{1,0:T(8,128)(2,1)S(1)} %copy-done), kind=kLoop, calls=%fused_computation.13 | loop fusion | flops 2359296 | bytes 4718592 | tf_op jit(solution)/shard_map/convert_element_type | solution.py:29
  6.9 73.3 %shard_map.55 = bf16[768,4096]{1,0:T(8,128)(2,1)} custom-call(bf16[96,4096]{1,0:T(8,128)(2,1)} %fusion.8.local_ref), custom_call_target="tpu_custom_call" | custom-call | tf_op jit(solution)/shard_map/pallas_call | solution.py:225
  80.2 0.0 copy-start.1
  80.2 20.4 %bitcast_reduce_fusion = (f32[32,1792]{1,0:T(8,128)S(1)}, f32[4096,1792]{1,0:T(8,128)}) fusion(bf16[768,4096]{1,0:T(8,128)(2,1)} %shard_map.55, bf16[768,1792]{1,0:T(8,128)(2,1)} %param.6), kind=kOutput, calls=%fused_computation.5 | convolution fusion | flops 11288911872 | bytes 38633472 | tf_op jit(solution)/shard_map/dot_general | solution.py:238
  100.7 0.0 copy-done.1
  100.7 18.1 %fusion.3 = bf16[4096,1792]{1,0:T(8,128)(2,1)} fusion(f32[4096,1792]{1,0:T(8,128)} %get-tuple-element.6, f32[4096]{0:T(1024)S(1)} %bitcast.30, f32[1792]{0:T(1024)S(1)} %reduce, f32[32,1792]{1,0:T(8,128)S(1)} %fusion.9), kind=kLoop, calls=%fused_computation.6 | loop fusion | flops 44040192 | bytes 44293120 | tf_op jit(solution)/shard_map/convert_element_type | solution.py:41
  118.7 105.3 %shard_map.56 = f32[128,1792]{1,0:T(8,128)} custom-call(bf16[4,4,2,128,1792]{4,3,2,1,0:T(8,128)(2,1)} %bitcast.27), custom_call_target="tpu_custom_call" | custom-call | tf_op jit(solution)/shard_map/pallas_call | solution.py:147
  224.0 2.2 copy.12
  (2 shorter events, 0.0 us)
Async XLA Ops:
  0.0 3.3 %copy-start = (bf16[96,4096]{1,0:T(8,128)(2,1)S(1)}, bf16[96,4096]{1,0:T(8,128)(2,1)}, u32[]{:S(2)}) copy-start(bf16[96,4096]{1,0:T(8,128)(2,1)} %param.5) | copy-start | bytes 2359300
  80.2 20.4 %copy-start.1 = (f32[1,4096]{1,0:T(1,128)S(1)}, f32[1,4096]{1,0:T(1,128)}, u32[]{:S(2)}) copy-start(f32[1,4096]{1,0:T(1,128)} %param.9) | copy-start | bytes 49156

commit v6 on v3

v6 whole, which is shorter than its diff:
```python
import functools

import jax
import jax.numpy as jnp
from jax import lax
from jax.experimental import pallas as pl
from jax.experimental.pallas import tpu as pltpu
from jax.sharding import PartitionSpec as P

BLOCK = 128
Y_LEVELS = 8
W_LEVELS = 7


epsilon = 1e-06


def as_bf16_value(value):
    return lax.reduce_precision(value, exponent_bits=8, mantissa_bits=7)


def code_rows(grad_out, grad_dither):
    row_count, feat_width = grad_out.shape
    block_count = feat_width // BLOCK
    grad_float = grad_out.astype(jnp.float32).reshape(row_count, block_count, BLOCK)
    magnitude = jnp.max(jnp.abs(grad_float), axis=2)
    y_scale = ((magnitude + epsilon) / Y_LEVELS).astype(jnp.bfloat16)
    scaled = grad_float / y_scale.astype(jnp.float32)[:, :, None]
    held = as_bf16_value(scaled.reshape(row_count, feat_width) + grad_dither)
    values = held.reshape(row_count, block_count, BLOCK) * y_scale.astype(jnp.float32)[:, :, None]
    return values.reshape(row_count, feat_width).astype(jnp.bfloat16)


def group_terms(partial_value, feature_part, hidden_part):
    feat_rows, unit_cols = partial_value.shape
    block_count = feat_rows // BLOCK
    blocks = partial_value.reshape(block_count, BLOCK, unit_cols)
    magnitude = jnp.max(jnp.abs(blocks), axis=1)
    block_scale = ((magnitude + epsilon) / W_LEVELS).astype(jnp.bfloat16)
    scaled = (blocks / block_scale.astype(jnp.float32)[:, None, :]).reshape(feat_rows, unit_cols)
    held = as_bf16_value(scaled + hidden_part[None, :] + feature_part[:, None])
    values = held.reshape(block_count, BLOCK, unit_cols) * block_scale.astype(jnp.float32)[:, None, :]
    return values.reshape(feat_rows, unit_cols).astype(jnp.bfloat16)


MESH = pl.DeviceIdType.MESH
RING = 4
TENSOR_RING = (0, 1, 3, 2, 4, 5, 7, 6)


def dp_at(y, x, z):
    return y * 8 + x * 2 + z


def ring_member(position):
    pair, within = position // 2, position % 2
    return pair * 2 + (within + pair) % 2


def sent_index(pos, direction, step):
    return (pos - direction * (step + 1) + 2 * RING) % RING


def remote(src, dst, send_sem, recv_sem, peer):
    return pltpu.make_async_remote_copy(
        src_ref=src, dst_ref=dst, send_sem=send_sem, recv_sem=recv_sem,
        device_id=peer, device_id_type=MESH)


def reduce_steps(chunk, terms_ref, out_ref, recv1, send1, res1, recv2, send2, res2, recvz, sendz,
                 ss1, sr1, ss2, sr2, ssz, srz):
    dp = lax.axis_index("dp")
    y, x, z = dp // 8, (dp // 2) % 4, dp % 2
    rows, cols = terms_ref.shape[2], terms_ref.shape[3]
    half, width = rows // 2, cols // 2
    x_up, x_dn = dp_at(y, (x + 1) % RING, z), dp_at(y, (x + RING - 1) % RING, z)
    y_up, y_dn = dp_at((y + 1) % RING, x, z), dp_at((y + RING - 1) % RING, x, z)
    first = [
        (x, 1, x_up, 0, 0, True),
        (x, -1, x_dn, half, 0, True),
        (y, 1, y_up, 0, width, False),
        (y, -1, y_dn, half, width, False),
    ]

    def local1(k, index):
        _, _, _, r0, c0, over_x = first[k]
        if over_x:
            return terms_ref.at[:, index, pl.ds(r0, half), pl.ds(c0, width)]
        return terms_ref.at[index, :, pl.ds(r0, half), pl.ds(c0, width)]

    pending = []
    copies = [None] * 4
    for k, (pos, direction, target, _, _, _) in enumerate(first):
        copies[k] = remote(local1(k, sent_index(pos, direction, 0)), recv1.at[k, 0],
                           ss1.at[k, 0], sr1.at[k, 0], {"dp": target})
        copies[k].start()
        pending.append(copies[k])
    yield
    for step in range(1, RING - 1):
        for k, (pos, direction, target, _, _, _) in enumerate(first):
            copies[k].wait_recv()
            index = sent_index(pos, direction, step)
            acc = recv1[k, step - 1].astype(jnp.float32) + local1(k, index)[...].astype(jnp.float32)
            send1[k, step - 1] = acc.astype(jnp.bfloat16)
            copies[k] = remote(send1.at[k, step - 1], recv1.at[k, step],
                               ss1.at[k, step], sr1.at[k, step], {"dp": target})
            copies[k].start()
            pending.append(copies[k])
        yield
    for k, (pos, _, _, _, _, _) in enumerate(first):
        copies[k].wait_recv()
        res1[k] = recv1[k, RING - 2].astype(jnp.float32) + local1(k, pos)[...].astype(jnp.float32)

    second = [(y, 1, y_up), (y, -1, y_dn), (x, 1, x_up), (x, -1, x_dn)]
    for k, (pos, direction, target) in enumerate(second):
        send2[k, 0] = res1[k, sent_index(pos, direction, 0)].astype(jnp.bfloat16)
        copies[k] = remote(send2.at[k, 0], recv2.at[k, 0], ss2.at[k, 0], sr2.at[k, 0], {"dp": target})
        copies[k].start()
        pending.append(copies[k])
    yield
    for step in range(1, RING - 1):
        for k, (pos, direction, target) in enumerate(second):
            copies[k].wait_recv()
            index = sent_index(pos, direction, step)
            acc = recv2[k, step - 1].astype(jnp.float32) + res1[k, index]
            send2[k, step] = acc.astype(jnp.bfloat16)
            copies[k] = remote(send2.at[k, step], recv2.at[k, step],
                               ss2.at[k, step], sr2.at[k, step], {"dp": target})
            copies[k].start()
            pending.append(copies[k])
        yield
    for k, (pos, _, _) in enumerate(second):
        copies[k].wait_recv()
        res2[k] = recv2[k, RING - 2].astype(jnp.float32) + res1[k, pos]

    swap = remote(sendz, recvz, ssz, srz, {"dp": dp_at(y, x, 1 - z)})
    corners = [(0, 0), (half, 0), (0, width), (half, width)]

    @pl.when(z != chunk)
    def _():
        for k in range(4):
            sendz[k] = res2[k].astype(jnp.bfloat16)
        swap.start()

    yield

    @pl.when(z == chunk)
    def _():
        swap.wait_recv()
        for k, (r0, c0) in enumerate(corners):
            out_ref[pl.ds(r0, half), pl.ds(c0, width)] = res2[k] + recvz[k].astype(jnp.float32)

    @pl.when(z != chunk)
    def _():
        for k, (r0, c0) in enumerate(corners):
            out_ref[pl.ds(r0, half), pl.ds(c0, width)] = res2[k]
        swap.wait_send()

    for copy in pending:
        copy.wait_send()


def gather_steps(local_ref, out_ref, send_sem, recv_sem):
    n = len(TENSOR_RING)
    me = lax.axis_index("tensor")
    pair = me // 2
    pos = pair * 2 + (me % 2 + pair) % 2
    right = ring_member((pos + 1) % n)
    left = ring_member((pos + n - 1) % n)
    rows, cols = local_ref.shape
    width = cols // 2
    out_ref[pl.ds(pl.multiple_of(me * rows, rows), rows), :] = local_ref[...]
    streams = [(right, 1, 0), (left, -1, width)]
    pending = []
    copies = [None, None]
    for step in range(n - 1):
        for d, (target, direction, c0) in enumerate(streams):
            if step == 0:
                src = local_ref.at[:, pl.ds(c0, width)]
            else:
                copies[d].wait_recv()
                owner = ring_member((pos - direction * step + 2 * n) % n)
                src = out_ref.at[pl.ds(pl.multiple_of(owner * rows, rows), rows), pl.ds(c0, width)]
            owner = ring_member((pos - direction * step + 2 * n) % n)
            copies[d] = remote(src, out_ref.at[pl.ds(pl.multiple_of(owner * rows, rows), rows), pl.ds(c0, width)],
                               send_sem.at[d, step], recv_sem.at[d, step], {"tensor": target})
            copies[d].start()
            pending.append(copies[d])
        yield
    for d in range(2):
        copies[d].wait_recv()
    for copy in pending:
        copy.wait_send()


def comm_kernel(chunk, do_reduce, do_gather, *refs):
    refs = list(refs)
    terms_ref = refs.pop(0) if do_reduce else None
    local_ref = refs.pop(0) if do_gather else None
    out_ref = refs.pop(0) if do_reduce else None
    gathered_ref = refs.pop(0) if do_gather else None
    reduce_scratch = refs[:14] if do_reduce else None
    gather_scratch = refs[-2:] if do_gather else None

    peers = []
    if do_reduce:
        dp = lax.axis_index("dp")
        y, x, z = dp // 8, (dp // 2) % 4, dp % 2
        for peer in (dp_at(y, (x + 1) % RING, z), dp_at(y, (x + RING - 1) % RING, z),
                     dp_at((y + 1) % RING, x, z), dp_at((y + RING - 1) % RING, x, z), dp_at(y, x, 1 - z)):
            peers.append({"dp": peer})
    if do_gather:
        n = len(TENSOR_RING)
        me = lax.axis_index("tensor")
        pair = me // 2
        pos = pair * 2 + (me % 2 + pair) % 2
        for peer in (ring_member((pos + 1) % n), ring_member((pos + n - 1) % n)):
            peers.append({"tensor": peer})
    barrier = pltpu.get_barrier_semaphore()
    for peer in peers:
        pl.semaphore_signal(barrier, inc=1, device_id=peer, device_id_type=MESH)
    pl.semaphore_wait(barrier, len(peers))

    runs = []
    if do_reduce:
        runs.append(reduce_steps(chunk, terms_ref, out_ref, *reduce_scratch))
    if do_gather:
        runs.append(gather_steps(local_ref, gathered_ref, *gather_scratch))
    while runs:
        for run in list(runs):
            try:
                next(run)
            except StopIteration:
                runs.remove(run)


def communicate(chunk, terms=None, local=None, collective_id=0):
    do_reduce, do_gather = terms is not None, local is not None
    args, outs, scratch = [], [], []
    if do_reduce:
        rows, cols = terms.shape[2], terms.shape[3]
        half, width = rows // 2, cols // 2
        args.append(terms)
        outs.append(jax.ShapeDtypeStruct((rows, cols), jnp.float32))
        scratch += [
            pltpu.VMEM((4, RING - 1, RING, half, width), jnp.bfloat16),
            pltpu.VMEM((4, RING - 2, RING, half, width), jnp.bfloat16),
            pltpu.VMEM((4, RING, half, width), jnp.float32),
            pltpu.VMEM((4, RING - 1, half, width), jnp.bfloat16),
            pltpu.VMEM((4, RING - 1, half, width), jnp.bfloat16),
            pltpu.VMEM((4, half, width), jnp.float32),
            pltpu.VMEM((4, half, width), jnp.bfloat16),
            pltpu.VMEM((4, half, width), jnp.bfloat16),
            pltpu.SemaphoreType.DMA((4, RING - 1)),
            pltpu.SemaphoreType.DMA((4, RING - 1)),
            pltpu.SemaphoreType.DMA((4, RING - 1)),
            pltpu.SemaphoreType.DMA((4, RING - 1)),
            pltpu.SemaphoreType.DMA(()),
            pltpu.SemaphoreType.DMA(()),
        ]
    if do_gather:
        n = len(TENSOR_RING)
        args.append(local)
        outs.append(jax.ShapeDtypeStruct((n * local.shape[0], local.shape[1]), local.dtype))
        scratch += [pltpu.SemaphoreType.DMA((2, n - 1)), pltpu.SemaphoreType.DMA((2, n - 1))]
    return pl.pallas_call(
        functools.partial(comm_kernel, chunk, do_reduce, do_gather),
        out_shape=tuple(outs),
        in_specs=[pl.BlockSpec(memory_space=pltpu.VMEM)] * len(args),
        out_specs=tuple(pl.BlockSpec(memory_space=pltpu.VMEM) for _ in outs),
        scratch_shapes=scratch,
        compiler_params=pltpu.CompilerParams(
            collective_id=collective_id, has_side_effects=True, vmem_limit_bytes=48 * 1024 * 1024),
    )(*args)


def per_device(grad_out, activations, grad_dither, hidden_dither, feature_dither):
    row_count, feat_width = grad_out.shape
    blocks = feat_width // BLOCK
    y_local = code_rows(grad_out, grad_dither)
    y_local = y_local.reshape(row_count, blocks // 2, 2, BLOCK).transpose(0, 2, 1, 3).reshape(row_count, feat_width)
    feature_noise = feature_dither[0].reshape(blocks // 2, 2, BLOCK).transpose(1, 0, 2).reshape(feat_width)
    hidden_noise = hidden_dither[0]
    half = feat_width // 2

    def terms_of(y_hat, part):
        partial_value = lax.dot_general(
            y_hat, activations, (((0,), (0,)), ((), ())), preferred_element_type=jnp.float32
        )
        terms = group_terms(partial_value, feature_noise[part * half:(part + 1) * half], hidden_noise)
        return terms.reshape(RING, RING, BLOCK, terms.shape[1])

    (first_y,) = communicate(0, None, y_local[:, :half], collective_id=1)
    first_out, second_y = communicate(0, terms_of(first_y, 0), y_local[:, half:], collective_id=2)
    (second_out,) = communicate(1, terms_of(second_y, 1), None, collective_id=0)
    z = lax.axis_index("dp") % 2
    return jnp.where(z == 0, first_out, second_out)


def solution(mesh):
    placed = (
        P(("dp", "tensor"), None),
        P("dp", "tensor"),
        P(("dp", "tensor"), None),
        P("dp", "tensor"),
        P("dp", None),
    )
    return jax.shard_map(
        per_device, mesh=mesh, in_specs=placed, out_specs=P("dp", "tensor"), check_vma=False
    )
```

time: 240 us -> 226 us (0.942)
  Pallas kernels: 105 us -> 180 us
  waiting for transfers between devices: 72.1 us -> 0 us
  between operations: 13.5 us -> 0.16 us
  matrix products: 19.7 us -> 15.7 us
  other arithmetic: 26.3 us -> 23.2 us
  local copies, waits for them, and re-layouts: 2.92 us -> 5.93 us
    pallas_call x1 -> x3, Pallas kernels: 105 us -> 180 us  [communicate(): pl.pallas_call(functools.partial(comm_kernel, chunk, do_reduce, do_gather...]
    all_gather x1 -> x0, waiting for transfers between devices: 72.1 us -> none  [per_device(): y_hat = lax.all_gather(y_local, 'tensor', axis=0, tiled=True)]
    convert_element_type x2 -> x0, other arithmetic: 15.3 us -> none  [the longest x1 12.6 us: group_terms(): (scaled + hidden_part[None, :] + feature_part[:, None]).astype(jnp.bfloat16)]
    convert_element_type x1 -> x2, other arithmetic: 7.35 us -> 14.7 us  [group_terms(): return values.reshape(feat_rows, unit_cols).astype(jnp.bfloat16)]
    dot_general x1 -> x2, matrix products: 19.7 us -> 15.7 us  [terms_of(): lax.dot_general(y_hat, activations, (((0,), (0,)), ((), ())), preferred_e...]
    reshape x0 -> x2, local copies, waits for them, and re-layouts: none -> 2.69 us  [per_device(): y_local.reshape(row_count, blocks // 2, 2, BLOCK).transpose(0, 2, 1, 3)]
  transfers between devices with their start and end apart: 1 -> 0, of which waited for: 1 -> 0; matrix products, arithmetic and copies ran while one was open for 0% -> 0% of each run, Pallas kernels for 0% -> 0%
where the time goes in v6:
time: 226 us; the launch traced here: 225 us
  Pallas kernels  180 us (80%)
  other arithmetic  23.2 us (10%)
  matrix products  15.7 us (7%)
  local copies, waits for them, and re-layouts  5.93 us (3%)
    pallas_call x3, Pallas kernels, communicate(): pl.pallas_call(functools.partial(comm_kernel, chunk, do_reduce, do_gather...  180 us
    dot_general x2, matrix products, terms_of(): lax.dot_general(y_hat, activations, (((0,), (0,)), ((), ())), preferred_e...  15.7 us
    convert_element_type x2, other arithmetic, group_terms(): return values.reshape(feat_rows, unit_cols).astype(jnp.bfloat16)  14.7 us

profile of v6, /device:TPU:32, one launch (start us, length us, event | category | flops | bytes accessed | tf_op | source)
XLA Modules:
  0.0 225.3 jit_solution(13546469833130237751)
XLA Ops:
  0.0 0.0 copy-start
  0.0 1.4 fusion.8
  1.5 1.4 copy.7
  2.9 1.9 reduce_max.27
  4.8 0.5 div.47
  5.3 2.9 %fusion.12 = bf16[96,4096]{1,0:T(8,128)(2,1)S(1)} fusion(f32[96,4096]{1,0:T(8,128)} %param.7, f32[12,8,32,128]{3,2,1,0:T(8,128)S(1)} %bitcast.58, bf16[96,4096]{1,0:T(8,128)(2,1)} %param.5), kind=kLoop, calls=%fused_computation.20 | loop fusion | flops 2359296 | bytes 4718592 | tf_op jit(solution)/shard_map/convert_element_type | solution.py:31
  8.1 1.4 reshape.58
  9.6 1.3 copy.6
  10.8 0.3 copy.14
  11.1 0.1 fusion.16
  11.2 42.7 %shard_map.55 = bf16[768,2048]{1,0:T(8,128)(2,1)S(1)} custom-call(bf16[96,2048]{1,0:T(8,128)(2,1)S(1)} %get-tuple-element.10.refs_0_), custom_call_target="tpu_custom_call" | custom-call | tf_op jit(solution)/shard_map/pallas_call | solution.py:266
  53.9 0.0 copy-start.4
  53.9 0.0 copy-start.5
  54.0 9.3 %bitcast_reduce_fusion.1 = (f32[16,1792]{1,0:T(8,128)S(1)}, f32[2048,1792]{1,0:T(8,128)}) fusion(bf16[768,2048]{1,0:T(8,128)(2,1)S(1)} %shard_map.55, bf16[768,1792]{1,0:T(8,128)(2,1)S(1)} %copy-done), kind=kOutput, calls=%fused_computation.11 | convolution fusion | flops 5644455936 | bytes 20692992 | tf_op jit(solution)/shard_map/dot_general | solution.py:287
  63.4 9.5 %fusion.6 = bf16[2048,1792]{1,0:T(8,128)(2,1)} fusion(f32[2048,1792]{1,0:T(8,128)} %get-tuple-element.14, f32[2048]{0:T(1024)S(1)} %bitcast.62, f32[1792]{0:T(1024)S(1)} %reduce, f32[16,1792]{1,0:T(8,128)S(1)} %fusion.13), kind=kLoop, calls=%fused_computation.12 | loop fusion | flops 22020096 | bytes 22150144 | tf_op jit(solution)/shard_map/convert_element_type | solution.py:43
  72.9 71.1 %shard_map.56 = (f32[128,1792]{1,0:T(8,128)S(1)}, bf16[768,2048]{1,0:T(8,128)(2,1)S(1)}) custom-call(bf16[4,4,128,1792]{3,2,1,0:T(8,128)(2,1)} %bitcast.55, bf16[96,2048]{1,0:T(8,128)(2,1)S(1)} %get-tuple-element.9.refs_1_), custom_call_target="tpu_custom_call" | custom-call | tf_op jit(solution)/shard_map/pallas_call | solution.py:266
  144.0 0.0 copy-start.3
  144.0 6.4 %bitcast_reduce_fusion = (f32[16,1792]{1,0:T(8,128)S(1)}, f32[2048,1792]{1,0:T(8,128)S(1)}) fusion(bf16[768,2048]{1,0:T(8,128)(2,1)S(1)} %get-tuple-element.8, bf16[768,1792]{1,0:T(8,128)(2,1)S(1)} %copy-done), kind=kOutput, calls=%fused_computation.10 | convolution fusion | flops 5644455936 | bytes 20692992 | tf_op jit(solution)/shard_map/dot_general | solution.py:287
  150.4 0.0 copy-done.3
  150.4 5.2 %fusion.7 = bf16[2048,1792]{1,0:T(8,128)(2,1)} fusion(f32[2048,1792]{1,0:T(8,128)S(1)} %get-tuple-element.16, f32[2048]{0:T(1024)S(1)} %bitcast.61, f32[16,1792]{1,0:T(8,128)S(1)} %fusion.14, f32[1792]{0:T(1024)S(1)} %reduce), kind=kLoop, calls=%fused_computation.13 | loop fusion | flops 22020096 | bytes 22150144 | tf_op jit(solution)/shard_map/convert_element_type | solution.py:43
  155.7 66.5 %shard_map.57 = f32[128,1792]{1,0:T(8,128)S(1)} custom-call(bf16[4,4,128,1792]{3,2,1,0:T(8,128)(2,1)} %bitcast.56), custom_call_target="tpu_custom_call" | custom-call | tf_op jit(solution)/shard_map/pallas_call | solution.py:266
  222.2 0.9 copy-done.2
  223.1 2.2 broadcast_select_fusion
  225.3 0.0 copy-done.1
  (10 shorter events, 0.1 us)
Async XLA Ops:
  0.0 53.9 %copy-start = (bf16[768,1792]{1,0:T(8,128)(2,1)S(1)}, bf16[768,1792]{1,0:T(8,128)(2,1)}, u32[]{:S(2)}) copy-start(bf16[768,1792]{1,0:T(8,128)(2,1)} %param.6) | copy-start | bytes 8257540
  53.9 9.4 %copy-start.4 = (f32[1,4096]{1,0:T(1,128)S(1)}, f32[1,4096]{1,0:T(1,128)}, u32[]{:S(2)}) copy-start(f32[1,4096]{1,0:T(1,128)} %param.9) | copy-start | bytes 49156
  53.9 9.4 %copy-start.5 = (f32[1,1792]{1,0:T(1,128)S(1)}, f32[1,1792]{1,0:T(1,128)}, u32[]{:S(2)}) copy-start(f32[1,1792]{1,0:T(1,128)} %param.8) | copy-start | bytes 21508
  144.0 6.4 %copy-start.3 = (f32[128,1792]{1,0:T(8,128)}, f32[128,1792]{1,0:T(8,128)S(1)}, u32[]{:S(2)}) copy-start(f32[128,1792]{1,0:T(8,128)S(1)} %get-tuple-element.7) | copy-start | bytes 2752516
  155.7 69.6 %copy-start.1 = (bf16[768,1792]{1,0:T(8,128)(2,1)S(1)}, bf16[768,1792]{1,0:T(8,128)(2,1)}, u32[]{:S(2)}) copy-start(bf16[768,1792]{1,0:T(8,128)(2,1)} %param.6) | copy-start | bytes 8257540
  222.2 0.9 copy-start.2

commit v7 on v6

--- a/solution.py
+++ b/solution.py
@@ -226,12 +226,16 @@
         runs.append(reduce_steps(chunk, terms_ref, out_ref, *reduce_scratch))
     if do_gather:
         runs.append(gather_steps(local_ref, gathered_ref, *gather_scratch))
+    pattern = [0, 1, 1] if len(runs) == 2 else [0]
     while runs:
-        for run in list(runs):
-            try:
-                next(run)
-            except StopIteration:
-                runs.remove(run)
+        for which in pattern:
+            if which < len(runs):
+                try:
+                    next(runs[which])
+                except StopIteration:
+                    runs.pop(which)
+                    pattern = [0]
+                    break
 
 
 def communicate(chunk, terms=None, local=None, collective_id=0):

time: 226 us -> 223 us (0.987)
    pallas_call x3, Pallas kernels: 180 us -> 178 us  [communicate(): pl.pallas_call(functools.partial(comm_kernel, chunk, do_reduce, do_gather...]
where the time goes in v7:
time: 223 us
  Pallas kernels  178 us (80%)
  other arithmetic  23.2 us (10%)
  matrix products  15.7 us (7%)
  local copies, waits for them, and re-layouts  5.93 us (3%)
    pallas_call x3, Pallas kernels, communicate(): pl.pallas_call(functools.partial(comm_kernel, chunk, do_reduce, do_gather...  178 us
    dot_general x2, matrix products, terms_of(): lax.dot_general(y_hat, activations, (((0,), (0,)), ((), ())), preferred_e...  15.7 us
    convert_element_type x2, other arithmetic, group_terms(): return values.reshape(feat_rows, unit_cols).astype(jnp.bfloat16)  14.7 us

profile of v7, /device:TPU:32, one launch (start us, length us, event | category | flops | bytes accessed | tf_op | source)
XLA Modules:
  0.0 222.5 jit_solution(2503729085827277317)
XLA Ops:
  0.0 0.0 copy-start
  0.0 1.4 fusion.8
  1.5 1.4 copy.7
  2.9 1.9 reduce_max.27
  4.8 0.5 div.47
  5.3 2.9 %fusion.12 = bf16[96,4096]{1,0:T(8,128)(2,1)S(1)} fusion(f32[96,4096]{1,0:T(8,128)} %param.7, f32[12,8,32,128]{3,2,1,0:T(8,128)S(1)} %bitcast.58, bf16[96,4096]{1,0:T(8,128)(2,1)} %param.5), kind=kLoop, calls=%fused_computation.20 | loop fusion | flops 2359296 | bytes 4718592 | tf_op jit(solution)/shard_map/convert_element_type | solution.py:31
  8.1 1.4 reshape.58
  9.6 1.3 copy.6
  10.8 0.3 copy.14
  11.1 0.1 fusion.16
  11.2 42.7 %shard_map.55 = bf16[768,2048]{1,0:T(8,128)(2,1)S(1)} custom-call(bf16[96,2048]{1,0:T(8,128)(2,1)S(1)} %get-tuple-element.10.refs_0_), custom_call_target="tpu_custom_call" | custom-call | tf_op jit(solution)/shard_map/pallas_call | solution.py:270
  53.9 0.0 copy-done
  53.9 0.0 copy-start.4
  53.9 0.0 copy-start.5
  54.0 9.3 %bitcast_reduce_fusion.1 = (f32[16,1792]{1,0:T(8,128)S(1)}, f32[2048,1792]{1,0:T(8,128)}) fusion(bf16[768,2048]{1,0:T(8,128)(2,1)S(1)} %shard_map.55, bf16[768,1792]{1,0:T(8,128)(2,1)S(1)} %copy-done), kind=kOutput, calls=%fused_computation.11 | convolution fusion | flops 5644455936 | bytes 20692992 | tf_op jit(solution)/shard_map/dot_general | solution.py:291
  63.3 0.0 copy-done.4
  63.4 9.5 %fusion.6 = bf16[2048,1792]{1,0:T(8,128)(2,1)} fusion(f32[2048,1792]{1,0:T(8,128)} %get-tuple-element.14, f32[2048]{0:T(1024)S(1)} %bitcast.62, f32[1792]{0:T(1024)S(1)} %reduce, f32[16,1792]{1,0:T(8,128)S(1)} %fusion.13), kind=kLoop, calls=%fused_computation.12 | loop fusion | flops 22020096 | bytes 22150144 | tf_op jit(solution)/shard_map/convert_element_type | solution.py:43
  72.9 71.8 %shard_map.56 = (f32[128,1792]{1,0:T(8,128)S(1)}, bf16[768,2048]{1,0:T(8,128)(2,1)S(1)}) custom-call(bf16[4,4,128,1792]{3,2,1,0:T(8,128)(2,1)} %bitcast.55, bf16[96,2048]{1,0:T(8,128)(2,1)S(1)} %get-tuple-element.9.refs_1_), custom_call_target="tpu_custom_call" | custom-call | tf_op jit(solution)/shard_map/pallas_call | solution.py:270
  144.7 0.0 copy-start.3
  144.8 6.4 %bitcast_reduce_fusion = (f32[16,1792]{1,0:T(8,128)S(1)}, f32[2048,1792]{1,0:T(8,128)S(1)}) fusion(bf16[768,2048]{1,0:T(8,128)(2,1)S(1)} %get-tuple-element.8, bf16[768,1792]{1,0:T(8,128)(2,1)S(1)} %copy-done), kind=kOutput, calls=%fused_computation.10 | convolution fusion | flops 5644455936 | bytes 20692992 | tf_op jit(solution)/shard_map/dot_general | solution.py:291
  151.2 5.2 %fusion.7 = bf16[2048,1792]{1,0:T(8,128)(2,1)} fusion(f32[2048,1792]{1,0:T(8,128)S(1)} %get-tuple-element.16, f32[2048]{0:T(1024)S(1)} %bitcast.61, f32[16,1792]{1,0:T(8,128)S(1)} %fusion.14, f32[1792]{0:T(1024)S(1)} %reduce), kind=kLoop, calls=%fused_computation.13 | loop fusion | flops 22020096 | bytes 22150144 | tf_op jit(solution)/shard_map/convert_element_type | solution.py:43
  156.4 63.0 %shard_map.57 = f32[128,1792]{1,0:T(8,128)S(1)} custom-call(bf16[4,4,128,1792]{3,2,1,0:T(8,128)(2,1)} %bitcast.56), custom_call_target="tpu_custom_call" | custom-call | tf_op jit(solution)/shard_map/pallas_call | solution.py:270
  219.4 0.9 copy-done.2
  220.3 2.2 broadcast_select_fusion
  (10 shorter events, 0.1 us)
Async XLA Ops:
  0.0 53.9 %copy-start = (bf16[768,1792]{1,0:T(8,128)(2,1)S(1)}, bf16[768,1792]{1,0:T(8,128)(2,1)}, u32[]{:S(2)}) copy-start(bf16[768,1792]{1,0:T(8,128)(2,1)} %param.6) | copy-start | bytes 8257540
  53.9 9.4 %copy-start.4 = (f32[1,4096]{1,0:T(1,128)S(1)}, f32[1,4096]{1,0:T(1,128)}, u32[]{:S(2)}) copy-start(f32[1,4096]{1,0:T(1,128)} %param.9) | copy-start | bytes 49156
  53.9 9.4 %copy-start.5 = (f32[1,1792]{1,0:T(1,128)S(1)}, f32[1,1792]{1,0:T(1,128)}, u32[]{:S(2)}) copy-start(f32[1,1792]{1,0:T(1,128)} %param.8) | copy-start | bytes 21508
  144.7 6.4 %copy-start.3 = (f32[128,1792]{1,0:T(8,128)}, f32[128,1792]{1,0:T(8,128)S(1)}, u32[]{:S(2)}) copy-start(f32[128,1792]{1,0:T(8,128)S(1)} %get-tuple-element.7) | copy-start | bytes 2752516
  156.4 66.1 %copy-start.1 = (bf16[768,1792]{1,0:T(8,128)(2,1)S(1)}, bf16[768,1792]{1,0:T(8,128)(2,1)}, u32[]{:S(2)}) copy-start(bf16[768,1792]{1,0:T(8,128)(2,1)} %param.6) | copy-start | bytes 8257540
  219.4 0.9 copy-start.2

commit v8 on v7

--- a/solution.py
+++ b/solution.py
@@ -17,18 +17,6 @@
 
 def as_bf16_value(value):
     return lax.reduce_precision(value, exponent_bits=8, mantissa_bits=7)
-
-
-def code_rows(grad_out, grad_dither):
-    row_count, feat_width = grad_out.shape
-    block_count = feat_width // BLOCK
-    grad_float = grad_out.astype(jnp.float32).reshape(row_count, block_count, BLOCK)
-    magnitude = jnp.max(jnp.abs(grad_float), axis=2)
-    y_scale = ((magnitude + epsilon) / Y_LEVELS).astype(jnp.bfloat16)
-    scaled = grad_float / y_scale.astype(jnp.float32)[:, :, None]
-    held = as_bf16_value(scaled.reshape(row_count, feat_width) + grad_dither)
-    values = held.reshape(row_count, block_count, BLOCK) * y_scale.astype(jnp.float32)[:, :, None]
-    return values.reshape(row_count, feat_width).astype(jnp.bfloat16)
 
 
 def group_terms(partial_value, feature_part, hidden_part):
@@ -278,11 +266,33 @@
     )(*args)
 
 
+def code_kernel(grad_ref, dither_ref, first_ref, second_ref):
+    blocks = grad_ref.shape[1] // BLOCK
+    for block in range(blocks):
+        cols = pl.ds(block * BLOCK, BLOCK)
+        grad_float = grad_ref[:, cols].astype(jnp.float32)
+        magnitude = jnp.max(jnp.abs(grad_float), axis=1, keepdims=True)
+        y_scale = ((magnitude + epsilon) / Y_LEVELS).astype(jnp.bfloat16).astype(jnp.float32)
+        code = (grad_float / y_scale + dither_ref[:, cols]).astype(jnp.bfloat16).astype(jnp.float32)
+        target = first_ref if block % 2 == 0 else second_ref
+        target[:, pl.ds((block // 2) * BLOCK, BLOCK)] = (code * y_scale).astype(jnp.bfloat16)
+
+
+def coded_halves(grad_out, grad_dither):
+    rows, feat_width = grad_out.shape
+    half = jax.ShapeDtypeStruct((rows, feat_width // 2), jnp.bfloat16)
+    return pl.pallas_call(
+        code_kernel,
+        out_shape=(half, half),
+        in_specs=[pl.BlockSpec(memory_space=pltpu.VMEM)] * 2,
+        out_specs=(pl.BlockSpec(memory_space=pltpu.VMEM), pl.BlockSpec(memory_space=pltpu.VMEM)),
+    )(grad_out, grad_dither)
+
+
 def per_device(grad_out, activations, grad_dither, hidden_dither, feature_dither):
     row_count, feat_width = grad_out.shape
     blocks = feat_width // BLOCK
-    y_local = code_rows(grad_out, grad_dither)
-    y_local = y_local.reshape(row_count, blocks // 2, 2, BLOCK).transpose(0, 2, 1, 3).reshape(row_count, feat_width)
+    first_local, second_local = coded_halves(grad_out, grad_dither)
     feature_noise = feature_dither[0].reshape(blocks // 2, 2, BLOCK).transpose(1, 0, 2).reshape(feat_width)
     hidden_noise = hidden_dither[0]
     half = feat_width // 2
@@ -294,8 +304,8 @@
         terms = group_terms(partial_value, feature_noise[part * half:(part + 1) * half], hidden_noise)
         return terms.reshape(RING, RING, BLOCK, terms.shape[1])
 
-    (first_y,) = communicate(0, None, y_local[:, :half], collective_id=1)
-    first_out, second_y = communicate(0, terms_of(first_y, 0), y_local[:, half:], collective_id=2)
+    (first_y,) = communicate(0, None, first_local, collective_id=1)
+    first_out, second_y = communicate(0, terms_of(first_y, 0), second_local, collective_id=2)
     (second_out,) = communicate(1, terms_of(second_y, 1), None, collective_id=0)
     z = lax.axis_index("dp") % 2
     return jnp.where(z == 0, first_out, second_out)

time: 223 us -> 216 us (0.969)
  other arithmetic: 23.2 us -> 17 us
  local copies, waits for them, and re-layouts: 5.93 us -> 1.96 us
  Pallas kernels: 178 us -> 181 us
    pallas_call x0 -> x1, Pallas kernels: none -> 3.4 us  [coded_halves(): pl.pallas_call(code_kernel, out_shape=(half, half), in_specs=[pl.BlockSpe...]
    convert_element_type x2 -> x0, other arithmetic: 2.88 us -> none  [the longest x1 2.87 us: code_rows(): return values.reshape(row_count, feat_width).astype(jnp.bfloat16)]
    reshape x2 -> x0, local copies, waits for them, and re-layouts: 2.69 us -> none  [per_device(): y_local.reshape(row_count, blocks // 2, 2, BLOCK).transpose(0, 2, 1, 3)]
where the time goes in v8:
time: 216 us; the launch traced here: 215 us
  Pallas kernels  181 us (84%)
  other arithmetic  17 us (8%)
  matrix products  15.7 us (7%)
    pallas_call x3, Pallas kernels, communicate(): pl.pallas_call(functools.partial(comm_kernel, chunk, do_reduce, do_gather...  177 us
    dot_general x2, matrix products, terms_of(): lax.dot_general(y_hat, activations, (((0,), (0,)), ((), ())), preferred_e...  15.7 us
    convert_element_type x2, other arithmetic, group_terms(): return values.reshape(feat_rows, unit_cols).astype(jnp.bfloat16)  14.7 us

profile of v8, /device:TPU:32, one launch (start us, length us, event | category | flops | bytes accessed | tf_op | source)
XLA Modules:
  0.0 215.4 jit_solution(4069841144564501548)
XLA Ops:
  0.0 0.0 copy-start
  0.0 3.4 %shard_map.55 = (bf16[96,2048]{1,0:T(8,128)(2,1)}, bf16[96,2048]{1,0:T(8,128)(2,1)}) custom-call(bf16[96,4096]{1,0:T(8,128)(2,1)} %grad_ref.1, f32[96,4096]{1,0:T(8,128)} %dither_ref.1), custom_call_target="tpu_custom_call" | custom-call | tf_op jit(solution)/shard_map/pallas_call | solution.py:284
  3.4 0.0 copy-start.3
  3.4 1.0 copy-done.3
  4.4 42.5 %shard_map.56 = bf16[768,2048]{1,0:T(8,128)(2,1)S(1)} custom-call(bf16[96,2048]{1,0:T(8,128)(2,1)S(1)} %copy-done.3), custom_call_target="tpu_custom_call" | custom-call | tf_op jit(solution)/shard_map/pallas_call | solution.py:258
  46.9 0.0 copy-done
  46.9 0.0 copy-start.5
  47.0 0.0 copy-start.6
  47.0 9.3 %bitcast_reduce_fusion.1 = (f32[16,1792]{1,0:T(8,128)S(1)}, f32[2048,1792]{1,0:T(8,128)}) fusion(bf16[768,2048]{1,0:T(8,128)(2,1)S(1)} %shard_map.56, bf16[768,1792]{1,0:T(8,128)(2,1)S(1)} %copy-done), kind=kOutput, calls=%fused_computation.11 | convolution fusion | flops 5644455936 | bytes 20692992 | tf_op jit(solution)/shard_map/dot_general | solution.py:301
  56.3 0.0 copy-start.4
  56.3 0.0 copy-done.5
  56.3 0.0 copy-done.6
  56.4 9.5 %fusion.6 = bf16[2048,1792]{1,0:T(8,128)(2,1)} fusion(f32[2048,1792]{1,0:T(8,128)} %get-tuple-element.16, f32[2048]{0:T(1024)S(1)} %bitcast.44, f32[1792]{0:T(1024)S(1)} %reduce, f32[16,1792]{1,0:T(8,128)S(1)} %fusion.8), kind=kLoop, calls=%fused_computation.12 | loop fusion | flops 22020096 | bytes 22150144 | tf_op jit(solution)/shard_map/convert_element_type | solution.py:31
  65.9 0.0 copy-done.4
  65.9 72.0 %shard_map.57 = (f32[128,1792]{1,0:T(8,128)S(1)}, bf16[768,2048]{1,0:T(8,128)(2,1)S(1)}) custom-call(bf16[4,4,128,1792]{3,2,1,0:T(8,128)(2,1)} %bitcast.41, bf16[96,2048]{1,0:T(8,128)(2,1)S(1)} %copy-done.4), custom_call_target="tpu_custom_call" | custom-call | tf_op jit(solution)/shard_map/pallas_call | solution.py:258
  137.9 0.0 copy-start.2
  137.9 6.4 %bitcast_reduce_fusion = (f32[16,1792]{1,0:T(8,128)S(1)}, f32[2048,1792]{1,0:T(8,128)S(1)}) fusion(bf16[768,2048]{1,0:T(8,128)(2,1)S(1)} %get-tuple-element.12, bf16[768,1792]{1,0:T(8,128)(2,1)S(1)} %copy-done), kind=kOutput, calls=%fused_computation.10 | convolution fusion | flops 5644455936 | bytes 20692992 | tf_op jit(solution)/shard_map/dot_general | solution.py:301
  144.3 0.0 copy-done.2
  144.3 5.2 %fusion.7 = bf16[2048,1792]{1,0:T(8,128)(2,1)} fusion(f32[2048,1792]{1,0:T(8,128)S(1)} %get-tuple-element.18, f32[2048]{0:T(1024)S(1)} %bitcast.43, f32[16,1792]{1,0:T(8,128)S(1)} %fusion.9, f32[1792]{0:T(1024)S(1)} %reduce), kind=kLoop, calls=%fused_computation.13 | loop fusion | flops 22020096 | bytes 22150144 | tf_op jit(solution)/shard_map/convert_element_type | solution.py:31
  149.5 62.7 %shard_map.58 = f32[128,1792]{1,0:T(8,128)S(1)} custom-call(bf16[4,4,128,1792]{3,2,1,0:T(8,128)(2,1)} %bitcast.42), custom_call_target="tpu_custom_call" | custom-call | tf_op jit(solution)/shard_map/pallas_call | solution.py:258
  212.2 0.0 copy-start.1
  212.2 0.9 copy-done.1
  213.2 2.2 %broadcast_select_fusion = f32[128,1792]{1,0:T(8,128)} fusion(f32[128,1792]{1,0:T(8,128)} %copy-done.2, f32[128,1792]{1,0:T(8,128)} %copy-done.1, pred[]{:T(512)S(6)} %eq.5), kind=kLoop, calls=%fused_computation.14 | loop fusion | flops 229376 | bytes 2752513 | tf_op jit(solution)/shard_map/jit(_where)/select_n | solution.py:311
  (4 shorter events, 0.1 us)
Async XLA Ops:
  0.0 46.9 %copy-start = (bf16[768,1792]{1,0:T(8,128)(2,1)S(1)}, bf16[768,1792]{1,0:T(8,128)(2,1)}, u32[]{:S(2)}) copy-start(bf16[768,1792]{1,0:T(8,128)(2,1)} %param.6) | copy-start | bytes 8257540
  3.4 1.0 copy-start.3
  46.9 9.4 %copy-start.5 = (f32[1,4096]{1,0:T(1,128)S(1)}, f32[1,4096]{1,0:T(1,128)}, u32[]{:S(2)}) copy-start(f32[1,4096]{1,0:T(1,128)} %param.9) | copy-start | bytes 49156
  47.0 9.4 %copy-start.6 = (f32[1,1792]{1,0:T(1,128)S(1)}, f32[1,1792]{1,0:T(1,128)}, u32[]{:S(2)}) copy-start(f32[1,1792]{1,0:T(1,128)} %param.8) | copy-start | bytes 21508
  56.3 9.6 %copy-start.4 = (bf16[96,2048]{1,0:T(8,128)(2,1)S(1)}, bf16[96,2048]{1,0:T(8,128)(2,1)}, u32[]{:S(2)}) copy-start(bf16[96,2048]{1,0:T(8,128)(2,1)} %get-tuple-element.10.refs_1_) | copy-start | bytes 1179652
  137.9 6.4 %copy-start.2 = (f32[128,1792]{1,0:T(8,128)}, f32[128,1792]{1,0:T(8,128)S(1)}, u32[]{:S(2)}) copy-start(f32[128,1792]{1,0:T(8,128)S(1)} %get-tuple-element.11) | copy-start | bytes 2752516
  212.2 0.9 copy-start.1

commit v9 on v8

--- a/solution.py
+++ b/solution.py
@@ -272,8 +272,8 @@
         cols = pl.ds(block * BLOCK, BLOCK)
         grad_float = grad_ref[:, cols].astype(jnp.float32)
         magnitude = jnp.max(jnp.abs(grad_float), axis=1, keepdims=True)
-        y_scale = ((magnitude + epsilon) / Y_LEVELS).astype(jnp.bfloat16).astype(jnp.float32)
-        code = (grad_float / y_scale + dither_ref[:, cols]).astype(jnp.bfloat16).astype(jnp.float32)
+        y_scale = as_bf16_value((magnitude + epsilon) / Y_LEVELS)
+        code = as_bf16_value(grad_float / y_scale + dither_ref[:, cols])
         target = first_ref if block % 2 == 0 else second_ref
         target[:, pl.ds((block // 2) * BLOCK, BLOCK)] = (code * y_scale).astype(jnp.bfloat16)
 
@@ -289,6 +289,39 @@
     )(grad_out, grad_dither)
 
 
+def terms_kernel(y_ref, act_ref, feature_ref, hidden_ref, out_ref):
+    partial_value = lax.dot_general(
+        y_ref[...], act_ref[...], (((0,), (0,)), ((), ())), preferred_element_type=jnp.float32
+    )
+    feat_rows, unit_cols = partial_value.shape
+    block_count = feat_rows // BLOCK
+    blocks = partial_value.reshape(block_count, BLOCK, unit_cols)
+    magnitude = jnp.max(jnp.abs(blocks), axis=1, keepdims=True)
+    block_scale = as_bf16_value((magnitude + epsilon) / W_LEVELS)
+    feature_part = feature_ref[...].reshape(block_count, BLOCK, 1)
+    code = blocks / block_scale + hidden_ref[...].reshape(1, 1, unit_cols) + feature_part
+    code = as_bf16_value(code)
+    out_ref[...] = (code * block_scale).astype(jnp.bfloat16).reshape(feat_rows, unit_cols)
+
+
+def group_terms_kernel(y_hat, activations, feature_part, hidden_part, tile=256):
+    tokens, feat_rows = y_hat.shape
+    unit_cols = activations.shape[1]
+    return pl.pallas_call(
+        terms_kernel,
+        out_shape=jax.ShapeDtypeStruct((feat_rows, unit_cols), jnp.bfloat16),
+        grid=(unit_cols // tile,),
+        in_specs=[
+            pl.BlockSpec((tokens, feat_rows), lambda j: (0, 0)),
+            pl.BlockSpec((tokens, tile), lambda j: (0, j)),
+            pl.BlockSpec((feat_rows, 1), lambda j: (0, 0)),
+            pl.BlockSpec((1, tile), lambda j: (0, j)),
+        ],
+        out_specs=pl.BlockSpec((feat_rows, tile), lambda j: (0, j)),
+        compiler_params=pltpu.CompilerParams(vmem_limit_bytes=48 * 1024 * 1024),
+    )(y_hat, activations, feature_part.reshape(feat_rows, 1), hidden_part.reshape(1, unit_cols))
+
+
 def per_device(grad_out, activations, grad_dither, hidden_dither, feature_dither):
     row_count, feat_width = grad_out.shape
     blocks = feat_width // BLOCK
@@ -298,10 +331,7 @@
     half = feat_width // 2
 
     def terms_of(y_hat, part):
-        partial_value = lax.dot_general(
-            y_hat, activations, (((0,), (0,)), ((), ())), preferred_element_type=jnp.float32
-        )
-        terms = group_terms(partial_value, feature_noise[part * half:(part + 1) * half], hidden_noise)
+        terms = group_terms_kernel(y_hat, activations, feature_noise[part * half:(part + 1) * half], hidden_noise)
         return terms.reshape(RING, RING, BLOCK, terms.shape[1])
 
     (first_y,) = communicate(0, None, first_local, collective_id=1)

time: 216 us -> 229 us (1.060)
  Pallas kernels: 181 us -> 217 us
  other arithmetic: 17 us -> 1.02 us
  matrix products: 15.7 us -> 0 us
  local copies, waits for them, and re-layouts: 1.96 us -> 10.5 us
    pallas_call x0 -> x2, Pallas kernels: none -> 34.9 us  [group_terms_kernel(): pl.pallas_call(terms_kernel, out_shape=jax.ShapeDtypeStruct((feat_rows, u...]
    dot_general x2 -> x0, matrix products: 15.7 us -> none  [terms_of(): lax.dot_general(y_hat, activations, (((0,), (0,)), ((), ())), preferred_e...]
    convert_element_type x4 -> x0, other arithmetic: 14.8 us -> none  [the longest x2 14.7 us: group_terms(): return values.reshape(feat_rows, unit_cols).astype(jnp.bfloat16)]
    unnamed x14 -> x22, local copies, waits for them, and re-layouts: 1.95 us -> 7.79 us
    reshape x0 -> x3, local copies, waits for them, and re-layouts: none -> 2.71 us  [group_terms_kernel(): feature_part.reshape(feat_rows, 1)]
where the time goes in v9:
time: 229 us
  Pallas kernels  217 us (95%)
  local copies, waits for them, and re-layouts  10.5 us (5%)
    pallas_call x3, Pallas kernels, communicate(): pl.pallas_call(functools.partial(comm_kernel, chunk, do_reduce, do_gather...  178 us
    pallas_call x2, Pallas kernels, group_terms_kernel(): pl.pallas_call(terms_kernel, out_shape=jax.ShapeDtypeStruct((feat_rows, u...  34.9 us
    unnamed x22, local copies, waits for them, and re-layouts  7.79 us

profile of v9, /device:TPU:32, one launch (start us, length us, event | category | flops | bytes accessed | tf_op | source)
XLA Modules:
  0.0 228.5 jit_solution(10770298050593976927)
XLA Ops:
  0.0 0.0 copy-start.1
  0.0 4.0 %shard_map.55 = (bf16[96,2048]{1,0:T(8,128)(2,1)}, bf16[96,2048]{1,0:T(8,128)(2,1)}) custom-call(bf16[96,4096]{1,0:T(8,128)(2,1)} %grad_ref.1, f32[96,4096]{1,0:T(8,128)} %dither_ref.1), custom_call_target="tpu_custom_call" | custom-call | tf_op jit(solution)/shard_map/pallas_call | solution.py:284
  4.0 0.0 copy-start.7
  4.0 1.0 copy-done.7
  5.0 42.5 %shard_map.56.y_ref = bf16[768,2048]{1,0:T(8,128)(2,1)S(1)} custom-call(bf16[96,2048]{1,0:T(8,128)(2,1)S(1)} %copy-done.7), custom_call_target="tpu_custom_call" | custom-call | tf_op jit(solution)/shard_map/pallas_call | solution.py:258
  47.6 0.0 copy-start
  47.6 1.7 copy-done
  49.3 0.0 copy-done.10
  49.3 1.3 copy.9.feature_ref
  50.6 0.0 copy-done.1
  50.7 0.0 copy-done.9
  50.7 1.2 copy-done.2
  51.9 17.5 %shard_map.57 = bf16[2048,1792]{1,0:T(8,128)(2,1)} custom-call(bf16[768,2048]{1,0:T(8,128)(2,1)} %copy-done, bf16[768,1792]{1,0:T(8,128)(2,1)S(1)} %copy-done.1, f32[2048,1]{1,0:T(8,128)S(1)} %copy-done.2, f32[1,1792]{1,0:T(1,128)S(1)} %copy-done.9), custom_call_target="tpu_custom_call" | custom-call | tf_op jit(solution)/shard_map/pallas_call | solution.py:310
  69.3 0.0 copy-done.8
  69.3 72.0 %shard_map.58 = (f32[128,1792]{1,0:T(8,128)S(1)}, bf16[768,2048]{1,0:T(8,128)(2,1)S(1)}) custom-call(bf16[4,4,128,1792]{3,2,1,0:T(8,128)(2,1)} %bitcast.9, bf16[96,2048]{1,0:T(8,128)(2,1)S(1)} %copy-done.8), custom_call_target="tpu_custom_call" | custom-call | tf_op jit(solution)/shard_map/pallas_call | solution.py:258
  141.4 0.0 copy-start.4
  141.4 1.7 copy-done.4
  143.1 0.9 copy-done.5
  144.0 1.3 copy.10.feature_ref
  145.3 1.2 copy-done.3
  146.6 17.4 %shard_map.59 = bf16[2048,1792]{1,0:T(8,128)(2,1)} custom-call(bf16[768,2048]{1,0:T(8,128)(2,1)} %copy-done.4, bf16[768,1792]{1,0:T(8,128)(2,1)S(1)} %copy-done.1, f32[2048,1]{1,0:T(8,128)S(1)} %copy-done.3, f32[1,1792]{1,0:T(1,128)S(1)} %copy-done.9), custom_call_target="tpu_custom_call" | custom-call | tf_op jit(solution)/shard_map/pallas_call | solution.py:310
  164.0 63.5 %shard_map.60 = f32[128,1792]{1,0:T(8,128)S(1)} custom-call(bf16[4,4,128,1792]{3,2,1,0:T(8,128)(2,1)} %bitcast.10), custom_call_target="tpu_custom_call" | custom-call | tf_op jit(solution)/shard_map/pallas_call | solution.py:258
  227.5 0.0 copy-done.6
  227.5 1.0 broadcast_select_fusion
  (8 shorter events, 0.0 us)
Async XLA Ops:
  0.0 50.7 %copy-start.1 = (bf16[768,1792]{1,0:T(8,128)(2,1)S(1)}, bf16[768,1792]{1,0:T(8,128)(2,1)}, u32[]{:S(2)}) copy-start(bf16[768,1792]{1,0:T(8,128)(2,1)} %act_ref.3) | copy-start | bytes 8257540
  4.0 1.0 copy-start.7
  5.0 44.2 %copy-start.10 = (f32[1,4096]{1,0:T(1,128)S(1)}, f32[1,4096]{1,0:T(1,128)}, u32[]{:S(2)}) copy-start(f32[1,4096]{1,0:T(1,128)} %param.9) | copy-start | bytes 49156
  5.0 45.6 %copy-start.9 = (f32[1,1792]{1,0:T(1,128)S(1)}, f32[1,1792]{1,0:T(1,128)}, u32[]{:S(2)}) copy-start(f32[1,1792]{1,0:T(1,128)} %hidden_ref.3) | copy-start | bytes 21508
  47.6 1.7 copy-start
  50.7 1.2 copy-start.2
  51.9 17.5 %copy-start.8 = (bf16[96,2048]{1,0:T(8,128)(2,1)S(1)}, bf16[96,2048]{1,0:T(8,128)(2,1)}, u32[]{:S(2)}) copy-start(bf16[96,2048]{1,0:T(8,128)(2,1)} %get-tuple-element.10.refs_1_) | copy-start | bytes 1179652
  141.4 1.7 copy-start.4
  143.1 0.9 copy-start.5
  145.3 1.2 copy-start.3
  164.0 63.5 %copy-start.6 = (f32[128,1792]{1,0:T(8,128)S(1)}, f32[128,1792]{1,0:T(8,128)}, u32[]{:S(2)}) copy-start(f32[128,1792]{1,0:T(8,128)} %copy-done.5) | copy-start | bytes 2752516

commit v10 on v9

--- a/solution.py
+++ b/solution.py
@@ -290,9 +290,7 @@
 
 
 def terms_kernel(y_ref, act_ref, feature_ref, hidden_ref, out_ref):
-    partial_value = lax.dot_general(
-        y_ref[...], act_ref[...], (((0,), (0,)), ((), ())), preferred_element_type=jnp.float32
-    )
+    partial_value = jnp.dot(y_ref[...], act_ref[...], preferred_element_type=jnp.float32)
     feat_rows, unit_cols = partial_value.shape
     block_count = feat_rows // BLOCK
     blocks = partial_value.reshape(block_count, BLOCK, unit_cols)
@@ -312,14 +310,14 @@
         out_shape=jax.ShapeDtypeStruct((feat_rows, unit_cols), jnp.bfloat16),
         grid=(unit_cols // tile,),
         in_specs=[
-            pl.BlockSpec((tokens, feat_rows), lambda j: (0, 0)),
+            pl.BlockSpec((feat_rows, tokens), lambda j: (0, 0)),
             pl.BlockSpec((tokens, tile), lambda j: (0, j)),
             pl.BlockSpec((feat_rows, 1), lambda j: (0, 0)),
             pl.BlockSpec((1, tile), lambda j: (0, j)),
         ],
         out_specs=pl.BlockSpec((feat_rows, tile), lambda j: (0, j)),
         compiler_params=pltpu.CompilerParams(vmem_limit_bytes=48 * 1024 * 1024),
-    )(y_hat, activations, feature_part.reshape(feat_rows, 1), hidden_part.reshape(1, unit_cols))
+    )(y_hat.T, activations, feature_part.reshape(feat_rows, 1), hidden_part.reshape(1, unit_cols))
 
 
 def per_device(grad_out, activations, grad_dither, hidden_dither, feature_dither):

time: 229 us -> 231 us (level)
  local copies, waits for them, and re-layouts: 10.5 us -> 15.9 us
  Pallas kernels: 217 us -> 214 us
    pallas_call x0 -> x2, local copies, waits for them, and re-layouts: none -> 7.65 us  [communicate(): pl.pallas_call(functools.partial(comm_kernel, chunk, do_reduce, do_gather...]
    unnamed x22 -> x20, local copies, waits for them, and re-layouts: 7.79 us -> 6.56 us
where the time goes in v10:
time: 231 us
  Pallas kernels  214 us (93%)
  local copies, waits for them, and re-layouts  15.9 us (7%)
    pallas_call x3, Pallas kernels, communicate(): pl.pallas_call(functools.partial(comm_kernel, chunk, do_reduce, do_gather...  177 us
    pallas_call x2, Pallas kernels, group_terms_kernel(): pl.pallas_call(terms_kernel, out_shape=jax.ShapeDtypeStruct((feat_rows, u...  32.6 us
    pallas_call x2, local copies, waits for them, and re-layouts, communicate(): pl.pallas_call(functools.partial(comm_kernel, chunk, do_reduce, do_gather...  7.65 us
    unnamed x20, local copies, waits for them, and re-layouts  6.56 us

profile of v10, /device:TPU:32, one launch (start us, length us, event | category | flops | bytes accessed | tf_op | source)
XLA Modules:
  0.0 230.6 jit_solution(1291727997316236856)
XLA Ops:
  0.0 3.9 %shard_map.55 = (bf16[96,2048]{1,0:T(8,128)(2,1)}, bf16[96,2048]{1,0:T(8,128)(2,1)}) custom-call(bf16[96,4096]{1,0:T(8,128)(2,1)} %grad_ref.1, f32[96,4096]{1,0:T(8,128)} %dither_ref.1), custom_call_target="tpu_custom_call" | custom-call | tf_op jit(solution)/shard_map/pallas_call | solution.py:284
  3.9 1.0 copy-done.6
  4.9 42.5 %shard_map.56 = bf16[768,2048]{1,0:T(8,128)(2,1)S(1)} custom-call(bf16[96,2048]{1,0:T(8,128)(2,1)S(1)} %copy-done.6), custom_call_target="tpu_custom_call" | custom-call | tf_op jit(solution)/shard_map/pallas_call | solution.py:258
  47.4 0.0 copy-start.9
  47.4 0.0 copy-start.8
  47.4 2.8 %copy.13 = bf16[768,2048]{0,1:T(8,128)(2,1)} copy(bf16[768,2048]{1,0:T(8,128)(2,1)S(1)} %shard_map.56) | data formatting | bytes 6291456 | tf_op jit(solution)/shard_map/pallas_call | solution.py:258
  50.3 0.0 copy-done.9
  50.3 0.4 copy.14.feature_ref
  50.7 0.0 copy-done.8
  50.7 0.0 copy-start
  50.7 1.8 copy-done
  52.5 16.3 %shard_map.57 = bf16[2048,1792]{1,0:T(8,128)(2,1)} custom-call(bf16[2048,768]{1,0:T(8,128)(2,1)} %bitcast.13, bf16[768,1792]{1,0:T(8,128)(2,1)S(1)} %copy-done, f32[2048,1]{1,0:T(8,128)S(1)} %copy.14.feature_ref, f32[1,1792]{1,0:T(1,128)S(1)} %copy-done.8), custom_call_target="tpu_custom_call" | custom-call | tf_op jit(solution)/shard_map/pallas_call | solution.py:308
  68.8 0.0 copy-done.7
  68.8 72.0 %shard_map.58 = (f32[128,1792]{1,0:T(8,128)S(1)}, bf16[768,2048]{1,0:T(8,128)(2,1)S(1)}) custom-call(bf16[4,4,128,1792]{3,2,1,0:T(8,128)(2,1)} %bitcast.11, bf16[96,2048]{1,0:T(8,128)(2,1)S(1)} %copy-done.7), custom_call_target="tpu_custom_call" | custom-call | tf_op jit(solution)/shard_map/pallas_call | solution.py:258
  140.8 1.6 copy-done.3
  142.4 0.9 copy-done.4
  143.3 4.8 %copy.15 = bf16[768,2048]{0,1:T(8,128)(2,1)} copy(bf16[768,2048]{1,0:T(8,128)(2,1)} %copy-done.3) | data formatting | bytes 6291456 | tf_op jit(solution)/shard_map/pallas_call | solution.py:258
  148.1 1.3 copy.16.feature_ref
  149.5 0.0 copy-done.1
  149.5 1.2 copy-done.2
  150.7 16.3 %shard_map.59 = bf16[2048,1792]{1,0:T(8,128)(2,1)} custom-call(bf16[2048,768]{1,0:T(8,128)(2,1)} %bitcast.14, bf16[768,1792]{1,0:T(8,128)(2,1)S(1)} %copy-done.1, f32[2048,1]{1,0:T(8,128)S(1)} %copy-done.2, f32[1,1792]{1,0:T(1,128)S(1)} %copy-done.8), custom_call_target="tpu_custom_call" | custom-call | tf_op jit(solution)/shard_map/pallas_call | solution.py:308
  167.0 62.5 %shard_map.60 = f32[128,1792]{1,0:T(8,128)S(1)} custom-call(bf16[4,4,128,1792]{3,2,1,0:T(8,128)(2,1)} %bitcast.12), custom_call_target="tpu_custom_call" | custom-call | tf_op jit(solution)/shard_map/pallas_call | solution.py:258
  229.5 0.0 copy-done.5
  229.5 1.0 broadcast_select_fusion
  (8 shorter events, 0.0 us)
Async XLA Ops:
  3.9 1.0 copy-start.6
  47.4 2.9 %copy-start.9 = (f32[1,4096]{1,0:T(1,128)S(1)}, f32[1,4096]{1,0:T(1,128)}, u32[]{:S(2)}) copy-start(f32[1,4096]{1,0:T(1,128)} %param.9) | copy-start | bytes 49156
  47.4 3.3 %copy-start.8 = (f32[1,1792]{1,0:T(1,128)S(1)}, f32[1,1792]{1,0:T(1,128)}, u32[]{:S(2)}) copy-start(f32[1,1792]{1,0:T(1,128)} %hidden_ref.3) | copy-start | bytes 21508
  50.7 1.8 copy-start
  52.5 16.3 %copy-start.7 = (bf16[96,2048]{1,0:T(8,128)(2,1)S(1)}, bf16[96,2048]{1,0:T(8,128)(2,1)}, u32[]{:S(2)}) copy-start(bf16[96,2048]{1,0:T(8,128)(2,1)} %get-tuple-element.10.refs_1_) | copy-start | bytes 1179652
  140.8 1.6 copy-start.3
  142.4 0.9 copy-start.4
  143.3 6.2 %copy-start.1 = (bf16[768,1792]{1,0:T(8,128)(2,1)S(1)}, bf16[768,1792]{1,0:T(8,128)(2,1)}, u32[]{:S(2)}) copy-start(bf16[768,1792]{1,0:T(8,128)(2,1)} %act_ref.3) | copy-start | bytes 8257540
  149.5 1.2 copy-start.2
  167.0 62.5 %copy-start.5 = (f32[128,1792]{1,0:T(8,128)S(1)}, f32[128,1792]{1,0:T(8,128)}, u32[]{:S(2)}) copy-start(f32[128,1792]{1,0:T(8,128)} %copy-done.4) | copy-start | bytes 2752516

commit v11 on v8

--- a/solution.py
+++ b/solution.py
@@ -298,10 +298,14 @@
     half = feat_width // 2
 
     def terms_of(y_hat, part):
-        partial_value = lax.dot_general(
-            y_hat, activations, (((0,), (0,)), ((), ())), preferred_element_type=jnp.float32
-        )
-        terms = group_terms(partial_value, feature_noise[part * half:(part + 1) * half], hidden_noise)
+        pieces = []
+        width = activations.shape[1] // 2
+        for cols in (slice(0, width), slice(width, 2 * width)):
+            partial_value = lax.dot_general(
+                y_hat, activations[:, cols], (((0,), (0,)), ((), ())), preferred_element_type=jnp.float32
+            )
+            pieces.append(group_terms(partial_value, feature_noise[part * half:(part + 1) * half], hidden_noise[cols]))
+        terms = jnp.concatenate(pieces, axis=1)
         return terms.reshape(RING, RING, BLOCK, terms.shape[1])
 
     (first_y,) = communicate(0, None, first_local, collective_id=1)

time: 216 us -> 221 us (1.023)
  other arithmetic: 17 us -> 23.1 us
    concatenate x0 -> x2, other arithmetic: none -> 12.6 us  [terms_of(): terms = jnp.concatenate(pieces, axis=1)]
    convert_element_type x2, other arithmetic: 14.7 us -> 9.42 us  [group_terms(): return values.reshape(feat_rows, unit_cols).astype(jnp.bfloat16)]
    dot_general x2 -> x4, matrix products: 15.7 us -> 15.9 us  [terms_of(): lax.dot_general(y_hat, activations[:, cols], (((0,), (0,)), ((), ())), pr...]
where the time goes in v11:
time: 221 us
  Pallas kernels  180 us (81%)
  other arithmetic  23.1 us (10%)
  matrix products  15.9 us (7%)
    pallas_call x3, Pallas kernels, communicate(): pl.pallas_call(functools.partial(comm_kernel, chunk, do_reduce, do_gather...  177 us
    dot_general x4, matrix products, terms_of(): lax.dot_general(y_hat, activations[:, cols], (((0,), (0,)), ((), ())), pr...  15.9 us
    concatenate x2, other arithmetic, terms_of(): terms = jnp.concatenate(pieces, axis=1)  12.6 us
    convert_element_type x2, other arithmetic, group_terms(): return values.reshape(feat_rows, unit_cols).astype(jnp.bfloat16)  9.42 us

profile of v11, /device:TPU:32, one launch (start us, length us, event | category | flops | bytes accessed | tf_op | source)
XLA Modules:
  0.0 220.6 jit_solution(7445881732574532311)
XLA Ops:
  0.0 3.3 %shard_map.55 = (bf16[96,2048]{1,0:T(8,128)(2,1)}, bf16[96,2048]{1,0:T(8,128)(2,1)}) custom-call(bf16[96,4096]{1,0:T(8,128)(2,1)} %grad_ref.1, f32[96,4096]{1,0:T(8,128)} %dither_ref.1), custom_call_target="tpu_custom_call" | custom-call | tf_op jit(solution)/shard_map/pallas_call | solution.py:284
  3.3 1.0 copy-done
  4.3 42.5 %shard_map.56 = bf16[768,2048]{1,0:T(8,128)(2,1)S(1)} custom-call(bf16[96,2048]{1,0:T(8,128)(2,1)S(1)} %copy-done), custom_call_target="tpu_custom_call" | custom-call | tf_op jit(solution)/shard_map/pallas_call | solution.py:258
  46.8 0.0 copy-start.2
  46.8 0.0 copy-start.3
  46.8 0.0 copy-start.4
  46.8 5.1 %bitcast_reduce_fusion.3 = (f32[16,896]{1,0:T(8,128)S(1)}, f32[2048,896]{1,0:T(8,128)S(1)}) fusion(bf16[768,2048]{1,0:T(8,128)(2,1)S(1)} %shard_map.56, bf16[768,1792]{1,0:T(8,128)(2,1)} %param.6), kind=kOutput, calls=%fused_computation.25 | convolution fusion | flops 2822227968 | bytes 11919360 | tf_op jit(solution)/shard_map/dot_general | solution.py:304
  51.9 0.0 copy-done.2
  52.0 0.0 copy-done.3
  52.0 0.0 copy-done.4
  52.0 3.6 %bitcast_reduce_fusion.2 = (f32[16,896]{1,0:T(8,128)S(1)}, f32[2048,896]{1,0:T(8,128)S(1)}) fusion(bf16[768,2048]{1,0:T(8,128)(2,1)S(1)} %shard_map.56, bf16[768,1792]{1,0:T(8,128)(2,1)S(1)} %copy-done.4), kind=kOutput, calls=%fused_computation.24 | convolution fusion | flops 2822227968 | bytes 11919360 | tf_op jit(solution)/shard_map/dot_general | solution.py:304
  55.6 4.4 %fusion.12 = (bf16[2048,896]{1,0:T(8,128)(2,1)S(1)}, bf16[2048,896]{1,0:T(8,128)(2,1)}) fusion(f32[2048,896]{1,0:T(8,128)S(1)} %get-tuple-element.22, f32[2048]{0:T(1024)S(1)} %bitcast.78, f32[896]{0:T(1024)S(1)} %get-tuple-element.13, f32[16,896]{1,0:T(8,128)S(1)} %get-tuple-element.29, f32[896]{0:T(1024)S(1)} %get-tuple-element.14, ...), kind=kLoop, calls=%fused_computation.26 | loop fusion | flops 22020096 | bytes 22150144 | tf_op jit(solution)/shard_map/convert_element_type | solution.py:31
  60.0 5.8 %pad_maximum_fusion.refs_0_ = bf16[4,4,128,1792]{3,2,1,0:T(8,128)(2,1)} fusion(bf16[4,4,128,896]{3,2,1,0:T(8,128)(2,1)} %bitcast.76, bf16[4,4,128,896]{3,2,1,0:T(8,128)(2,1)S(1)} %bitcast.75), kind=kLoop, calls=%fused_computation.20 | loop fusion | flops 14680064 | bytes 14680064 | tf_op jit(solution)/shard_map/concatenate | solution.py:308
  65.8 0.0 copy-done.1
  65.8 72.2 %shard_map.57 = (f32[128,1792]{1,0:T(8,128)S(1)}, bf16[768,2048]{1,0:T(8,128)(2,1)S(1)}) custom-call(bf16[4,4,128,1792]{3,2,1,0:T(8,128)(2,1)} %pad_maximum_fusion.refs_0_, bf16[96,2048]{1,0:T(8,128)(2,1)S(1)} %copy-done.1), custom_call_target="tpu_custom_call" | custom-call | tf_op jit(solution)/shard_map/pallas_call | solution.py:258
  138.0 0.0 copy-done.5
  138.0 0.0 copy-start.6
  138.0 3.6 %bitcast_reduce_fusion.1 = (f32[16,896]{1,0:T(8,128)S(1)}, f32[2048,896]{1,0:T(8,128)S(1)}) fusion(bf16[768,2048]{1,0:T(8,128)(2,1)S(1)} %get-tuple-element.12, bf16[768,1792]{1,0:T(8,128)(2,1)S(1)} %copy-done.5), kind=kOutput, calls=%fused_computation.23 | convolution fusion | flops 2822227968 | bytes 11919360 | tf_op jit(solution)/shard_map/dot_general | solution.py:304
  141.7 0.0 copy-done.6
  141.7 3.6 %bitcast_reduce_fusion = (f32[16,896]{1,0:T(8,128)S(1)}, f32[2048,896]{1,0:T(8,128)S(1)}) fusion(bf16[768,2048]{1,0:T(8,128)(2,1)S(1)} %get-tuple-element.12, bf16[768,1792]{1,0:T(8,128)(2,1)S(1)} %copy-done.6), kind=kOutput, calls=%fused_computation.22 | convolution fusion | flops 2822227968 | bytes 11919360 | tf_op jit(solution)/shard_map/dot_general | solution.py:304
  145.3 5.0 %fusion.14 = (bf16[2048,896]{1,0:T(8,128)(2,1)}, bf16[2048,896]{1,0:T(8,128)(2,1)}) fusion(f32[2048,896]{1,0:T(8,128)S(1)} %get-tuple-element.26, f32[2048]{0:T(1024)S(1)} %bitcast.77, f32[16,896]{1,0:T(8,128)S(1)} %fusion.26, f32[896]{0:T(1024)S(1)} %get-tuple-element.13, f32[896]{0:T(1024)S(1)} %get-tuple-element.14, ...), kind=kLoop, calls=%fused_computation.28 | loop fusion | flops 22020096 | bytes 22150144 | tf_op jit(solution)/shard_map/convert_element_type | solution.py:31
  150.3 6.8 %pad_maximum_fusion.1.refs_0_ = bf16[4,4,128,1792]{3,2,1,0:T(8,128)(2,1)} fusion(bf16[4,4,128,896]{3,2,1,0:T(8,128)(2,1)} %bitcast.74, bf16[4,4,128,896]{3,2,1,0:T(8,128)(2,1)} %bitcast.73), kind=kLoop, calls=%fused_computation.21 | loop fusion | flops 14680064 | bytes 14680064 | tf_op jit(solution)/shard_map/concatenate | solution.py:308
  157.1 62.4 %shard_map.58 = f32[128,1792]{1,0:T(8,128)S(1)} custom-call(bf16[4,4,128,1792]{3,2,1,0:T(8,128)(2,1)} %pad_maximum_fusion.1.refs_0_), custom_call_target="tpu_custom_call" | custom-call | tf_op jit(solution)/shard_map/pallas_call | solution.py:258
  219.6 1.0 broadcast_select_fusion
  (8 shorter events, 0.1 us)
Async XLA Ops:
  3.3 1.0 copy-start
  46.8 5.2 %copy-start.2 = (f32[1,4096]{1,0:T(1,128)S(1)}, f32[1,4096]{1,0:T(1,128)}, u32[]{:S(2)}) copy-start(f32[1,4096]{1,0:T(1,128)} %param.9) | copy-start | bytes 49156
  46.8 5.2 %copy-start.3 = (f32[1,1792]{1,0:T(1,128)S(1)}, f32[1,1792]{1,0:T(1,128)}, u32[]{:S(2)}) copy-start(f32[1,1792]{1,0:T(1,128)} %param.8) | copy-start | bytes 21508
  46.8 5.2 %copy-start.4 = (bf16[768,1792]{1,0:T(8,128)(2,1)S(1)}, bf16[768,1792]{1,0:T(8,128)(2,1)}, u32[]{:S(2)}) copy-start(bf16[768,1792]{1,0:T(8,128)(2,1)} %param.6) | copy-start | bytes 8257540
  60.0 5.8 %copy-start.1 = (bf16[96,2048]{1,0:T(8,128)(2,1)S(1)}, bf16[96,2048]{1,0:T(8,128)(2,1)}, u32[]{:S(2)}) copy-start(bf16[96,2048]{1,0:T(8,128)(2,1)} %get-tuple-element.10.refs_1_) | copy-start | bytes 1179652
  65.8 72.2 %copy-start.5 = (bf16[768,1792]{1,0:T(8,128)(2,1)S(1)}, bf16[768,1792]{1,0:T(8,128)(2,1)}, u32[]{:S(2)}) copy-start(bf16[768,1792]{1,0:T(8,128)(2,1)} %param.6) | copy-start | bytes 8257540
  138.0 3.7 %copy-start.6 = (bf16[768,1792]{1,0:T(8,128)(2,1)S(1)}, bf16[768,1792]{1,0:T(8,128)(2,1)}, u32[]{:S(2)}) copy-start(bf16[768,1792]{1,0:T(8,128)(2,1)} %param.6) | copy-start | bytes 8257540

commit v12 on v11

--- a/solution.py
+++ b/solution.py
@@ -55,12 +55,12 @@
         device_id=peer, device_id_type=MESH)
 
 
-def reduce_steps(chunk, terms_ref, out_ref, recv1, send1, res1, recv2, send2, res2, recvz, sendz,
+def reduce_steps(chunk, first_ref, second_ref, out_ref, recv1, send1, res1, recv2, send2, res2, recvz, sendz,
                  ss1, sr1, ss2, sr2, ssz, srz):
     dp = lax.axis_index("dp")
     y, x, z = dp // 8, (dp // 2) % 4, dp % 2
-    rows, cols = terms_ref.shape[2], terms_ref.shape[3]
-    half, width = rows // 2, cols // 2
+    rows, width = first_ref.shape[2], first_ref.shape[3]
+    half = rows // 2
     x_up, x_dn = dp_at(y, (x + 1) % RING, z), dp_at(y, (x + RING - 1) % RING, z)
     y_up, y_dn = dp_at((y + 1) % RING, x, z), dp_at((y + RING - 1) % RING, x, z)
     first = [
@@ -71,10 +71,10 @@
     ]
 
     def local1(k, index):
-        _, _, _, r0, c0, over_x = first[k]
+        _, _, _, r0, _, over_x = first[k]
         if over_x:
-            return terms_ref.at[:, index, pl.ds(r0, half), pl.ds(c0, width)]
-        return terms_ref.at[index, :, pl.ds(r0, half), pl.ds(c0, width)]
+            return first_ref.at[:, index, pl.ds(r0, half), :]
+        return second_ref.at[index, :, pl.ds(r0, half), :]
 
     pending = []
     copies = [None] * 4
@@ -183,7 +183,7 @@
 
 def comm_kernel(chunk, do_reduce, do_gather, *refs):
     refs = list(refs)
-    terms_ref = refs.pop(0) if do_reduce else None
+    terms_refs = [refs.pop(0), refs.pop(0)] if do_reduce else None
     local_ref = refs.pop(0) if do_gather else None
     out_ref = refs.pop(0) if do_reduce else None
     gathered_ref = refs.pop(0) if do_gather else None
@@ -211,7 +211,7 @@
 
     runs = []
     if do_reduce:
-        runs.append(reduce_steps(chunk, terms_ref, out_ref, *reduce_scratch))
+        runs.append(reduce_steps(chunk, *terms_refs, out_ref, *reduce_scratch))
     if do_gather:
         runs.append(gather_steps(local_ref, gathered_ref, *gather_scratch))
     pattern = [0, 1, 1] if len(runs) == 2 else [0]
@@ -230,10 +230,10 @@
     do_reduce, do_gather = terms is not None, local is not None
     args, outs, scratch = [], [], []
     if do_reduce:
-        rows, cols = terms.shape[2], terms.shape[3]
-        half, width = rows // 2, cols // 2
-        args.append(terms)
-        outs.append(jax.ShapeDtypeStruct((rows, cols), jnp.float32))
+        rows, width = terms[0].shape[2], terms[0].shape[3]
+        half = rows // 2
+        args.extend(terms)
+        outs.append(jax.ShapeDtypeStruct((rows, 2 * width), jnp.float32))
         scratch += [
             pltpu.VMEM((4, RING - 1, RING, half, width), jnp.bfloat16),
             pltpu.VMEM((4, RING - 2, RING, half, width), jnp.bfloat16),
@@ -305,8 +305,7 @@
                 y_hat, activations[:, cols], (((0,), (0,)), ((), ())), preferred_element_type=jnp.float32
             )
             pieces.append(group_terms(partial_value, feature_noise[part * half:(part + 1) * half], hidden_noise[cols]))
-        terms = jnp.concatenate(pieces, axis=1)
-        return terms.reshape(RING, RING, BLOCK, terms.shape[1])
+        return tuple(piece.reshape(RING, RING, BLOCK, piece.shape[1]) for piece in pieces)
 
     (first_y,) = communicate(0, None, first_local, collective_id=1)
     first_out, second_y = communicate(0, terms_of(first_y, 0), second_local, collective_id=2)

time: 221 us -> 207 us (0.937)
  other arithmetic: 23.1 us -> 10.5 us
    concatenate x2 -> x0, other arithmetic: 12.6 us -> none  [terms_of(): terms = jnp.concatenate(pieces, axis=1)]
where the time goes in v12:
time: 207 us
  Pallas kernels  179 us (86%)
  matrix products  15.8 us (8%)
  other arithmetic  10.5 us (5%)
    pallas_call x3, Pallas kernels, communicate(): pl.pallas_call(functools.partial(comm_kernel, chunk, do_reduce, do_gather...  176 us
    dot_general x4, matrix products, terms_of(): lax.dot_general(y_hat, activations[:, cols], (((0,), (0,)), ((), ())), pr...  15.8 us
    convert_element_type x2, other arithmetic, group_terms(): return values.reshape(feat_rows, unit_cols).astype(jnp.bfloat16)  9.48 us

profile of v12, /device:TPU:32, one launch (start us, length us, event | category | flops | bytes accessed | tf_op | source)
XLA Modules:
  0.0 207.0 jit_solution(6460273560072757878)
XLA Ops:
  0.0 3.2 %shard_map.55 = (bf16[96,2048]{1,0:T(8,128)(2,1)}, bf16[96,2048]{1,0:T(8,128)(2,1)}) custom-call(bf16[96,4096]{1,0:T(8,128)(2,1)} %grad_ref.1, f32[96,4096]{1,0:T(8,128)} %dither_ref.1), custom_call_target="tpu_custom_call" | custom-call | tf_op jit(solution)/shard_map/pallas_call | solution.py:284
  3.2 0.0 copy-start
  3.3 1.0 copy-done
  4.2 42.5 %shard_map.56 = bf16[768,2048]{1,0:T(8,128)(2,1)S(1)} custom-call(bf16[96,2048]{1,0:T(8,128)(2,1)S(1)} %copy-done), custom_call_target="tpu_custom_call" | custom-call | tf_op jit(solution)/shard_map/pallas_call | solution.py:258
  46.8 0.0 copy-start.3
  46.8 0.0 copy-start.4
  46.8 5.1 %bitcast_reduce_fusion.2 = (f32[16,896]{1,0:T(8,128)S(1)}, f32[2048,896]{1,0:T(8,128)S(1)}) fusion(bf16[768,2048]{1,0:T(8,128)(2,1)S(1)} %shard_map.56, bf16[768,1792]{1,0:T(8,128)(2,1)} %param.6), kind=kOutput, calls=%fused_computation.22 | convolution fusion | flops 2822227968 | bytes 11919360 | tf_op jit(solution)/shard_map/dot_general | solution.py:304
  51.9 0.0 copy-done.3
  52.0 0.0 copy-done.4
  52.0 0.0 copy-start.2
  52.0 3.6 %bitcast_reduce_fusion.3 = (f32[16,896]{1,0:T(8,128)S(1)}, f32[2048,896]{1,0:T(8,128)S(1)}) fusion(bf16[768,2048]{1,0:T(8,128)(2,1)S(1)} %shard_map.56, bf16[768,1792]{1,0:T(8,128)(2,1)S(1)} %copy-done.4), kind=kOutput, calls=%fused_computation.23 | convolution fusion | flops 2822227968 | bytes 11919360 | tf_op jit(solution)/shard_map/dot_general | solution.py:304
  55.6 0.0 copy-done.2
  55.6 0.0 copy-start.1
  55.6 5.0 %fusion.13 = (bf16[2048,896]{1,0:T(8,128)(2,1)}, bf16[2048,896]{1,0:T(8,128)(2,1)}) fusion(f32[2048,896]{1,0:T(8,128)S(1)} %get-tuple-element.22, f32[896]{0:T(1024)S(1)} %get-tuple-element.13, f32[16,896]{1,0:T(8,128)S(1)} %get-tuple-element.30, f32[2048]{0:T(1024)S(1)} %bitcast.78, f32[896]{0:T(1024)S(1)} %get-tuple-element.14, ...), kind=kLoop, calls=%fused_computation.25 | loop fusion | flops 22020096 | bytes 22150144 | tf_op jit(solution)/shard_map/convert_element_type | solution.py:31
  60.6 0.0 copy-done.1
  60.6 72.1 %shard_map.57 = (f32[128,1792]{1,0:T(8,128)S(1)}, bf16[768,2048]{1,0:T(8,128)(2,1)S(1)}) custom-call(bf16[4,4,128,896]{3,2,1,0:T(8,128)(2,1)} %bitcast.75, bf16[4,4,128,896]{3,2,1,0:T(8,128)(2,1)} %bitcast.74, bf16[96,2048]{1,0:T(8,128)(2,1)S(1)} %copy-done.1), custom_call_target="tpu_custom_call" | custom-call | tf_op jit(solution)/shard_map/pallas_call | solution.py:258
  132.7 3.5 %bitcast_reduce_fusion = (f32[16,896]{1,0:T(8,128)S(1)}, f32[2048,896]{1,0:T(8,128)S(1)}) fusion(bf16[768,2048]{1,0:T(8,128)(2,1)S(1)} %get-tuple-element.12, bf16[768,1792]{1,0:T(8,128)(2,1)S(1)} %copy-done.4), kind=kOutput, calls=%fused_computation.20 | convolution fusion | flops 2822227968 | bytes 11919360 | tf_op jit(solution)/shard_map/dot_general | solution.py:304
  136.3 3.6 %bitcast_reduce_fusion.1 = (f32[16,896]{1,0:T(8,128)S(1)}, f32[2048,896]{1,0:T(8,128)S(1)}) fusion(bf16[768,2048]{1,0:T(8,128)(2,1)S(1)} %get-tuple-element.12, bf16[768,1792]{1,0:T(8,128)(2,1)S(1)} %copy-done.4), kind=kOutput, calls=%fused_computation.21 | convolution fusion | flops 2822227968 | bytes 11919360 | tf_op jit(solution)/shard_map/dot_general | solution.py:304
  139.9 4.5 %fusion.15 = (bf16[2048,896]{1,0:T(8,128)(2,1)}, bf16[2048,896]{1,0:T(8,128)(2,1)S(1)}) fusion(f32[2048,896]{1,0:T(8,128)S(1)} %get-tuple-element.26, f32[16,896]{1,0:T(8,128)S(1)} %fusion.27, f32[2048]{0:T(1024)S(1)} %bitcast.77, f32[896]{0:T(1024)S(1)} %get-tuple-element.13, f32[896]{0:T(1024)S(1)} %get-tuple-element.14, ...), kind=kLoop, calls=%fused_computation.27 | loop fusion | flops 22020096 | bytes 22150144 | tf_op jit(solution)/shard_map/convert_element_type | solution.py:31
  144.4 61.5 %shard_map.58 = f32[128,1792]{1,0:T(8,128)S(1)} custom-call(bf16[4,4,128,896]{3,2,1,0:T(8,128)(2,1)S(1)} %bitcast.73, bf16[4,4,128,896]{3,2,1,0:T(8,128)(2,1)} %bitcast.76), custom_call_target="tpu_custom_call" | custom-call | tf_op jit(solution)/shard_map/pallas_call | solution.py:258
  206.0 1.0 broadcast_select_fusion
  (5 shorter events, 0.1 us)
Async XLA Ops:
  3.2 1.0 copy-start
  46.8 5.1 %copy-start.3 = (f32[1,1792]{1,0:T(1,128)S(1)}, f32[1,1792]{1,0:T(1,128)}, u32[]{:S(2)}) copy-start(f32[1,1792]{1,0:T(1,128)} %param.8) | copy-start | bytes 21508
  46.8 5.2 %copy-start.4 = (bf16[768,1792]{1,0:T(8,128)(2,1)S(1)}, bf16[768,1792]{1,0:T(8,128)(2,1)}, u32[]{:S(2)}) copy-start(bf16[768,1792]{1,0:T(8,128)(2,1)} %param.6) | copy-start | bytes 8257540
  52.0 3.6 %copy-start.2 = (f32[1,4096]{1,0:T(1,128)S(1)}, f32[1,4096]{1,0:T(1,128)}, u32[]{:S(2)}) copy-start(f32[1,4096]{1,0:T(1,128)} %param.9) | copy-start | bytes 49156
  55.6 5.0 %copy-start.1 = (bf16[96,2048]{1,0:T(8,128)(2,1)S(1)}, bf16[96,2048]{1,0:T(8,128)(2,1)}, u32[]{:S(2)}) copy-start(bf16[96,2048]{1,0:T(8,128)(2,1)} %get-tuple-element.10.refs_2_) | copy-start | bytes 1179652

commit v13 on v12

--- a/solution.py
+++ b/solution.py
@@ -214,7 +214,7 @@
         runs.append(reduce_steps(chunk, *terms_refs, out_ref, *reduce_scratch))
     if do_gather:
         runs.append(gather_steps(local_ref, gathered_ref, *gather_scratch))
-    pattern = [0, 1, 1] if len(runs) == 2 else [0]
+    pattern = [0, 1] if len(runs) == 2 else [0]
     while runs:
         for which in pattern:
             if which < len(runs):

time: 207 us -> 209 us (level)
    pallas_call x3, Pallas kernels: 176 us -> 178 us  [communicate(): pl.pallas_call(functools.partial(comm_kernel, chunk, do_reduce, do_gather...]
where the time goes in v13:
time: 209 us
  Pallas kernels  181 us (87%)
  matrix products  15.8 us (8%)
  other arithmetic  10.1 us (5%)
    pallas_call x3, Pallas kernels, communicate(): pl.pallas_call(functools.partial(comm_kernel, chunk, do_reduce, do_gather...  178 us
    dot_general x4, matrix products, terms_of(): lax.dot_general(y_hat, activations[:, cols], (((0,), (0,)), ((), ())), pr...  15.8 us
    convert_element_type x2, other arithmetic, group_terms(): return values.reshape(feat_rows, unit_cols).astype(jnp.bfloat16)  9.08 us

profile of v13, /device:TPU:32, one launch (start us, length us, event | category | flops | bytes accessed | tf_op | source)
XLA Modules:
  0.0 208.7 jit_solution(10393390756235541813)
XLA Ops:
  0.0 3.2 %shard_map.55 = (bf16[96,2048]{1,0:T(8,128)(2,1)}, bf16[96,2048]{1,0:T(8,128)(2,1)}) custom-call(bf16[96,4096]{1,0:T(8,128)(2,1)} %grad_ref.1, f32[96,4096]{1,0:T(8,128)} %dither_ref.1), custom_call_target="tpu_custom_call" | custom-call | tf_op jit(solution)/shard_map/pallas_call | solution.py:284
  3.2 0.0 copy-start
  3.3 1.0 copy-done
  4.2 42.5 %shard_map.56 = bf16[768,2048]{1,0:T(8,128)(2,1)S(1)} custom-call(bf16[96,2048]{1,0:T(8,128)(2,1)S(1)} %copy-done), custom_call_target="tpu_custom_call" | custom-call | tf_op jit(solution)/shard_map/pallas_call | solution.py:258
  46.8 0.0 copy-start.3
  46.8 0.0 copy-start.4
  46.8 5.1 %bitcast_reduce_fusion.2 = (f32[16,896]{1,0:T(8,128)S(1)}, f32[2048,896]{1,0:T(8,128)S(1)}) fusion(bf16[768,2048]{1,0:T(8,128)(2,1)S(1)} %shard_map.56, bf16[768,1792]{1,0:T(8,128)(2,1)} %param.6), kind=kOutput, calls=%fused_computation.22 | convolution fusion | flops 2822227968 | bytes 11919360 | tf_op jit(solution)/shard_map/dot_general | solution.py:304
  51.9 0.0 copy-done.3
  52.0 0.0 copy-done.4
  52.0 0.0 copy-start.2
  52.0 3.6 %bitcast_reduce_fusion.3 = (f32[16,896]{1,0:T(8,128)S(1)}, f32[2048,896]{1,0:T(8,128)S(1)}) fusion(bf16[768,2048]{1,0:T(8,128)(2,1)S(1)} %shard_map.56, bf16[768,1792]{1,0:T(8,128)(2,1)S(1)} %copy-done.4), kind=kOutput, calls=%fused_computation.23 | convolution fusion | flops 2822227968 | bytes 11919360 | tf_op jit(solution)/shard_map/dot_general | solution.py:304
  55.6 0.0 copy-done.2
  55.6 0.0 copy-start.1
  55.6 4.8 %fusion.13 = (bf16[2048,896]{1,0:T(8,128)(2,1)}, bf16[2048,896]{1,0:T(8,128)(2,1)}) fusion(f32[2048,896]{1,0:T(8,128)S(1)} %get-tuple-element.22, f32[896]{0:T(1024)S(1)} %get-tuple-element.13, f32[16,896]{1,0:T(8,128)S(1)} %get-tuple-element.30, f32[2048]{0:T(1024)S(1)} %bitcast.78, f32[896]{0:T(1024)S(1)} %get-tuple-element.14, ...), kind=kLoop, calls=%fused_computation.25 | loop fusion | flops 22020096 | bytes 22150144 | tf_op jit(solution)/shard_map/convert_element_type | solution.py:31
  60.4 0.0 copy-done.1
  60.4 71.0 %shard_map.57 = (f32[128,1792]{1,0:T(8,128)S(1)}, bf16[768,2048]{1,0:T(8,128)(2,1)S(1)}) custom-call(bf16[4,4,128,896]{3,2,1,0:T(8,128)(2,1)} %bitcast.75, bf16[4,4,128,896]{3,2,1,0:T(8,128)(2,1)} %bitcast.74, bf16[96,2048]{1,0:T(8,128)(2,1)S(1)} %copy-done.1), custom_call_target="tpu_custom_call" | custom-call | tf_op jit(solution)/shard_map/pallas_call | solution.py:258
  131.5 3.5 %bitcast_reduce_fusion = (f32[16,896]{1,0:T(8,128)S(1)}, f32[2048,896]{1,0:T(8,128)S(1)}) fusion(bf16[768,2048]{1,0:T(8,128)(2,1)S(1)} %get-tuple-element.12, bf16[768,1792]{1,0:T(8,128)(2,1)S(1)} %copy-done.4), kind=kOutput, calls=%fused_computation.20 | convolution fusion | flops 2822227968 | bytes 11919360 | tf_op jit(solution)/shard_map/dot_general | solution.py:304
  135.0 3.6 %bitcast_reduce_fusion.1 = (f32[16,896]{1,0:T(8,128)S(1)}, f32[2048,896]{1,0:T(8,128)S(1)}) fusion(bf16[768,2048]{1,0:T(8,128)(2,1)S(1)} %get-tuple-element.12, bf16[768,1792]{1,0:T(8,128)(2,1)S(1)} %copy-done.4), kind=kOutput, calls=%fused_computation.21 | convolution fusion | flops 2822227968 | bytes 11919360 | tf_op jit(solution)/shard_map/dot_general | solution.py:304
  138.7 4.3 %fusion.15 = (bf16[2048,896]{1,0:T(8,128)(2,1)}, bf16[2048,896]{1,0:T(8,128)(2,1)S(1)}) fusion(f32[2048,896]{1,0:T(8,128)S(1)} %get-tuple-element.26, f32[16,896]{1,0:T(8,128)S(1)} %fusion.27, f32[2048]{0:T(1024)S(1)} %bitcast.77, f32[896]{0:T(1024)S(1)} %get-tuple-element.13, f32[896]{0:T(1024)S(1)} %get-tuple-element.14, ...), kind=kLoop, calls=%fused_computation.27 | loop fusion | flops 22020096 | bytes 22150144 | tf_op jit(solution)/shard_map/convert_element_type | solution.py:31
  143.0 64.7 %shard_map.58 = f32[128,1792]{1,0:T(8,128)S(1)} custom-call(bf16[4,4,128,896]{3,2,1,0:T(8,128)(2,1)S(1)} %bitcast.73, bf16[4,4,128,896]{3,2,1,0:T(8,128)(2,1)} %bitcast.76), custom_call_target="tpu_custom_call" | custom-call | tf_op jit(solution)/shard_map/pallas_call | solution.py:258
  207.7 1.0 broadcast_select_fusion
  (5 shorter events, 0.1 us)
Async XLA Ops:
  3.2 1.0 copy-start
  46.8 5.1 %copy-start.3 = (f32[1,1792]{1,0:T(1,128)S(1)}, f32[1,1792]{1,0:T(1,128)}, u32[]{:S(2)}) copy-start(f32[1,1792]{1,0:T(1,128)} %param.8) | copy-start | bytes 21508
  46.8 5.2 %copy-start.4 = (bf16[768,1792]{1,0:T(8,128)(2,1)S(1)}, bf16[768,1792]{1,0:T(8,128)(2,1)}, u32[]{:S(2)}) copy-start(bf16[768,1792]{1,0:T(8,128)(2,1)} %param.6) | copy-start | bytes 8257540
  52.0 3.6 %copy-start.2 = (f32[1,4096]{1,0:T(1,128)S(1)}, f32[1,4096]{1,0:T(1,128)}, u32[]{:S(2)}) copy-start(f32[1,4096]{1,0:T(1,128)} %param.9) | copy-start | bytes 49156
  55.6 4.8 %copy-start.1 = (bf16[96,2048]{1,0:T(8,128)(2,1)S(1)}, bf16[96,2048]{1,0:T(8,128)(2,1)}, u32[]{:S(2)}) copy-start(bf16[96,2048]{1,0:T(8,128)(2,1)} %get-tuple-element.10.refs_2_) | copy-start | bytes 1179652

commit v14 on v12

--- a/solution.py
+++ b/solution.py
@@ -55,7 +55,7 @@
         device_id=peer, device_id_type=MESH)
 
 
-def reduce_steps(chunk, first_ref, second_ref, out_ref, recv1, send1, res1, recv2, send2, res2, recvz, sendz,
+def reduce_steps(chunk, first_ref, second_ref, kept_ref, out_ref, recv1, send1, res1, recv2, send2, res2, recvz, sendz,
                  ss1, sr1, ss2, sr2, ssz, srz):
     dp = lax.axis_index("dp")
     y, x, z = dp // 8, (dp // 2) % 4, dp % 2
@@ -140,8 +140,11 @@
 
     @pl.when(z != chunk)
     def _():
-        for k, (r0, c0) in enumerate(corners):
-            out_ref[pl.ds(r0, half), pl.ds(c0, width)] = res2[k]
+        if kept_ref is None:
+            for k, (r0, c0) in enumerate(corners):
+                out_ref[pl.ds(r0, half), pl.ds(c0, width)] = res2[k]
+        else:
+            out_ref[...] = kept_ref[...]
         swap.wait_send()
 
     for copy in pending:
@@ -181,9 +184,10 @@
         copy.wait_send()
 
 
-def comm_kernel(chunk, do_reduce, do_gather, *refs):
+def comm_kernel(chunk, do_reduce, do_gather, do_keep, *refs):
     refs = list(refs)
     terms_refs = [refs.pop(0), refs.pop(0)] if do_reduce else None
+    kept_ref = refs.pop(0) if do_keep else None
     local_ref = refs.pop(0) if do_gather else None
     out_ref = refs.pop(0) if do_reduce else None
     gathered_ref = refs.pop(0) if do_gather else None
@@ -211,7 +215,7 @@
 
     runs = []
     if do_reduce:
-        runs.append(reduce_steps(chunk, *terms_refs, out_ref, *reduce_scratch))
+        runs.append(reduce_steps(chunk, *terms_refs, kept_ref, out_ref, *reduce_scratch))
     if do_gather:
         runs.append(gather_steps(local_ref, gathered_ref, *gather_scratch))
     pattern = [0, 1, 1] if len(runs) == 2 else [0]
@@ -226,13 +230,15 @@
                     break
 
 
-def communicate(chunk, terms=None, local=None, collective_id=0):
+def communicate(chunk, terms=None, local=None, collective_id=0, kept=None):
     do_reduce, do_gather = terms is not None, local is not None
     args, outs, scratch = [], [], []
     if do_reduce:
         rows, width = terms[0].shape[2], terms[0].shape[3]
         half = rows // 2
         args.extend(terms)
+        if kept is not None:
+            args.append(kept)
         outs.append(jax.ShapeDtypeStruct((rows, 2 * width), jnp.float32))
         scratch += [
             pltpu.VMEM((4, RING - 1, RING, half, width), jnp.bfloat16),
@@ -256,7 +262,7 @@
         outs.append(jax.ShapeDtypeStruct((n * local.shape[0], local.shape[1]), local.dtype))
         scratch += [pltpu.SemaphoreType.DMA((2, n - 1)), pltpu.SemaphoreType.DMA((2, n - 1))]
     return pl.pallas_call(
-        functools.partial(comm_kernel, chunk, do_reduce, do_gather),
+        functools.partial(comm_kernel, chunk, do_reduce, do_gather, kept is not None),
         out_shape=tuple(outs),
         in_specs=[pl.BlockSpec(memory_space=pltpu.VMEM)] * len(args),
         out_specs=tuple(pl.BlockSpec(memory_space=pltpu.VMEM) for _ in outs),
@@ -309,9 +315,8 @@
 
     (first_y,) = communicate(0, None, first_local, collective_id=1)
     first_out, second_y = communicate(0, terms_of(first_y, 0), second_local, collective_id=2)
-    (second_out,) = communicate(1, terms_of(second_y, 1), None, collective_id=0)
-    z = lax.axis_index("dp") % 2
-    return jnp.where(z == 0, first_out, second_out)
+    (result,) = communicate(1, terms_of(second_y, 1), None, collective_id=0, kept=first_out)
+    return result
 
 
 def solution(mesh):

time: 207 us -> 208 us (level)
  local copies, waits for them, and re-layouts: 1.06 us -> 3.47 us
where the time goes in v14:
time: 208 us
  Pallas kernels  179 us (86%)
  matrix products  15.9 us (8%)
  other arithmetic  9.4 us (5%)
  local copies, waits for them, and re-layouts  3.47 us (2%)
    pallas_call x3, Pallas kernels, communicate(): pl.pallas_call(functools.partial(comm_kernel, chunk, do_reduce, do_gather...  176 us
    dot_general x4, matrix products, terms_of(): lax.dot_general(y_hat, activations[:, cols], (((0,), (0,)), ((), ())), pr...  15.9 us
    convert_element_type x2, other arithmetic, group_terms(): return values.reshape(feat_rows, unit_cols).astype(jnp.bfloat16)  9.36 us

profile of v14, /device:TPU:32, one launch (start us, length us, event | category | flops | bytes accessed | tf_op | source)
XLA Modules:
  0.0 208.1 jit_solution(17696983317042437773)
XLA Ops:
  0.0 0.7 slice_reduce_fusion
  0.7 0.8 fusion.28
  1.5 3.3 %shard_map.55 = (bf16[96,2048]{1,0:T(8,128)(2,1)}, bf16[96,2048]{1,0:T(8,128)(2,1)}) custom-call(bf16[96,4096]{1,0:T(8,128)(2,1)} %grad_ref.1, f32[96,4096]{1,0:T(8,128)} %dither_ref.1), custom_call_target="tpu_custom_call" | custom-call | tf_op jit(solution)/shard_map/pallas_call | solution.py:290
  4.8 0.0 copy-start
  4.8 1.0 copy-done
  5.8 42.5 %shard_map.56 = bf16[768,2048]{1,0:T(8,128)(2,1)S(1)} custom-call(bf16[96,2048]{1,0:T(8,128)(2,1)S(1)} %copy-done), custom_call_target="tpu_custom_call" | custom-call | tf_op jit(solution)/shard_map/pallas_call | solution.py:264
  48.3 0.0 copy-start.2
  48.3 5.1 %bitcast_reduce_fusion.2 = (f32[16,896]{1,0:T(8,128)S(1)}, f32[2048,896]{1,0:T(8,128)S(1)}) fusion(bf16[768,2048]{1,0:T(8,128)(2,1)S(1)} %shard_map.56, bf16[768,1792]{1,0:T(8,128)(2,1)} %param.6), kind=kOutput, calls=%fused_computation.22 | convolution fusion | flops 2822227968 | bytes 11919360 | tf_op jit(solution)/shard_map/dot_general | solution.py:310
  53.5 0.0 copy-done.2
  53.5 3.6 %bitcast_reduce_fusion.3 = (f32[16,896]{1,0:T(8,128)S(1)}, f32[2048,896]{1,0:T(8,128)S(1)}) fusion(bf16[768,2048]{1,0:T(8,128)(2,1)S(1)} %shard_map.56, bf16[768,1792]{1,0:T(8,128)(2,1)S(1)} %copy-done.2), kind=kOutput, calls=%fused_computation.23 | convolution fusion | flops 2822227968 | bytes 11919360 | tf_op jit(solution)/shard_map/dot_general | solution.py:310
  57.1 0.0 copy-start.1
  57.1 5.0 %fusion.13 = (bf16[2048,896]{1,0:T(8,128)(2,1)}, bf16[2048,896]{1,0:T(8,128)(2,1)}) fusion(f32[2048,896]{1,0:T(8,128)S(1)} %get-tuple-element.22, f32[896]{0:T(1024)S(1)} %get-tuple-element.13, f32[16,896]{1,0:T(8,128)S(1)} %get-tuple-element.30, f32[2048]{0:T(1024)S(1)} %bitcast.78, f32[896]{0:T(1024)S(1)} %get-tuple-element.14, ...), kind=kLoop, calls=%fused_computation.25 | loop fusion | flops 22020096 | bytes 22150144 | tf_op jit(solution)/shard_map/convert_element_type | solution.py:31
  62.1 0.0 copy-done.1
  62.1 72.1 %shard_map.57 = (f32[128,1792]{1,0:T(8,128)S(1)}, bf16[768,2048]{1,0:T(8,128)(2,1)S(1)}) custom-call(bf16[4,4,128,896]{3,2,1,0:T(8,128)(2,1)} %bitcast.76, bf16[4,4,128,896]{3,2,1,0:T(8,128)(2,1)} %bitcast.75, bf16[96,2048]{1,0:T(8,128)(2,1)S(1)} %copy-done.1), custom_call_target="tpu_custom_call" | custom-call | tf_op jit(solution)/shard_map/pallas_call | solution.py:264
  134.1 3.6 %bitcast_reduce_fusion = (f32[16,896]{1,0:T(8,128)S(1)}, f32[2048,896]{1,0:T(8,128)S(1)}) fusion(bf16[768,2048]{1,0:T(8,128)(2,1)S(1)} %get-tuple-element.11, bf16[768,1792]{1,0:T(8,128)(2,1)S(1)} %copy-done.2), kind=kOutput, calls=%fused_computation.20 | convolution fusion | flops 2822227968 | bytes 11919360 | tf_op jit(solution)/shard_map/dot_general | solution.py:310
  137.8 3.5 %bitcast_reduce_fusion.1 = (f32[16,896]{1,0:T(8,128)S(1)}, f32[2048,896]{1,0:T(8,128)S(1)}) fusion(bf16[768,2048]{1,0:T(8,128)(2,1)S(1)} %get-tuple-element.11, bf16[768,1792]{1,0:T(8,128)(2,1)S(1)} %copy-done.2), kind=kOutput, calls=%fused_computation.21 | convolution fusion | flops 2822227968 | bytes 11919360 | tf_op jit(solution)/shard_map/dot_general | solution.py:310
  141.4 4.4 %fusion.15 = (bf16[2048,896]{1,0:T(8,128)(2,1)}, bf16[2048,896]{1,0:T(8,128)(2,1)S(1)}) fusion(f32[2048,896]{1,0:T(8,128)S(1)} %get-tuple-element.26, f32[16,896]{1,0:T(8,128)S(1)} %fusion.27, f32[2048]{0:T(1024)S(1)} %bitcast.77, f32[896]{0:T(1024)S(1)} %get-tuple-element.13, f32[896]{0:T(1024)S(1)} %get-tuple-element.14, ...), kind=kLoop, calls=%fused_computation.27 | loop fusion | flops 22020096 | bytes 22150144 | tf_op jit(solution)/shard_map/convert_element_type | solution.py:31
  145.8 61.4 %shard_map.58 = f32[128,1792]{1,0:T(8,128)S(1)} custom-call(bf16[4,4,128,896]{3,2,1,0:T(8,128)(2,1)S(1)} %bitcast.73, bf16[4,4,128,896]{3,2,1,0:T(8,128)(2,1)} %bitcast.74, f32[128,1792]{1,0:T(8,128)S(1)} %get-tuple-element.12.refs_2_), custom_call_target="tpu_custom_call" | custom-call | tf_op jit(solution)/shard_map/pallas_call | solution.py:264
  207.2 0.9 copy.7
  (3 shorter events, 0.0 us)
Async XLA Ops:
  4.8 1.0 copy-start
  48.3 5.2 %copy-start.2 = (bf16[768,1792]{1,0:T(8,128)(2,1)S(1)}, bf16[768,1792]{1,0:T(8,128)(2,1)}, u32[]{:S(2)}) copy-start(bf16[768,1792]{1,0:T(8,128)(2,1)} %param.6) | copy-start | bytes 8257540
  57.1 5.0 %copy-start.1 = (bf16[96,2048]{1,0:T(8,128)(2,1)S(1)}, bf16[96,2048]{1,0:T(8,128)(2,1)}, u32[]{:S(2)}) copy-start(bf16[96,2048]{1,0:T(8,128)(2,1)} %get-tuple-element.10.refs_2_) | copy-start | bytes 1179652

commit v15 on v14

--- a/solution.py
+++ b/solution.py
@@ -218,7 +218,7 @@
         runs.append(reduce_steps(chunk, *terms_refs, kept_ref, out_ref, *reduce_scratch))
     if do_gather:
         runs.append(gather_steps(local_ref, gathered_ref, *gather_scratch))
-    pattern = [0, 1, 1] if len(runs) == 2 else [0]
+    pattern = [0, 1] if len(runs) == 2 else [0]
     while runs:
         for which in pattern:
             if which < len(runs):

time: 208 us -> 211 us (1.014)
  Pallas kernels: 179 us -> 182 us
    pallas_call x3, Pallas kernels: 176 us -> 179 us  [communicate(): pl.pallas_call(functools.partial(comm_kernel, chunk, do_reduce, do_gather...]
where the time goes in v15:
time: 211 us; the launch traced here: 210 us
  Pallas kernels  182 us (86%)
  matrix products  15.9 us (8%)
  other arithmetic  9 us (4%)
  local copies, waits for them, and re-layouts  3.47 us (2%)
    pallas_call x3, Pallas kernels, communicate(): pl.pallas_call(functools.partial(comm_kernel, chunk, do_reduce, do_gather...  179 us
    dot_general x4, matrix products, terms_of(): lax.dot_general(y_hat, activations[:, cols], (((0,), (0,)), ((), ())), pr...  15.9 us
    convert_element_type x2, other arithmetic, group_terms(): return values.reshape(feat_rows, unit_cols).astype(jnp.bfloat16)  8.96 us

profile of v15, /device:TPU:32, one launch (start us, length us, event | category | flops | bytes accessed | tf_op | source)
XLA Modules:
  0.0 210.4 jit_solution(14293375053133252385)
XLA Ops:
  0.0 0.7 slice_reduce_fusion
  0.7 0.8 fusion.28
  1.5 3.3 %shard_map.55 = (bf16[96,2048]{1,0:T(8,128)(2,1)}, bf16[96,2048]{1,0:T(8,128)(2,1)}) custom-call(bf16[96,4096]{1,0:T(8,128)(2,1)} %grad_ref.1, f32[96,4096]{1,0:T(8,128)} %dither_ref.1), custom_call_target="tpu_custom_call" | custom-call | tf_op jit(solution)/shard_map/pallas_call | solution.py:290
  4.8 0.0 copy-start
  4.8 1.0 copy-done
  5.8 42.5 %shard_map.56 = bf16[768,2048]{1,0:T(8,128)(2,1)S(1)} custom-call(bf16[96,2048]{1,0:T(8,128)(2,1)S(1)} %copy-done), custom_call_target="tpu_custom_call" | custom-call | tf_op jit(solution)/shard_map/pallas_call | solution.py:264
  48.3 0.0 copy-start.2
  48.3 5.1 %bitcast_reduce_fusion.2 = (f32[16,896]{1,0:T(8,128)S(1)}, f32[2048,896]{1,0:T(8,128)S(1)}) fusion(bf16[768,2048]{1,0:T(8,128)(2,1)S(1)} %shard_map.56, bf16[768,1792]{1,0:T(8,128)(2,1)} %param.6), kind=kOutput, calls=%fused_computation.22 | convolution fusion | flops 2822227968 | bytes 11919360 | tf_op jit(solution)/shard_map/dot_general | solution.py:310
  53.5 0.0 copy-done.2
  53.5 3.6 %bitcast_reduce_fusion.3 = (f32[16,896]{1,0:T(8,128)S(1)}, f32[2048,896]{1,0:T(8,128)S(1)}) fusion(bf16[768,2048]{1,0:T(8,128)(2,1)S(1)} %shard_map.56, bf16[768,1792]{1,0:T(8,128)(2,1)S(1)} %copy-done.2), kind=kOutput, calls=%fused_computation.23 | convolution fusion | flops 2822227968 | bytes 11919360 | tf_op jit(solution)/shard_map/dot_general | solution.py:310
  57.1 0.0 copy-start.1
  57.1 4.8 %fusion.13 = (bf16[2048,896]{1,0:T(8,128)(2,1)}, bf16[2048,896]{1,0:T(8,128)(2,1)}) fusion(f32[2048,896]{1,0:T(8,128)S(1)} %get-tuple-element.22, f32[896]{0:T(1024)S(1)} %get-tuple-element.13, f32[16,896]{1,0:T(8,128)S(1)} %get-tuple-element.30, f32[2048]{0:T(1024)S(1)} %bitcast.78, f32[896]{0:T(1024)S(1)} %get-tuple-element.14, ...), kind=kLoop, calls=%fused_computation.25 | loop fusion | flops 22020096 | bytes 22150144 | tf_op jit(solution)/shard_map/convert_element_type | solution.py:31
  61.9 0.0 copy-done.1
  61.9 71.0 %shard_map.57 = (f32[128,1792]{1,0:T(8,128)S(1)}, bf16[768,2048]{1,0:T(8,128)(2,1)S(1)}) custom-call(bf16[4,4,128,896]{3,2,1,0:T(8,128)(2,1)} %bitcast.76, bf16[4,4,128,896]{3,2,1,0:T(8,128)(2,1)} %bitcast.75, bf16[96,2048]{1,0:T(8,128)(2,1)S(1)} %copy-done.1), custom_call_target="tpu_custom_call" | custom-call | tf_op jit(solution)/shard_map/pallas_call | solution.py:264
  132.9 3.6 %bitcast_reduce_fusion = (f32[16,896]{1,0:T(8,128)S(1)}, f32[2048,896]{1,0:T(8,128)S(1)}) fusion(bf16[768,2048]{1,0:T(8,128)(2,1)S(1)} %get-tuple-element.11, bf16[768,1792]{1,0:T(8,128)(2,1)S(1)} %copy-done.2), kind=kOutput, calls=%fused_computation.20 | convolution fusion | flops 2822227968 | bytes 11919360 | tf_op jit(solution)/shard_map/dot_general | solution.py:310
  136.6 3.5 %bitcast_reduce_fusion.1 = (f32[16,896]{1,0:T(8,128)S(1)}, f32[2048,896]{1,0:T(8,128)S(1)}) fusion(bf16[768,2048]{1,0:T(8,128)(2,1)S(1)} %get-tuple-element.11, bf16[768,1792]{1,0:T(8,128)(2,1)S(1)} %copy-done.2), kind=kOutput, calls=%fused_computation.21 | convolution fusion | flops 2822227968 | bytes 11919360 | tf_op jit(solution)/shard_map/dot_general | solution.py:310
  140.1 4.2 %fusion.15 = (bf16[2048,896]{1,0:T(8,128)(2,1)}, bf16[2048,896]{1,0:T(8,128)(2,1)S(1)}) fusion(f32[2048,896]{1,0:T(8,128)S(1)} %get-tuple-element.26, f32[16,896]{1,0:T(8,128)S(1)} %fusion.27, f32[2048]{0:T(1024)S(1)} %bitcast.77, f32[896]{0:T(1024)S(1)} %get-tuple-element.13, f32[896]{0:T(1024)S(1)} %get-tuple-element.14, ...), kind=kLoop, calls=%fused_computation.27 | loop fusion | flops 22020096 | bytes 22150144 | tf_op jit(solution)/shard_map/convert_element_type | solution.py:31
  144.3 65.1 %shard_map.58 = f32[128,1792]{1,0:T(8,128)S(1)} custom-call(bf16[4,4,128,896]{3,2,1,0:T(8,128)(2,1)S(1)} %bitcast.73, bf16[4,4,128,896]{3,2,1,0:T(8,128)(2,1)} %bitcast.74, f32[128,1792]{1,0:T(8,128)S(1)} %get-tuple-element.12.refs_2_), custom_call_target="tpu_custom_call" | custom-call | tf_op jit(solution)/shard_map/pallas_call | solution.py:264
  209.4 0.9 copy.7
  (3 shorter events, 0.0 us)
Async XLA Ops:
  4.8 1.0 copy-start
  48.3 5.2 %copy-start.2 = (bf16[768,1792]{1,0:T(8,128)(2,1)S(1)}, bf16[768,1792]{1,0:T(8,128)(2,1)}, u32[]{:S(2)}) copy-start(bf16[768,1792]{1,0:T(8,128)(2,1)} %param.6) | copy-start | bytes 8257540
  57.1 4.8 %copy-start.1 = (bf16[96,2048]{1,0:T(8,128)(2,1)S(1)}, bf16[96,2048]{1,0:T(8,128)(2,1)}, u32[]{:S(2)}) copy-start(bf16[96,2048]{1,0:T(8,128)(2,1)} %get-tuple-element.10.refs_2_) | copy-start | bytes 1179652

commit v16 on v13

--- a/solution.py
+++ b/solution.py
@@ -214,7 +214,7 @@
         runs.append(reduce_steps(chunk, *terms_refs, out_ref, *reduce_scratch))
     if do_gather:
         runs.append(gather_steps(local_ref, gathered_ref, *gather_scratch))
-    pattern = [0, 1] if len(runs) == 2 else [0]
+    pattern = [0, 1, 1, 1] if len(runs) == 2 else [0]
     while runs:
         for which in pattern:
             if which < len(runs):

time: 209 us -> 208 us (level)
  no operation moved by 1% of the time
where the time goes in v16:
time: 208 us
  Pallas kernels  181 us (87%)
  matrix products  15.8 us (8%)
  other arithmetic  10.5 us (5%)
    pallas_call x3, Pallas kernels, communicate(): pl.pallas_call(functools.partial(comm_kernel, chunk, do_reduce, do_gather...  177 us
    dot_general x4, matrix products, terms_of(): lax.dot_general(y_hat, activations[:, cols], (((0,), (0,)), ((), ())), pr...  15.8 us
    convert_element_type x2, other arithmetic, group_terms(): return values.reshape(feat_rows, unit_cols).astype(jnp.bfloat16)  9.48 us

profile of v16, /device:TPU:32, one launch (start us, length us, event | category | flops | bytes accessed | tf_op | source)
XLA Modules:
  0.0 208.3 jit_solution(8010575309774134704)
XLA Ops:
  0.0 3.2 %shard_map.55 = (bf16[96,2048]{1,0:T(8,128)(2,1)}, bf16[96,2048]{1,0:T(8,128)(2,1)}) custom-call(bf16[96,4096]{1,0:T(8,128)(2,1)} %grad_ref.1, f32[96,4096]{1,0:T(8,128)} %dither_ref.1), custom_call_target="tpu_custom_call" | custom-call | tf_op jit(solution)/shard_map/pallas_call | solution.py:284
  3.2 0.0 copy-start
  3.3 1.0 copy-done
  4.2 42.5 %shard_map.56 = bf16[768,2048]{1,0:T(8,128)(2,1)S(1)} custom-call(bf16[96,2048]{1,0:T(8,128)(2,1)S(1)} %copy-done), custom_call_target="tpu_custom_call" | custom-call | tf_op jit(solution)/shard_map/pallas_call | solution.py:258
  46.8 0.0 copy-start.3
  46.8 0.0 copy-start.4
  46.8 5.1 %bitcast_reduce_fusion.2 = (f32[16,896]{1,0:T(8,128)S(1)}, f32[2048,896]{1,0:T(8,128)S(1)}) fusion(bf16[768,2048]{1,0:T(8,128)(2,1)S(1)} %shard_map.56, bf16[768,1792]{1,0:T(8,128)(2,1)} %param.6), kind=kOutput, calls=%fused_computation.22 | convolution fusion | flops 2822227968 | bytes 11919360 | tf_op jit(solution)/shard_map/dot_general | solution.py:304
  51.9 0.0 copy-done.3
  52.0 0.0 copy-done.4
  52.0 0.0 copy-start.2
  52.0 3.6 %bitcast_reduce_fusion.3 = (f32[16,896]{1,0:T(8,128)S(1)}, f32[2048,896]{1,0:T(8,128)S(1)}) fusion(bf16[768,2048]{1,0:T(8,128)(2,1)S(1)} %shard_map.56, bf16[768,1792]{1,0:T(8,128)(2,1)S(1)} %copy-done.4), kind=kOutput, calls=%fused_computation.23 | convolution fusion | flops 2822227968 | bytes 11919360 | tf_op jit(solution)/shard_map/dot_general | solution.py:304
  55.6 0.0 copy-done.2
  55.6 0.0 copy-start.1
  55.6 5.0 %fusion.13 = (bf16[2048,896]{1,0:T(8,128)(2,1)}, bf16[2048,896]{1,0:T(8,128)(2,1)}) fusion(f32[2048,896]{1,0:T(8,128)S(1)} %get-tuple-element.22, f32[896]{0:T(1024)S(1)} %get-tuple-element.13, f32[16,896]{1,0:T(8,128)S(1)} %get-tuple-element.30, f32[2048]{0:T(1024)S(1)} %bitcast.78, f32[896]{0:T(1024)S(1)} %get-tuple-element.14, ...), kind=kLoop, calls=%fused_computation.25 | loop fusion | flops 22020096 | bytes 22150144 | tf_op jit(solution)/shard_map/convert_element_type | solution.py:31
  60.6 0.0 copy-done.1
  60.6 74.8 %shard_map.57 = (f32[128,1792]{1,0:T(8,128)S(1)}, bf16[768,2048]{1,0:T(8,128)(2,1)S(1)}) custom-call(bf16[4,4,128,896]{3,2,1,0:T(8,128)(2,1)} %bitcast.75, bf16[4,4,128,896]{3,2,1,0:T(8,128)(2,1)} %bitcast.74, bf16[96,2048]{1,0:T(8,128)(2,1)S(1)} %copy-done.1), custom_call_target="tpu_custom_call" | custom-call | tf_op jit(solution)/shard_map/pallas_call | solution.py:258
  135.3 3.5 %bitcast_reduce_fusion = (f32[16,896]{1,0:T(8,128)S(1)}, f32[2048,896]{1,0:T(8,128)S(1)}) fusion(bf16[768,2048]{1,0:T(8,128)(2,1)S(1)} %get-tuple-element.12, bf16[768,1792]{1,0:T(8,128)(2,1)S(1)} %copy-done.4), kind=kOutput, calls=%fused_computation.20 | convolution fusion | flops 2822227968 | bytes 11919360 | tf_op jit(solution)/shard_map/dot_general | solution.py:304
  138.9 3.6 %bitcast_reduce_fusion.1 = (f32[16,896]{1,0:T(8,128)S(1)}, f32[2048,896]{1,0:T(8,128)S(1)}) fusion(bf16[768,2048]{1,0:T(8,128)(2,1)S(1)} %get-tuple-element.12, bf16[768,1792]{1,0:T(8,128)(2,1)S(1)} %copy-done.4), kind=kOutput, calls=%fused_computation.21 | convolution fusion | flops 2822227968 | bytes 11919360 | tf_op jit(solution)/shard_map/dot_general | solution.py:304
  142.6 4.5 %fusion.15 = (bf16[2048,896]{1,0:T(8,128)(2,1)}, bf16[2048,896]{1,0:T(8,128)(2,1)S(1)}) fusion(f32[2048,896]{1,0:T(8,128)S(1)} %get-tuple-element.26, f32[16,896]{1,0:T(8,128)S(1)} %fusion.27, f32[2048]{0:T(1024)S(1)} %bitcast.77, f32[896]{0:T(1024)S(1)} %get-tuple-element.13, f32[896]{0:T(1024)S(1)} %get-tuple-element.14, ...), kind=kLoop, calls=%fused_computation.27 | loop fusion | flops 22020096 | bytes 22150144 | tf_op jit(solution)/shard_map/convert_element_type | solution.py:31
  147.1 60.2 %shard_map.58 = f32[128,1792]{1,0:T(8,128)S(1)} custom-call(bf16[4,4,128,896]{3,2,1,0:T(8,128)(2,1)S(1)} %bitcast.73, bf16[4,4,128,896]{3,2,1,0:T(8,128)(2,1)} %bitcast.76), custom_call_target="tpu_custom_call" | custom-call | tf_op jit(solution)/shard_map/pallas_call | solution.py:258
  207.3 1.0 broadcast_select_fusion
  (5 shorter events, 0.1 us)
Async XLA Ops:
  3.2 1.0 copy-start
  46.8 5.1 %copy-start.3 = (f32[1,1792]{1,0:T(1,128)S(1)}, f32[1,1792]{1,0:T(1,128)}, u32[]{:S(2)}) copy-start(f32[1,1792]{1,0:T(1,128)} %param.8) | copy-start | bytes 21508
  46.8 5.2 %copy-start.4 = (bf16[768,1792]{1,0:T(8,128)(2,1)S(1)}, bf16[768,1792]{1,0:T(8,128)(2,1)}, u32[]{:S(2)}) copy-start(bf16[768,1792]{1,0:T(8,128)(2,1)} %param.6) | copy-start | bytes 8257540
  52.0 3.6 %copy-start.2 = (f32[1,4096]{1,0:T(1,128)S(1)}, f32[1,4096]{1,0:T(1,128)}, u32[]{:S(2)}) copy-start(f32[1,4096]{1,0:T(1,128)} %param.9) | copy-start | bytes 49156
  55.6 5.0 %copy-start.1 = (bf16[96,2048]{1,0:T(8,128)(2,1)S(1)}, bf16[96,2048]{1,0:T(8,128)(2,1)}, u32[]{:S(2)}) copy-start(bf16[96,2048]{1,0:T(8,128)(2,1)} %get-tuple-element.10.refs_2_) | copy-start | bytes 1179652
